TPU v7x, 32 devices: a whole 2x2x4 slice. The times are simulated.
32 devices in a mesh: rep: 16 (over z, x, core), shard: 2 (over y).
Axes of the slice: x: 2, y: 2, z: 4, core: 2. Of those that a mesh axis runs over, the one named last changes fastest.
Arguments:
- hidden_in: bfloat16 [4096, 1024], P(('rep', 'shard')), may hold values from -6 to 6
- cotangent: bfloat16 [4096, 1024], P(('rep', 'shard')), may hold values from -6 to 6
- norm_gain: float32 [1, 1024], P(None, 'shard'), may hold values from 0.5 to 1.5
- w_z: bfloat16 [1, 1024, 2048], P(None, None, 'shard'), may hold values from -0.1875 to 0.1875
- w_x: bfloat16 [1, 1024, 2048], P(None, None, 'shard'), may hold values from -0.1875 to 0.1875
- w_bc: bfloat16 [1, 1024, 256], P(None, None, 'shard'), may hold values from -0.1875 to 0.1875
- w_dt: bfloat16 [1, 1024, 32], P(None, None, 'shard'), may hold values from -0.1875 to 0.1875
- conv_x: float32 [1, 4, 2048], P(None, None, 'shard'), may hold values from -3 to 3
- conv_bc: float32 [1, 4, 256], P(None, None, 'shard'), may hold values from -3 to 3
- bias_x: float32 [1, 2048], P(None, 'shard'), may hold values from -1.75 to 1.75
- bias_bc: float32 [1, 256], P(None, 'shard'), may hold values from -1.75 to 1.75
- dt_bias: float32 [1, 32], P(None, 'shard'), may hold values from -5 to -2
- a_log: float32 [1, 32], P(None, 'shard'), may hold values from 0 to 2.77
- d_skip: float32 [1, 32], P(None, 'shard'), may hold values from 0.5 to 1.5
- gate_gain: float32 [1, 2048], P(None, 'shard'), may hold values from 0.5 to 1.5
- w_out: bfloat16 [1, 2048, 1024], P(None, 'shard'), may hold values from -0.125 to 0.125
- seq_len: int32 [256], replicated, may hold values from 0 to 128, as said below
- seq_owner: int32 [256], replicated, may hold values from 0 to 31, as said below
- seq_start: int32 [256], replicated, may hold values from 0 to 128, as said below
Outputs:
- hidden_out: float32 [4096, 1024], P(('rep', 'shard'))
- grad_hidden: float32 [4096, 1024], P(('rep', 'shard'))
- grad_norm_gain: float32 [1, 1024], P(None, 'shard')
- grad_w_z: float32 [1, 1024, 2048], P(None, None, 'shard')
- grad_w_x: float32 [1, 1024, 2048], P(None, None, 'shard')
- grad_w_bc: float32 [1, 1024, 256], P(None, None, 'shard')
- grad_w_dt: float32 [1, 1024, 32], P(None, None, 'shard')
- grad_conv_x: float32 [1, 4, 2048], P(None, None, 'shard')
- grad_conv_bc: float32 [1, 4, 256], P(None, None, 'shard')
- grad_bias_x: float32 [1, 2048], P(None, 'shard')
- grad_bias_bc: float32 [1, 256], P(None, 'shard')
- grad_dt_bias: float32 [1, 32], P(None, 'shard')
- grad_a_log: float32 [1, 32], P(None, 'shard')
- grad_d_skip: float32 [1, 32], P(None, 'shard')
- grad_gate_gain: float32 [1, 2048], P(None, 'shard')
- grad_w_out: float32 [1, 2048, 1024], P(None, 'shard')
Inputs may be any that keep to these rules, and one draw needn't show every extreme that they name: `seq_len`: the records come in groups of 8 in a row; each group belongs to exactly one device, and every device has one group. A group's sequences lie back to back from its device's first slot in record order, never past its last slot; some records are empty. `seq_owner`: all records of a group name the same device. `seq_start`: A record starts where the previous record of its group ends, the first at slot 0; an empty record may start at slot 128.
All inputs are finite; a program needn't handle non-finite values.
Results may differ from a plain program's by a relative error of at most 0.04.
Values may be sent and summed in bfloat16 or wider, within the bound.
No kernel may reach another device: no remote copies, remote signals or barrier semaphores. Data moves between devices by JAX's collectives and lax.ppermute only.
A program may use at most 128 MiB of HBM per device.

v0:
```python
from functools import partial

import jax
import jax.numpy as jnp
from jax import lax
from jax.sharding import PartitionSpec as P

BLOCK = 64
INNER = 2048


epsilon = 1e-05
HIGHEST = lax.Precision.HIGHEST


def slot_segments(seq_len, seq_owner, seq_start, device, row_count):
    slot_ids = jnp.arange(row_count, dtype=jnp.int32)
    record_ids = jnp.arange(seq_len.shape[0], dtype=jnp.int32)
    covers = (
        (seq_owner[:, None] == device)
        & (slot_ids[None, :] >= seq_start[:, None])
        & (slot_ids[None, :] < seq_start[:, None] + seq_len[:, None])
    )
    in_use = jnp.sum(covers.astype(jnp.int32), axis=0)
    covering = jnp.sum(jnp.where(covers, record_ids[:, None], 0), axis=0)
    lone_ids = seq_len.shape[0] + device * row_count + slot_ids
    segment = jnp.where(in_use > 0, covering, lone_ids)
    return (segment, in_use)


def causal_conv(inputs, kernel, bias_row, segment):
    kernel_len = kernel.shape[0]
    row_count = inputs.shape[0]
    result = bias_row[None, :] + kernel[kernel_len - 1][None, :] * inputs
    for offset in range(1, kernel_len):
        shifted = jnp.pad(inputs, ((offset, 0), (0, 0)))[:row_count]
        earlier = jnp.pad(segment, (offset, 0), constant_values=-1)[:row_count]
        same_seq = (earlier == segment).astype(inputs.dtype)
        result = result + kernel[kernel_len - 1 - offset][None, :] * shifted * same_seq[:, None]
    return result


def carry_state(state, inputs):
    local_part, span_total, keep_flag = inputs
    updated = local_part + keep_flag * jnp.exp(span_total)[:, None, None] * state
    return (updated, state)


def mixer_core(
    inner_x, inner_bc, dt_raw, conv_x, conv_bc, bias_x, bias_bc, dt_bias, a_log, d_skip, segment
):
    row_count = inner_x.shape[0]
    head_count = dt_raw.shape[1]
    head_size = inner_x.shape[1] // head_count
    state_size = inner_bc.shape[1] // 2
    bin_count = row_count // BLOCK
    values = jax.nn.silu(causal_conv(inner_x, conv_x, bias_x, segment))
    maps_both = jax.nn.silu(causal_conv(inner_bc, conv_bc, bias_bc, segment))
    step_size = jax.nn.softplus(dt_raw + dt_bias[None, :])
    log_decay = -step_size * jnp.exp(a_log)[None, :]
    cumulative = jnp.transpose(
        jnp.cumsum(log_decay.reshape(bin_count, BLOCK, head_count), axis=1), (0, 2, 1)
    )
    step_rows = jnp.transpose(step_size.reshape(bin_count, BLOCK, head_count), (0, 2, 1))
    bin_segment = segment.reshape(bin_count, BLOCK)
    positions = jnp.arange(BLOCK, dtype=jnp.int32)
    causal = (positions[:, None] >= positions[None, :])[None, :, :] & (
        bin_segment[:, :, None] == bin_segment[:, None, :]
    )
    causal = causal[:, None, :, :]
    log_gaps = cumulative[:, :, :, None] - cumulative[:, :, None, :]
    decay_rows = jnp.where(causal, jnp.exp(jnp.where(causal, log_gaps, 0.0)), 0.0)
    key_rows = maps_both[:, :state_size].reshape(bin_count, BLOCK, state_size)
    query_rows = maps_both[:, state_size:].reshape(bin_count, BLOCK, state_size)
    scores = jnp.einsum("btn,bsn->bts", query_rows, key_rows, precision=HIGHEST)
    mixing = scores[:, None, :, :] * decay_rows * step_rows[:, :, None, :]
    head_values = values.reshape(bin_count, BLOCK, head_count, head_size)
    result = jnp.einsum("bhts,bshp->bthp", mixing, head_values, precision=HIGHEST)
    span_total = cumulative[:, :, BLOCK - 1]
    last_segment = bin_segment[:, BLOCK - 1]
    prior_segment = jnp.concatenate([jnp.full((1,), -1, jnp.int32), last_segment[:-1]])
    in_last = (bin_segment == last_segment[:, None]).astype(jnp.float32)
    tail_weights = jnp.exp(span_total[:, :, None] - cumulative) * step_rows * in_last[:, None, :]
    weighted_values = head_values * jnp.transpose(tail_weights, (0, 2, 1))[:, :, :, None]
    local_states = jnp.einsum("bshp,bsn->bhpn", weighted_values, key_rows, precision=HIGHEST)
    keep_flags = (prior_segment == last_segment).astype(jnp.float32)
    start_state = jnp.zeros((head_count, head_size, state_size), jnp.float32)
    unused, incoming = lax.scan(carry_state, start_state, (local_states, span_total, keep_flags))
    reads = (bin_segment == prior_segment[:, None]).astype(jnp.float32)
    entry_decay = jnp.exp(cumulative) * reads[:, None, :]
    carried = jnp.einsum("btn,bhpn->bthp", query_rows, incoming, precision=HIGHEST)
    result = result + carried * jnp.transpose(entry_decay, (0, 2, 1))[:, :, :, None]
    result = result + d_skip[None, None, :, None] * head_values
    return result.reshape(row_count, head_count * head_size)


def pre_norm(residual, gain_row):
    scale_rows = lax.rsqrt(jnp.mean(residual * residual, axis=1, keepdims=True) + epsilon)
    return residual * scale_rows * gain_row[None, :]


def shard_squares(row_sums):
    return lax.psum(row_sums, "shard")


def shard_dots(row_sums):
    return lax.psum(row_sums, "shard")


def rows_product(left, right):
    return lax.dot_general(
        left, right, (((0,), (0,)), ((), ())), preferred_element_type=jnp.float32
    )


def back_product(left, right):
    return lax.dot_general(
        left, right, (((1,), (1,)), ((), ())), preferred_element_type=jnp.float32
    )


def branch_forward(normed, matrices, smalls, segment, square_total):
    proj_z = jnp.dot(normed, matrices[0], preferred_element_type=jnp.float32)
    proj_x = jnp.dot(normed, matrices[1], preferred_element_type=jnp.float32)
    proj_bc = jnp.dot(normed, matrices[2], preferred_element_type=jnp.float32)
    proj_dt = jnp.dot(normed, matrices[3], preferred_element_type=jnp.float32)
    core_fn = partial(mixer_core, segment=segment)
    core_out, core_back = jax.vjp(
        core_fn,
        proj_x,
        proj_bc,
        proj_dt,
        smalls[0],
        smalls[1],
        smalls[2],
        smalls[3],
        smalls[4],
        smalls[5],
        smalls[6],
    )
    gated_rows = core_out * jax.nn.silu(proj_z)
    inverse = lax.rsqrt(square_total(jnp.sum(gated_rows * gated_rows, axis=1)) / INNER + epsilon)
    mixed_rows = (gated_rows * inverse[:, None] * smalls[7][None, :]).astype(jnp.bfloat16)
    return (mixed_rows, (proj_z, core_out, core_back, gated_rows, inverse))


def branch_backward(d_mixed, kept_state, gain_row, dot_total):
    proj_z, core_out, core_back, gated_rows, inverse = kept_state
    grad_gate = jnp.sum(d_mixed * gated_rows * inverse[:, None], axis=0)
    d_hat = d_mixed * gain_row[None, :]
    dot_sum = dot_total(jnp.sum(d_hat * gated_rows, axis=1))
    d_gated = (
        inverse[:, None] * d_hat
        - gated_rows * (inverse * inverse * inverse * dot_sum / INNER)[:, None]
    )
    sigmoid_z = jax.nn.sigmoid(proj_z)
    d_core = d_gated * proj_z * sigmoid_z
    d_proj_z = d_gated * core_out * sigmoid_z * (1.0 + proj_z * (1.0 - sigmoid_z))
    core_grads = core_back(d_core)
    return (grad_gate, d_proj_z, core_grads)


def sum_replicas(parts):
    return (
        lax.psum(parts[0].astype(jnp.bfloat16), "rep").astype(jnp.float32),
        lax.psum(parts[1].astype(jnp.bfloat16), "rep").astype(jnp.float32),
        lax.psum(parts[2].astype(jnp.bfloat16), "rep").astype(jnp.float32),
        lax.psum(parts[3].astype(jnp.bfloat16), "rep").astype(jnp.float32),
        lax.psum(parts[4].astype(jnp.bfloat16), "rep").astype(jnp.float32),
        lax.psum(parts[5].astype(jnp.bfloat16), "rep").astype(jnp.float32),
        lax.psum(parts[6].astype(jnp.bfloat16), "rep").astype(jnp.float32),
        lax.psum(parts[7].astype(jnp.bfloat16), "rep").astype(jnp.float32),
        lax.psum(parts[8].astype(jnp.bfloat16), "rep").astype(jnp.float32),
        lax.psum(parts[9].astype(jnp.bfloat16), "rep").astype(jnp.float32),
        lax.psum(parts[10].astype(jnp.bfloat16), "rep").astype(jnp.float32),
        lax.psum(parts[11].astype(jnp.bfloat16), "rep").astype(jnp.float32),
        lax.psum(parts[12].astype(jnp.bfloat16), "rep").astype(jnp.float32),
        lax.psum(parts[13].astype(jnp.bfloat16), "rep").astype(jnp.float32),
    )


def on_device(
    hidden_in,
    cotangent,
    norm_gain,
    w_z,
    w_x,
    w_bc,
    w_dt,
    conv_x,
    conv_bc,
    bias_x,
    bias_bc,
    dt_bias,
    a_log,
    d_skip,
    gate_gain,
    w_out,
    seq_len,
    seq_owner,
    seq_start,
):
    shard_count = lax.axis_size("shard")
    shard_index = lax.axis_index("shard")
    first_device = lax.axis_index("rep") * shard_count
    own_rows = hidden_in.shape[0]
    own_segment, own_use = slot_segments(
        seq_len, seq_owner, seq_start, first_device + shard_index, own_rows
    )
    use_rows = own_use.astype(jnp.float32)[:, None]
    residual = hidden_in.astype(jnp.float32)
    d_residual = cotangent.astype(jnp.float32) * use_rows
    small_parts = (
        lax.all_gather(norm_gain.astype(jnp.bfloat16), "shard", axis=1, tiled=True).astype(
            norm_gain.dtype
        ),
        lax.all_gather(w_bc, "shard", axis=2, tiled=True),
        lax.all_gather(conv_bc.astype(jnp.bfloat16), "shard", axis=2, tiled=True).astype(
            conv_bc.dtype
        ),
        lax.all_gather(bias_bc.astype(jnp.bfloat16), "shard", axis=1, tiled=True).astype(
            bias_bc.dtype
        ),
    )
    member_ids = first_device + jnp.arange(shard_count, dtype=jnp.int32)
    group_segment = jax.vmap(
        lambda member: slot_segments(seq_len, seq_owner, seq_start, member, own_rows)[0]
    )(member_ids).reshape(-1)
    layer_index = 0
    normed_own = pre_norm(residual, small_parts[0][layer_index]).astype(jnp.bfloat16)
    normed = lax.all_gather(normed_own, "shard", axis=0, tiled=True)
    smalls = (
        conv_x[layer_index],
        small_parts[2][layer_index],
        bias_x[layer_index],
        small_parts[3][layer_index],
        dt_bias[layer_index],
        a_log[layer_index],
        d_skip[layer_index],
        gate_gain[layer_index],
    )
    matrices = (w_z[layer_index], w_x[layer_index], small_parts[1][layer_index], w_dt[layer_index])
    mixed_rows, kept_state = branch_forward(normed, matrices, smalls, group_segment, shard_squares)
    saved_layers = [(residual, normed, mixed_rows, kept_state)]

    def branch_term(row_start, row_count, mixed_rows=mixed_rows, out_weight=w_out[layer_index]):
        return jnp.dot(mixed_rows, out_weight, preferred_element_type=jnp.float32)

    residual = residual + lax.psum_scatter(
        branch_term(jnp.int32(0), lax.axis_size("shard") * own_rows).astype(jnp.bfloat16),
        "shard",
        scatter_dimension=0,
        tiled=True,
    ).astype(jnp.float32)
    layer_index = 0
    residual_in, normed, mixed_rows, kept_state = saved_layers[layer_index]
    out_cot = d_residual.astype(jnp.bfloat16)
    cot_all = lax.all_gather(out_cot, "shard", axis=0, tiled=True)
    grad_out = rows_product(mixed_rows, cot_all)
    d_mixed = back_product(cot_all, w_out[layer_index])
    grad_gate, d_proj_z, core_grads = branch_backward(
        d_mixed, kept_state, gate_gain[layer_index], shard_dots
    )
    bc_own = lax.psum_scatter(
        core_grads[1].astype(jnp.bfloat16), "shard", scatter_dimension=1, tiled=True
    )
    conv_own = lax.psum_scatter(
        core_grads[4].astype(jnp.bfloat16), "shard", scatter_dimension=1, tiled=True
    ).astype(jnp.float32)
    bias_own = lax.psum_scatter(
        core_grads[6].astype(jnp.bfloat16), "shard", scatter_dimension=0, tiled=True
    ).astype(jnp.float32)
    cot_z = d_proj_z.astype(jnp.bfloat16)
    cot_x = core_grads[0].astype(jnp.bfloat16)
    cot_dt = core_grads[2].astype(jnp.bfloat16)
    cotangents = (cot_z, cot_x, bc_own, cot_dt)
    matrices = (w_z[layer_index], w_x[layer_index], w_bc[layer_index], w_dt[layer_index])

    def input_term(row_start, row_count, cotangents=cotangents, matrices=matrices):
        running_sum = jnp.zeros((row_count, matrices[0].shape[0]), jnp.float32)
        for cot_part, matrix in zip(cotangents, matrices):
            running_sum = running_sum + back_product(cot_part, matrix)
        return running_sum

    d_normed = lax.psum_scatter(
        input_term(jnp.int32(0), lax.axis_size("shard") * own_rows).astype(jnp.bfloat16),
        "shard",
        scatter_dimension=0,
        tiled=True,
    ).astype(jnp.float32)
    norm_back = jax.vjp(pre_norm, residual_in, small_parts[0][layer_index])[1]
    d_previous, grad_norm_full = norm_back(d_normed)
    grad_norm = lax.psum_scatter(grad_norm_full, "shard", scatter_dimension=0, tiled=True)
    d_residual = d_residual + d_previous
    layer_grads = (
        grad_norm,
        rows_product(normed, cot_z),
        rows_product(normed, cot_x),
        rows_product(normed, bc_own),
        rows_product(normed, cot_dt),
        core_grads[3],
        conv_own,
        core_grads[5],
        bias_own,
        core_grads[7],
        core_grads[8],
        core_grads[9],
        grad_gate,
        grad_out,
    )
    collected = [layer_grads]
    ordered = collected[::-1]
    stacked = tuple(
        (jnp.stack([layer_grads[grad_slot] for layer_grads in ordered]) for grad_slot in range(14))
    )
    stacked = sum_replicas(stacked)
    hidden_out = residual * use_rows
    return (hidden_out, d_residual) + tuple(stacked)


def solution(mesh):
    in_specs = (
        P(("rep", "shard"), None),
        P(("rep", "shard"), None),
        P(None, "shard"),
        P(None, None, "shard"),
        P(None, None, "shard"),
        P(None, None, "shard"),
        P(None, None, "shard"),
        P(None, None, "shard"),
        P(None, None, "shard"),
        P(None, "shard"),
        P(None, "shard"),
        P(None, "shard"),
        P(None, "shard"),
        P(None, "shard"),
        P(None, "shard"),
        P(None, "shard", None),
        P(),
        P(),
        P(),
    )
    out_specs = (
        P(("rep", "shard"), None),
        P(("rep", "shard"), None),
        P(None, "shard"),
        P(None, None, "shard"),
        P(None, None, "shard"),
        P(None, None, "shard"),
        P(None, None, "shard"),
        P(None, None, "shard"),
        P(None, None, "shard"),
        P(None, "shard"),
        P(None, "shard"),
        P(None, "shard"),
        P(None, "shard"),
        P(None, "shard"),
        P(None, "shard"),
        P(None, "shard", None),
    )
    return jax.shard_map(
        on_device, mesh=mesh, in_specs=in_specs, out_specs=out_specs, check_vma=False
    )
```

profile of v0, /device:TPU:0, one launch (start us, length us, event | category | flops | bytes accessed | tf_op | source)
XLA Modules:
  0.0 437.3 jit_solution(8193885522419835834)
XLA Ops:
  15.0 5.2 %all_gather.18 = bf16[1,1024]{1,0:T(2,128)(2,1)S(1)} all-gather(bf16[1,512]{1,0:T(2,128)(2,1)S(1)} %convert_element_type.269), channel_id=1, replica_groups=mesh['rep'=16,'shard'=2] {'shard'}, dimensions={1}, use_global_device_ids=true | all-gather | bytes 3072 | tf_op jit(solution)/shard_map/all_gather | solution.py:214
  21.3 7.9 %all_gather.19 = bf16[256,1024]{1,0:T(8,128)(2,1)S(1)} all-gather(bf16[128,1024]{1,0:T(8,128)(2,1)S(1)} %fusion.84), channel_id=1, replica_groups=mesh['rep'=16,'shard'=2] {'shard'}, dimensions={0}, use_global_device_ids=true | all-gather | bytes 786432 | tf_op jit(solution)/shard_map/all_gather | solution.py:231
  32.2 2.3 fusion.19
  35.6 2.1 fusion.79
  37.7 2.8 reshape.543
  40.5 3.1 copy.204
  43.6 7.2 %all_gather.22 = bf16[1,1024,256]{2,1,0:T(8,128)(2,1)S(1)} all-gather(bf16[1,1024,128]{2,1,0:T(8,128)(2,1)S(1)} %copy-done.24), channel_id=1, replica_groups=mesh['rep'=16,'shard'=2] {'shard'}, dimensions={2}, use_global_device_ids=true | all-gather | bytes 786432 | tf_op jit(solution)/shard_map/all_gather | solution.py:217
  51.1 4.2 all_gather.21
  55.5 4.4 %all_gather.20 = bf16[1,256]{1,0:T(2,128)(2,1)S(1)} all-gather(bf16[1,128]{1,0:T(2,128)(2,1)S(1)} %convert_element_type.275), channel_id=1, replica_groups=mesh['rep'=16,'shard'=2] {'shard'}, dimensions={1}, use_global_device_ids=true | all-gather | bytes 768 | tf_op jit(solution)/shard_map/all_gather | solution.py:221
  62.2 4.9 %fusion.34 = f32[4,16,64,128]{3,2,1,0:T(8,128)} fusion(f32[4,64,128,1]{2,1,3,0:T(8,128)S(1)} %bitcast.247, f32[4,64,16,64]{1,3,2,0:T(8,128)} %copy.204, f32[4,64,16]{1,2,0:T(8,128)S(1)} %get-tuple-element.401), kind=kOutput, calls=%fused_computation.53 | convolution fusion | flops 402915328 | bytes 3293184 | tf_op jit(solution)/shard_map/jvp(bshp,bsn->bhpn)/dot_general | solution.py:85
  69.2 27.4 %while.36 = (s32[]{:T(128)}, f32[16,64,128]{2,1,0:T(8,128)S(1)}, f32[4,16,64,128]{3,2,1,0:T(8,128)}, f32[4,16]{1,0:T(4,128)}, f32[4,16,1,1]{1,3,2,0:T(1,128)}, /...) while((s32[]{:T(128)}, f32[16,64,128]{2,1,0:T(8,128)S(1)}, ...), condition=%wide.region_5.6_spmd.clone, body=%wide.region_4.5_spmd.clone.sunk | while | flops 524323 | bytes 2624072 | solution.py:88
  97.5 3.5 fusion.133
  102.4 5.3 %fusion.16 = f32[4,64,16,64]{1,3,2,0:T(8,128)} fusion(f32[4,64,16,64]{1,3,2,0:T(8,128)S(1)} %copy-done.4, f32[4,64,16,64]{1,3,2,0:T(8,128)S(1)} %fusion.133, f32[16]{0:T(128)S(1)} %bitcast.304, f32[4,64,16]{1,2,0:T(8,128)S(1)} %get-tuple-element.402, f32[4,16,64]{2,1,0:T(8,128)S(1)} %copy-done.39, f32[4,16,64]{2,1,0:T(8,128)S(1)} %bitcast.256, ...), kind=kOutput, calls=%fused_computation.28 | convolution fusion | flops 203685888 | bytes 3276864 | tf_op jit(solution)/shard_map/jvp(bhts,bshp->bthp)/dot_general | solution.py:78
  107.7 3.1 copy.210
  110.8 2.7 reshape.548
  113.6 3.4 multiply_reduce_fusion.11
  117.0 5.0 %psum.112 = f32[256]{0:T(256)S(1)} all-reduce(f32[256]{0:T(256)S(1)} %get-tuple-element.378), channel_id=1, replica_groups=mesh['rep'=16,'shard'=2] {'shard'}, use_global_device_ids=true, to_apply=%region_7.8 | all-reduce | flops 256 | bytes 2048 | tf_op jit(solution)/shard_map/psum | solution.py:103
  122.7 7.0 %all_gather.23 = bf16[256,1024]{1,0:T(8,128)(2,1)S(1)} all-gather(bf16[128,1024]{1,0:T(8,128)(2,1)S(1)} %fusion.92), channel_id=1, replica_groups=mesh['rep'=16,'shard'=2] {'shard'}, dimensions={0}, use_global_device_ids=true | all-gather | bytes 786432 | tf_op jit(solution)/shard_map/all_gather | solution.py:258
  129.7 4.5 %multiply_reduce_fusion.4 = (bf16[1024]{0:T(1024)(128)(2,1)}, f32[256]{0:T(256)S(1)}, f32[256,1024]{1,0:T(8,128)}) fusion(f32[256,1024]{1,0:T(8,128)} %get-tuple-element.379, f32[256]{0:T(256)S(1)} %add_rsqrt_fusion, f32[1024]{0:T(1024)S(1)} %bitcast.265, bf16[256,1024]{1,0:T(8,128)(2,1)S(1)} %all_gather.23, bf16[1,1024,1024]{2,1,0:T(8,128)(2,1)} %param.38), kind=kOutput, calls=%fused_computation.84 | convolution fusion | flops 538442496 | bytes 4726784 | tf_op jit(solution)/shard_map/dot_general | solution.py:117
  134.3 5.2 %psum.113 = f32[256]{0:T(256)S(1)} all-reduce(f32[256]{0:T(256)S(1)} %get-tuple-element.307), channel_id=1, replica_groups=mesh['rep'=16,'shard'=2] {'shard'}, use_global_device_ids=true, to_apply=%region_11.12 | all-reduce | flops 256 | bytes 2048 | tf_op jit(solution)/shard_map/psum | solution.py:107
  139.4 5.2 %multiply_reduce_fusion.5 = (f32[1024]{0:T(1024)}, f32[256,1024]{1,0:T(8,128)}, bf16[256,1024]{1,0:T(8,128)(2,1)}) fusion(f32[256,1024]{1,0:T(8,128)} %get-tuple-element.383, f32[256,1024]{1,0:T(8,128)} %get-tuple-element.419, f32[256,1024]{1,0:T(8,128)} %get-tuple-element.379, f32[256]{0:T(256)S(1)} %fusion.119, f32[256,1024]{1,0:T(8,128)} %get-tuple-element.420, ...), kind=kLoop, calls=%fused_computation.85 | loop fusion | flops 5766144 | bytes 6825984 | tf_op jit(solution)/shard_map/transpose(jvp())/reduce_sum | solution.py:93
  144.6 2.8 reshape.549
  147.4 3.1 copy.211
  150.5 7.4 %fusion.58 = (f32[4,16,64]{2,1,0:T(8,128)}, f32[4,16,64]{2,1,0:T(8,128)}, f32[4,16,64]{2,1,0:T(8,128)}, f32[4,64,64]{2,1,0:T(8,128)}) fusion(f32[4,16,64]{2,1,0:T(8,128)S(1)} %copy-done.40, f32[4,16,64]{2,1,0:T(8,128)S(1)} %bitcast.257, f32[4,64,64]{2,1,0:T(8,128)S(1)} %copy-done.30, pred[4,64,64]{2,1,0:T(8,128)(4,1)S(1)} %copy-done.37, ...), kind=kOutput, calls=%fused_computation.71 | convolution fusion | flops 205230080 | bytes 2326528 | tf_op jit(solution)/shard_map/transpose(jvp(bhts,bshp->bthp))/dot_general | solution.py:78
  157.9 4.2 fusion.49
  162.1 3.3 fusion.30
  167.0 22.5 %while.37 = (s32[]{:T(128)}, f32[16,64,128]{2,1,0:T(8,128)S(1)}, f32[4,16,64,128]{3,2,1,0:T(8,128)}, f32[4,16]{1,0:T(4,128)S(1)}, f32[4,16,64,128]{3,2,1,0:T(8,1...) while((s32[]{:T(128)}, f32[16,64,128]{2,1,0:T(8,128)S(1)}, ...), condition=%wide.region_14.15_spmd.clone, body=%wide.region_12.14_spmd.clone.sunk | while | flops 786452 | bytes 3146480 | solution.py:88
  190.2 5.9 %fusion.46 = f32[4,64,128]{2,1,0:T(8,128)S(1)} fusion(f32[4,16,64,128]{3,2,1,0:T(8,128)} %get-tuple-element.243, f32[4,64,16,64]{1,3,2,0:T(8,128)} %copy.204, f32[4,64,16]{1,2,0:T(8,128)S(1)} %get-tuple-element.401), kind=kOutput, calls=%fused_computation.63 | convolution fusion | flops 402915328 | bytes 3293184 | tf_op jit(solution)/shard_map/transpose(jvp(bshp,bsn->bhpn))/dot_general | solution.py:85
  199.7 4.3 multiply_reduce_fusion.2
  205.6 5.6 %bitcast_add_fusion.2 = f32[4,64,16,64]{1,3,2,0:T(8,128)} fusion(f32[4,64,16,64]{1,3,2,0:T(8,128)S(1)} %get-tuple-element.422, f32[4,64,16,64]{1,3,2,0:T(8,128)S(1)} %copy-done.2, f32[4,16,64,64]{2,1,3,0:T(8,128)S(1)} %bitcast.246, f32[16]{0:T(128)S(1)} %bitcast.305, f32[4,64,16]{1,2,0:T(8,128)S(1)} %get-tuple-element.401, f32[4,16,64]{2,1,0:T(8,128)S(1)} %copy-done.41, ...), kind=kOutput, calls=%fused_computation.14 | convolution fusion | flops 203685888 | bytes 4325440 | tf_op jit(solution)/shard_map/transpose(jvp(bhts,bshp->bthp))/dot_general | solution.py:78
  211.2 3.1 copy.215
  214.3 2.7 reshape.550
  217.0 5.0 %multiply_reduce_fusion.9 = (f32[1024]{0:T(1024)S(1)}, f32[1024]{0:T(1024)}, f32[1024]{0:T(1024)}, f32[1024]{0:T(1024)}, bf16[1024]{0:T(1024)(128)(2,1)}, /*index=5*/f32[256,1024]{1,0:T(8,128)S(1)}) fusion(f32[256,1024]{1,0:T(8,128)} %copy-done.7, f32[256]{0:T(256)S(1)} %copy-done.52, f32[256]{0:T(256)S(1)} %copy-done.50, f32[256]{0:T(256)S(1)} %copy-done.48, ...), kind=kLoop, calls=%fused_computation.89 | loop fusion | flops 5499904 | bytes 4215808 | tf_op jit(solution)/shard_map/transpose(jvp())/reduce_sum | solution.py:39
  222.1 1.9 multiply_multiply_fusion.2
  224.6 1.8 reduce_window_sum.23
  230.2 1.9 fusion.62
  236.8 3.5 fusion.42
  240.4 3.1 convert_bitcast_fusion.1
  243.5 2.1 convert_bitcast_fusion.2
  245.6 2.1 convert_bitcast_fusion
  251.5 5.2 %all-reduce.27 = bf16[256]{0:T(256)(128)(2,1)S(1)} all-reduce(bf16[256]{0:T(256)(128)(2,1)S(1)} %copy-done.99), channel_id=7, replica_groups=mesh['rep'=16,'shard'=2] {'shard'}, use_global_device_ids=true, to_apply=%region_47.48.clone | all-reduce | flops 256 | bytes 1024
  259.1 4.9 %all-reduce.26 = bf16[1024]{0:T(1024)(128)(2,1)S(1)} all-reduce(f32[1024]{0:T(1024)S(1)} %get-tuple-element.317), channel_id=5, replica_groups=mesh['rep'=16,'shard'=2] {'shard'}, use_global_device_ids=true, to_apply=%region_27.28.clone | all-reduce | flops 1024 | bytes 6144
  264.1 60.9 %all-reduce.28 = (bf16[1,512]{1,0:T(2,128)(2,1)S(1)}, bf16[1,1024,16]{1,2,0:T(8,128)(2,1)S(1)}, bf16[1,4,1024]{2,1,0:T(4,128)(2,1)S(1)}, bf16[1,4,128]{2,1,0:T(4...) all-reduce(bf16[1,512]{1,0:T(2,128)(2,1)S(1)} %convert_element_type, ...), channel_id=1, replica_groups=mesh['rep'=16,'shard'=2] {'rep'}, use_global_device_ids=true, to_apply=%region_28.29 | all-reduce | flops 23728 | bytes 94912 | tf_op jit(solution)/shard_map/psum | solution.py:165
  330.7 2.4 fusion.86
  333.1 87.4 %all-reduce.32.cloned.1.call-done = (bf16[1,1024,1024]{2,1,0:T(8,128)(2,1)}, bf16[1,1024,1024]{2,1,0:T(8,128)(2,1)}, bf16[1,1024,128]{2,1,0:T(8,128)(2,1)}, bf16[1,1024,1024]{2,1,0:T(8,128)(2,1)}) async-done(((bf16[1,1024,1024]{2,1,0:T(8,128)(2,1)}, bf16[1,1024,1024]{2,1,0:T(8,128)(2,1)}, bf16[1,1024,128]{2,1,0:T(8,128)(2,1)}, bf16[1,1024,1024]{2,1,0:T(8,128)(2,1)}), (bf16[1,1024,1024]{2,1,0:T(8,128)(2,1)}, ...) | async-done | bytes 6553616 | tf_op jit(solution)/shard_map/psum | solution.py:166
  420.5 4.2 convert_element_type.299
  424.7 2.5 convert_element_type.302
  427.2 2.5 convert_element_type.334
  (373 shorter events, 97.3 us)
Async XLA Ops:
  7.2 106.3 %copy-start = (bf16[1,1024,1024]{2,1,0:T(8,128)(2,1)S(1)}, bf16[1,1024,1024]{2,1,0:T(8,128)(2,1)}, u32[]{:S(2)}) copy-start(bf16[1,1024,1024]{2,1,0:T(8,128)(2,1)} %param.26) | copy-start | bytes 6291460
  7.2 226.8 %reduce-scatter.13.cloned.1.call-start = ((), (), s32[]{:S(2)}) async-start(), calls=%async_computation.6 | async-start | bytes 196608
  8.1 12.1 %copy-start.70 = (s32[256]{0:T(256)}, s32[256]{0:T(256)S(1)}, u32[]{:S(2)}) copy-start(s32[256]{0:T(256)S(1)} %add.321) | copy-start | bytes 3076
  12.6 48.3 %copy-start.45 = (f32[4,64]{1,0:T(4,128)}, f32[4,64]{1,0:T(4,128)S(1)}, u32[]{:S(2)}) copy-start(f32[4,64]{1,0:T(4,128)S(1)} %get-tuple-element.410) | copy-start | bytes 3076
  14.3 5.9 %copy-start.86 = (f32[128]{0:T(128)}, f32[128]{0:T(128)S(1)}, u32[]{:S(2)}) copy-start(f32[128]{0:T(128)S(1)} %fusion.121) | copy-start | bytes 1540
  32.2 27.7 %copy-start.47 = (f32[256]{0:T(256)}, f32[256]{0:T(256)S(1)}, u32[]{:S(2)}) copy-start(f32[256]{0:T(256)S(1)} %get-tuple-element.415) | copy-start | bytes 3076
  32.2 27.7 %copy-start.49 = (f32[256]{0:T(256)}, f32[256]{0:T(256)S(1)}, u32[]{:S(2)}) copy-start(f32[256]{0:T(256)S(1)} %get-tuple-element.416) | copy-start | bytes 3076
  32.2 27.7 %copy-start.51 = (f32[256]{0:T(256)}, f32[256]{0:T(256)S(1)}, u32[]{:S(2)}) copy-start(f32[256]{0:T(256)S(1)} %get-tuple-element.417) | copy-start | bytes 3076
  34.5 6.0 %copy-start.53 = (f32[1,1,1024]{2,1,0:T(1,128)}, f32[1,1,1024]{2,1,0:T(1,128)S(1)}, u32[]{:S(2)}) copy-start(f32[1,1,1024]{2,1,0:T(1,128)S(1)} %get-tuple-element.406) | copy-start | bytes 12292
  34.5 6.0 %copy-start.55 = (f32[1,1,1024]{2,1,0:T(1,128)}, f32[1,1,1024]{2,1,0:T(1,128)S(1)}, u32[]{:S(2)}) copy-start(f32[1,1,1024]{2,1,0:T(1,128)S(1)} %get-tuple-element.407) | copy-start | bytes 12292
  34.5 6.0 %copy-start.57 = (f32[1,1,1024]{2,1,0:T(1,128)}, f32[1,1,1024]{2,1,0:T(1,128)S(1)}, u32[]{:S(2)}) copy-start(f32[1,1,1024]{2,1,0:T(1,128)S(1)} %get-tuple-element.408) | copy-start | bytes 12292
  34.6 5.9 %copy-start.59 = (f32[1,1,1024]{2,1,0:T(1,128)}, f32[1,1,1024]{2,1,0:T(1,128)S(1)}, u32[]{:S(2)}) copy-start(f32[1,1,1024]{2,1,0:T(1,128)S(1)} %get-tuple-element.405) | copy-start | bytes 12292
  43.6 7.5 %copy-start.94 = (f32[1,4,128]{2,1,0:T(4,128)S(1)}, f32[1,4,128]{2,1,0:T(4,128)}, u32[]{:S(2)}) copy-start(f32[1,4,128]{2,1,0:T(4,128)} %param.31) | copy-start | bytes 6148
  43.6 11.8 %copy-start.100 = (f32[1,128]{1,0:T(1,128)S(1)}, f32[1,128]{1,0:T(1,128)}, u32[]{:S(2)}) copy-start(f32[1,128]{1,0:T(1,128)} %param.33) | copy-start | bytes 1540
  51.1 9.7 %copy-start.20 = (f32[256,256]{1,0:T(8,128)}, f32[256,256]{1,0:T(8,128)S(1)}, u32[]{:S(2)}) copy-start(f32[256,256]{1,0:T(8,128)S(1)} %fusion.90) | copy-start | bytes 786436
  55.4 5.4 %copy-start.74 = (f32[1,1,256]{2,1,0:T(1,128)}, f32[1,1,256]{2,1,0:T(1,128)S(1)}, u32[]{:S(2)}) copy-start(f32[1,1,256]{2,1,0:T(1,128)S(1)} %get-tuple-element.411) | copy-start | bytes 3076
  55.4 5.4 %copy-start.76 = (f32[1,1,256]{2,1,0:T(1,128)}, f32[1,1,256]{2,1,0:T(1,128)S(1)}, u32[]{:S(2)}) copy-start(f32[1,1,256]{2,1,0:T(1,128)S(1)} %get-tuple-element.412) | copy-start | bytes 3076
  55.4 5.4 %copy-start.78 = (f32[1,1,256]{2,1,0:T(1,128)}, f32[1,1,256]{2,1,0:T(1,128)S(1)}, u32[]{:S(2)}) copy-start(f32[1,1,256]{2,1,0:T(1,128)S(1)} %get-tuple-element.413) | copy-start | bytes 3076
  113.5 8.5 %copy-start.89 = (s32[256]{0:T(256)S(1)}, s32[256]{0:T(256)}, u32[]{:S(2)}) copy-start(s32[256]{0:T(256)} %param.40) | copy-start | bytes 3076
  113.5 8.5 %copy-start.69 = (s32[256]{0:T(256)S(1)}, s32[256]{0:T(256)}, u32[]{:S(2)}) copy-start(s32[256]{0:T(256)} %param.41) | copy-start | bytes 3076
  113.5 8.5 %copy-start.71 = (s32[256]{0:T(256)S(1)}, s32[256]{0:T(256)}, u32[]{:S(2)}) copy-start(s32[256]{0:T(256)} %copy-done.70) | copy-start | bytes 3076
  113.5 9.0 %copy-start.27 = (bf16[128,1024]{1,0:T(8,128)(2,1)S(1)}, bf16[128,1024]{1,0:T(8,128)(2,1)}, u32[]{:S(2)}) copy-start(bf16[128,1024]{1,0:T(8,128)(2,1)} %param.24) | copy-start | bytes 786436
  113.5 16.2 %copy-start.43 = (f32[1,1024]{1,0:T(1,128)S(1)}, f32[1,1024]{1,0:T(1,128)}, u32[]{:S(2)}) copy-start(f32[1,1024]{1,0:T(1,128)} %param.37) | copy-start | bytes 12292
  122.5 7.2 %copy-start.90 = (f32[128]{0:T(128)}, f32[128]{0:T(128)S(1)}, u32[]{:S(2)}) copy-start(f32[128]{0:T(128)S(1)} %convert_element_type.285) | copy-start | bytes 1540
  129.7 9.7 %copy-start.73 = (f32[256]{0:T(256)S(1)}, f32[256]{0:T(256)}, u32[]{:S(2)}) copy-start(f32[256]{0:T(256)} %copy-done.72) | copy-start | bytes 3076
  150.5 7.4 %copy-start.1 = (f32[4,64,16,64]{1,3,2,0:T(8,128)S(1)}, f32[4,64,16,64]{1,3,2,0:T(8,128)}, u32[]{:S(2)}) copy-start(f32[4,64,16,64]{1,3,2,0:T(8,128)} %copy.211) | copy-start | bytes 3145732
  150.5 7.4 %copy-start.3 = (f32[4,16,64,128]{3,2,1,0:T(8,128)S(1)}, f32[4,16,64,128]{3,2,1,0:T(8,128)}, u32[]{:S(2)}) copy-start(f32[4,16,64,128]{3,2,1,0:T(8,128)} %get-tuple-element.579) | copy-start | bytes 6291460
  190.2 6.0 %copy-start.32 = (f32[4,64,128]{2,1,0:T(8,128)S(1)}, f32[4,64,128]{2,1,0:T(8,128)}, u32[]{:S(2)}) copy-start(f32[4,64,128]{2,1,0:T(8,128)} %fusion.49) | copy-start | bytes 393220
  190.2 6.0 %copy-start.33 = (f32[4,64,64]{2,1,0:T(8,128)S(1)}, f32[4,64,64]{2,1,0:T(8,128)}, u32[]{:S(2)}) copy-start(f32[4,64,64]{2,1,0:T(8,128)} %get-tuple-element.305) | copy-start | bytes 196612
  190.2 6.6 %copy-start.21 = (f32[256,256]{1,0:T(8,128)S(1)}, f32[256,256]{1,0:T(8,128)}, u32[]{:S(2)}) copy-start(f32[256,256]{1,0:T(8,128)} %copy-done.20) | copy-start | bytes 786436
  190.2 6.7 %copy-start.26 = (f32[256,256]{1,0:T(8,128)S(1)}, f32[256,256]{1,0:T(8,128)}, u32[]{:S(2)}) copy-start(f32[256,256]{1,0:T(8,128)} %get-tuple-element.381) | copy-start | bytes 786436
  190.2 6.7 %copy-start.48 = (f32[256]{0:T(256)S(1)}, f32[256]{0:T(256)}, u32[]{:S(2)}) copy-start(f32[256]{0:T(256)} %copy-done.47) | copy-start | bytes 3076
  190.2 6.7 %copy-start.50 = (f32[256]{0:T(256)S(1)}, f32[256]{0:T(256)}, u32[]{:S(2)}) copy-start(f32[256]{0:T(256)} %copy-done.49) | copy-start | bytes 3076
  190.2 6.7 %copy-start.52 = (f32[256]{0:T(256)S(1)}, f32[256]{0:T(256)}, u32[]{:S(2)}) copy-start(f32[256]{0:T(256)} %copy-done.51) | copy-start | bytes 3076
  198.7 58.3 %reduce-scatter.15.cloned.1.call-start = ((), (), s32[]{:S(2)}) async-start(), calls=%async_computation.7 | async-start | bytes 98304
  199.6 58.3 %reduce-scatter.11.cloned.1.call-start = ((), (), s32[]{:S(2)}) async-start(), calls=%async_computation.5 | async-start | bytes 786432 | tf_op jit(solution)/shard_map/reduce_scatter | solution.py:285
  222.1 6.2 %copy-start.15 = (bf16[256,1024]{1,0:T(8,128)(2,1)S(1)}, bf16[256,1024]{1,0:T(8,128)(2,1)}, u32[]{:S(2)}) copy-start(bf16[256,1024]{1,0:T(8,128)(2,1)} %get-tuple-element.388) | copy-start | bytes 1572868
  236.8 93.9 %reduce-scatter.9.cloned.1.call-start = ((), (), s32[]{:S(2)}) async-start(), calls=%async_computation.4 | async-start | bytes 786432 | tf_op jit(solution)/shard_map/reduce_scatter | solution.py:249
  240.3 180.2 %all-reduce.32.cloned.1.call-start = ((), (), s32[]{:S(2)}) async-start(), calls=%async_computation.8 | async-start | bytes 13107200 | tf_op jit(solution)/shard_map/psum | solution.py:166
  248.8 8.0 %copy-start.66 = (f32[1024]{0:T(1024)S(1)}, f32[1024]{0:T(1024)}, u32[]{:S(2)}) copy-start(f32[1024]{0:T(1024)} %get-tuple-element.309) | copy-start | bytes 12292
  248.8 8.0 %copy-start.67 = (f32[1024]{0:T(1024)S(1)}, f32[1024]{0:T(1024)}, u32[]{:S(2)}) copy-start(f32[1024]{0:T(1024)} %get-tuple-element.310) | copy-start | bytes 12292
  248.8 8.0 %copy-start.68 = (f32[1024]{0:T(1024)S(1)}, f32[1024]{0:T(1024)}, u32[]{:S(2)}) copy-start(f32[1024]{0:T(1024)} %get-tuple-element.311) | copy-start | bytes 12292
  248.8 8.2 %copy-start.101 = (f32[1,16]{1,0:T(1,128)S(1)}, f32[1,16]{1,0:T(1,128)}, u32[]{:S(2)}) copy-start(f32[1,16]{1,0:T(1,128)} %param.35) | copy-start | bytes 196
  248.8 9.0 %copy-start.17 = (bf16[128,1024]{1,0:T(8,128)(2,1)S(1)}, bf16[128,1024]{1,0:T(8,128)(2,1)}, u32[]{:S(2)}) copy-start(bf16[128,1024]{1,0:T(8,128)(2,1)} %param.23) | copy-start | bytes 786436
  248.8 9.0 %copy-start.87 = (f32[128]{0:T(128)S(1)}, f32[128]{0:T(128)}, u32[]{:S(2)}) copy-start(f32[128]{0:T(128)} %copy-done.86) | copy-start | bytes 1540
  248.9 81.8 %copy-start.98 = (f32[128]{0:T(128)S(1)}, f32[128]{0:T(128)}, u32[]{:S(2)}) copy-start(f32[128]{0:T(128)} %copy-done.97) | copy-start | bytes 1540
  248.9 81.8 %copy-start.28 = (bf16[128,1024]{1,0:T(8,128)(2,1)S(1)}, bf16[128,1024]{1,0:T(8,128)(2,1)}, u32[]{:S(2)}) copy-start(bf16[128,1024]{1,0:T(8,128)(2,1)} %param.24) | copy-start | bytes 786436
  248.9 81.8 %copy-start.91 = (f32[128]{0:T(128)S(1)}, f32[128]{0:T(128)}, u32[]{:S(2)}) copy-start(f32[128]{0:T(128)} %copy-done.90) | copy-start | bytes 1540
  (60 other events, 151.1 us)
Sparse Core Ops, SparseCore 0:
  198.9 11.6 reduce-scatter.12
  213.3 9.8 reduce-scatter.14
  236.9 16.0 reduce-scatter.10
  255.7 14.5 reduce-scatter.8
  275.4 145.0 all-reduce.31
where the time goes:
time: 443 us; the launch traced here: 437 us
  blocking collectives  117 us (26%)
  waiting for transfers between devices  87.5 us (20%)
  other arithmetic  83 us (19%)
  matrix products  74.7 us (17%)
  local copies, waits for them, and re-layouts  57.6 us (13%)
  between operations  16.5 us (4%)
    psum x1, waiting for transfers between devices, sum_replicas(): lax.psum(parts[1].astype(jnp.bfloat16), 'rep').astype(jnp.float32)  87.4 us
    psum x1, blocking collectives, sum_replicas(): lax.psum(parts[0].astype(jnp.bfloat16), 'rep').astype(jnp.float32)  60.9 us
    dot_general x3, matrix products, mixer_core(): jnp.einsum('bhts,bshp->bthp', mixing, head_values, precision=HIGHEST)  18.2 us
    dot_general x3, matrix products, mixer_core(): jnp.einsum('bshp,bsn->bhpn', weighted_values, key_rows, precision=HIGHEST)  15.1 us
    dynamic_update_slice x12, other arithmetic, mixer_core(): lax.scan(carry_state, start_state, (local_states, span_total, keep_flags))  11.4 us
    dot_general x3, matrix products, mixer_core(): jnp.einsum('btn,bhpn->bthp', query_rows, incoming, precision=HIGHEST)  11.1 us
    unnamed x2, blocking collectives  10.1 us
    dynamic_slice x8, local copies, waits for them, and re-layouts, mixer_core(): lax.scan(carry_state, start_state, (local_states, span_total, keep_flags))  9.92 us
  transfers between devices with their start and end apart: 5, of which 1 were waited for; matrix products, arithmetic and copies ran while one was open for 13% of the time, Pallas kernels for 0%

commit v1 on v0

v1 whole, which is shorter than its diff:
```python
from functools import partial

import jax
import jax.numpy as jnp
from jax import lax
from jax.experimental import pallas as pl
from jax.experimental.pallas import tpu as pltpu
from jax.sharding import PartitionSpec as P

epsilon = 1e-05
PARTS = 4
F32 = jnp.float32
BF16 = jnp.bfloat16
HEADS = 32
STATE = 128


def exchange(array, axis, bit):
    count = lax.axis_size(axis)
    return lax.ppermute(array, axis, [(i, i ^ bit) for i in range(count)])


def mm(left, right):
    return lax.dot_general(left, right, (((1,), (0,)), ((), ())), preferred_element_type=F32)


def mm_rt(left, right):
    return lax.dot_general(left, right, (((1,), (1,)), ((), ())), preferred_element_type=F32)


def mm_lt(left, right):
    return lax.dot_general(left, right, (((0,), (0,)), ((), ())), preferred_element_type=F32)


def whole(array):
    zeros = (0,) * array.ndim
    return (array, pl.BlockSpec(array.shape, lambda *_: zeros))


def chunked(array):
    tail = (0,) * (array.ndim - 1)
    return (array, pl.BlockSpec((1,) + array.shape[1:], lambda c, dev: (c,) + tail))


def columns(array, width):
    if width % 128 == 0:
        return (array, pl.BlockSpec((array.shape[0], width), lambda c, dev: (0, c)))
    pieces = array.reshape(array.shape[0], -1, width).transpose(1, 0, 2)
    return (pieces, pl.BlockSpec((None, array.shape[0], width), lambda c, dev: (c, 0, 0)))


def rows(array, height):
    return (array, pl.BlockSpec((height, array.shape[1]), lambda c, dev: (c, 0)))


def out_whole(shape, dtype):
    zeros = (0,) * len(shape)
    return (jax.ShapeDtypeStruct(shape, dtype), pl.BlockSpec(shape, lambda *_: zeros))


def out_chunked(shape, dtype):
    tail = (0,) * (len(shape) - 1)
    spec = pl.BlockSpec((1,) + shape[1:], lambda c, dev: (c,) + tail)
    return (jax.ShapeDtypeStruct(shape, dtype), spec)


def run(body, name, device, ins, outs, steps, scratch=(), flops=0):
    total = sum(a.size * a.dtype.itemsize for a, _ in ins)
    total += sum(s.size * s.dtype.itemsize for s, _ in outs)
    return pl.pallas_call(
        body,
        name=name,
        out_shape=[shape for shape, _ in outs],
        grid_spec=pltpu.PrefetchScalarGridSpec(
            num_scalar_prefetch=1,
            grid=(steps,),
            in_specs=[spec for _, spec in ins],
            out_specs=[spec for _, spec in outs],
            scratch_shapes=list(scratch),
        ),
        compiler_params=pltpu.CompilerParams(dimension_semantics=("arbitrary",)),
        cost_estimate=pl.CostEstimate(flops=flops, bytes_accessed=total, transcendentals=0),
    )(device, *[a for a, _ in ins])


def iota(shape, dim):
    return lax.broadcasted_iota(jnp.int32, shape, dim)


def roll_rows(array, shift):
    if array.shape[1] % 128 == 0:
        return pltpu.roll(array, shift % array.shape[0], 0)
    return jnp.roll(array, shift, 0)


def conv_rows(inputs, taps, bias, marks):
    result = bias + taps[3:4] * inputs
    for offset in range(1, 4):
        shifted = roll_rows(inputs, offset) * marks[:, offset : offset + 1]
        result = result + taps[3 - offset : 4 - offset] * shifted
    return result


def conv_back(d_out, inputs, taps, marks):
    d_in = taps[3:4] * d_out
    grads = [None] * 4
    grads[3] = jnp.sum(d_out * inputs, axis=0, keepdims=True)
    for offset in range(1, 4):
        kept = d_out * marks[:, offset : offset + 1]
        d_in = d_in + taps[3 - offset : 4 - offset] * roll_rows(kept, -offset)
        grads[3 - offset] = jnp.sum(kept * roll_rows(inputs, offset), axis=0, keepdims=True)
    return d_in, grads, jnp.sum(d_out, axis=0, keepdims=True)


def softplus(value):
    return jnp.maximum(value, 0.0) + jnp.log1p(jnp.exp(-jnp.abs(value)))


def solution(mesh):
    members = mesh.shape["shard"]
    replicas = mesh.shape["rep"]
    assert replicas % PARTS == 0 and replicas // PARTS >= 2
    assert replicas & (replicas - 1) == 0 and members & (members - 1) == 0
    return jax.shard_map(
        partial(on_device, members, replicas),
        mesh=mesh,
        in_specs=(
            P(("rep", "shard"), None),
            P(("rep", "shard"), None),
            P(None, "shard"),
            P(None, None, "shard"),
            P(None, None, "shard"),
            P(None, None, "shard"),
            P(None, None, "shard"),
            P(None, None, "shard"),
            P(None, None, "shard"),
            P(None, "shard"),
            P(None, "shard"),
            P(None, "shard"),
            P(None, "shard"),
            P(None, "shard"),
            P(None, "shard"),
            P(None, "shard", None),
            P(),
            P(),
            P(),
        ),
        out_specs=(
            P(("rep", "shard"), None),
            P(("rep", "shard"), None),
            P(None, "shard"),
            P(None, None, "shard"),
            P(None, None, "shard"),
            P(None, None, "shard"),
            P(None, None, "shard"),
            P(None, None, "shard"),
            P(None, None, "shard"),
            P(None, "shard"),
            P(None, "shard"),
            P(None, "shard"),
            P(None, "shard"),
            P(None, "shard"),
            P(None, "shard"),
            P(None, "shard", None),
        ),
        check_vma=False,
    )


def on_device(
    members,
    replicas,
    hidden_in,
    cotangent,
    norm_gain,
    w_z,
    w_x,
    w_bc,
    w_dt,
    conv_x,
    conv_bc,
    bias_x,
    bias_bc,
    dt_bias,
    a_log,
    d_skip,
    gate_gain,
    w_out,
    seq_len,
    seq_owner,
    seq_start,
):
    S = members
    T, D = hidden_in.shape
    R = S * T
    C = w_z.shape[2]
    H = w_dt.shape[2]
    NB = w_bc.shape[2]
    CH = C // PARTS
    HC = H // PARTS
    HS = C // H
    inner = C * S
    spans = replicas // PARTS
    DCH = D // spans
    w_z, w_x, w_bc, w_dt, w_out = w_z[0], w_x[0], w_bc[0], w_dt[0], w_out[0]

    shard_at = lax.axis_index("shard")
    device = (lax.axis_index("rep") * S + shard_at).astype(jnp.int32).reshape(1)

    def me_of(dev):
        return lax.rem(dev[0], S)

    def part_of(dev):
        return lax.rem(lax.div(dev[0], S), PARTS)

    def span_of(dev):
        return lax.div(dev[0], S * PARTS)

    blocks = [slice(b * T, (b + 1) * T) for b in range(S)]

    if S == 2:
        gain_other = exchange(norm_gain, "shard", 1)
        first = shard_at == 0
        gain = jnp.concatenate(
            [
                jnp.where(first, norm_gain, gain_other),
                jnp.where(first, gain_other, norm_gain),
            ],
            axis=1,
        )
    else:
        gain = lax.all_gather(norm_gain, "shard", axis=1, tiled=True)
    hidden = [hidden_in] + [exchange(hidden_in, "shard", j) for j in range(1, S)]
    cots = [cotangent] + [exchange(cotangent, "shard", j) for j in range(1, S)]

    lens = seq_len.reshape(1, -1)
    owners = seq_owner.reshape(1, -1)
    starts = seq_start.reshape(1, -1)
    records = lens.shape[1]
    taps_bc = jnp.concatenate([conv_bc[0], bias_bc, jnp.zeros((3, NB), F32)], axis=0)
    taps_x = jnp.concatenate(
        [
            conv_x[0],
            bias_x,
            gate_gain,
            jnp.repeat(d_skip, HS, axis=1),
            jnp.zeros((1, C), F32),
        ],
        axis=0,
    )
    wdt_parts = jnp.pad(
        w_dt.reshape(D, PARTS, HC).transpose(1, 0, 2), ((0, 0), (0, 0), (0, 128 - HC))
    )
    head_rows = jnp.concatenate([dt_bias, a_log], axis=0).reshape(2, PARTS, HC)
    head_rows = jnp.pad(head_rows.transpose(1, 0, 2), ((0, 0), (0, 6), (0, 128 - HC)))

    def prepare(dev, ln, ow, st, gain_r, wbc, tbc, *refs):
        hid, refs = refs[:S], refs[S:]
        normed_r, mask_r, cols_r, pbc_r, pre_r, map_r = refs[:6]
        sends = refs[6:]
        me = me_of(dev)
        base = dev[0] - me
        lane = iota((T, 128), 1)
        row = iota((T, 128), 0)
        for b in range(S):
            x = hid[b][...].astype(F32)
            scale = lax.rsqrt(jnp.mean(x * x, axis=1, keepdims=True) + epsilon)
            normed_r[blocks[b], :] = (x * scale * gain_r[...]).astype(BF16)
            slot = iota((T, records), 0)
            covers = (
                (ow[...] == base + (me ^ b)) & (slot >= st[...]) & (slot < st[...] + ln[...])
            )
            ids = iota((T, records), 1).astype(F32)
            used = jnp.sum(jnp.where(covers, 1.0, 0.0), axis=1, keepdims=True)
            found = jnp.sum(jnp.where(covers, ids, 0.0), axis=1, keepdims=True)
            lone = (records + row).astype(F32)
            seg = jnp.where(used > 0.5, found, lone)
            seg_t = seg.T
            same = (seg == seg_t) & (row >= lane)
            mask_r[blocks[b], :] = jnp.where(same, 1.0, 0.0)
            cols = jnp.where(lane == 0, used, 0.0)
            for offset in range(1, 4):
                mark = (pltpu.roll(seg, offset, 0) == seg) & (row >= offset)
                cols = jnp.where(lane == offset, jnp.where(mark, 1.0, 0.0), cols)
            cols_r[blocks[b], :] = cols
        pbc_r[...] = mm(normed_r[...], wbc[...])
        for b in range(S):
            marks = cols_r[blocks[b], :]
            pre = conv_rows(pbc_r[blocks[b], :], tbc[...], tbc[4:5], marks)
            pre_r[blocks[b], :] = pre
            out = (pre * jax.nn.sigmoid(pre)).astype(BF16)
            map_r[blocks[b], :] = out
            for j in range(1, S):
                sends[j - 1][blocks[b ^ j], :] = out

    outs = run(
        prepare,
        "norm_and_maps",
        device,
        [whole(a) for a in (lens, owners, starts, gain, w_bc, taps_bc, *hidden)],
        [
            out_whole((R, D), BF16),
            out_whole((R, 128), F32),
            out_whole((R, 128), F32),
            out_whole((R, NB), F32),
            out_whole((R, NB), F32),
            out_whole((R, NB), BF16),
        ]
        + [out_whole((R, NB), BF16) for _ in range(1, S)],
        1,
        flops=2 * R * D * NB,
    )
    normed, mask, cols, proj_bc, pre_bc, map_own = outs[:6]
    maps = [map_own] + [exchange(outs[5 + j], "shard", j) for j in range(1, S)]
    if S == 2:
        map_a, map_b = maps
    else:
        map_a = jnp.concatenate(maps[: S // 2], axis=1)
        map_b = jnp.concatenate(maps[S // 2 :], axis=1)

    normed_far = exchange(normed, "rep", 2)
    normed_all = [normed, exchange(normed, "rep", 1), normed_far, exchange(normed_far, "rep", 1)]
    cots_far = [exchange(c, "rep", 2) for c in cots]
    cots_all = [
        cots,
        [exchange(c, "rep", 1) for c in cots],
        cots_far,
        [exchange(c, "rep", 1) for c in cots_far],
    ]

    def project(dev, n_r, wz, wx, wdt, hp, tx, cols_r, wo, *refs):
        cot, refs = refs[:S], refs[S:]
        z_r, x_r, pre_r, y_r, cum_r, cumt_r, dm_r = refs
        n = n_r[...]
        z_r[0] = mm(n, wz[...])
        x_r[0] = mm(n, wx[...])
        y_r[0] = mm(n, wdt[0]) + hp[0, 0:1, :]
        row = iota((T, 128), 0)
        for b in range(S):
            marks = cols_r[blocks[b], :]
            pre_r[0, blocks[b], :] = conv_rows(x_r[0, blocks[b], :], tx[...], tx[4:5], marks)
            total = -softplus(y_r[0, blocks[b], :]) * jnp.exp(hp[0, 1:2, :])
            shift = 1
            while shift < T:
                total = total + jnp.where(row >= shift, pltpu.roll(total, shift, 0), 0.0)
                shift *= 2
            cum_r[0, blocks[b], :] = total
            cumt_r[0, b] = total.T[0:8]
            dm_r[0, blocks[b], :] = mm_rt(cot[b][...], wo[...]) * marks[:, 0:1]

    z, px, pre, y, cum, cum_t, d_mixed = run(
        project,
        "projections",
        device,
        [
            whole(normed),
            columns(w_z, CH),
            columns(w_x, CH),
            chunked(wdt_parts),
            chunked(head_rows),
            columns(taps_x, CH),
            whole(cols),
            rows(w_out, CH),
        ]
        + [whole(c) for c in cots],
        [
            out_chunked((PARTS, R, CH), F32),
            out_chunked((PARTS, R, CH), F32),
            out_chunked((PARTS, R, CH), F32),
            out_chunked((PARTS, R, 128), F32),
            out_chunked((PARTS, R, 128), F32),
            out_chunked((PARTS, S, 8, 128), F32),
            out_chunked((PARTS, R, CH), F32),
        ],
        PARTS,
        flops=6 * R * D * C,
    )

    def fill_scores(dev, a_r, b_r, mask_r, scores):
        a_is_key = me_of(dev) < S // 2
        for b in range(S):

            @pl.when(a_is_key)
            def _():
                scores[b] = mm_rt(b_r[blocks[b], :], a_r[blocks[b], :]) * mask_r[blocks[b], :]

            @pl.when(jnp.logical_not(a_is_key))
            def _():
                scores[b] = mm_rt(a_r[blocks[b], :], b_r[blocks[b], :]) * mask_r[blocks[b], :]

    def scan_forward(dev, a_r, b_r, mask_r, pre_r, y_r, cum_r, cumt_r, tx, z_r, dm_r, wo, *refs):
        core_r, sums_r, own_r = refs[0], refs[1], refs[2]
        sum_sends = refs[3 : 2 + S]
        sends = refs[2 + S : 1 + 2 * S]
        scores, acc, sums, gated_s = refs[1 + 2 * S :]
        c = pl.program_id(0)

        @pl.when(c == 0)
        def _():
            fill_scores(dev, a_r, b_r, mask_r, scores)
            acc[...] = jnp.zeros_like(acc)
            sums[...] = jnp.zeros_like(sums)

        lane = iota((T, 128), 1)
        for b in range(S):
            before = pre_r[0, blocks[b], :]
            values = before * jax.nn.sigmoid(before)
            step = softplus(y_r[0, blocks[b], :])
            parts = []
            for h in range(HC):
                at = slice(h * HS, (h + 1) * HS)
                gap = cum_r[0, blocks[b], h : h + 1] - cumt_r[0, b, h : h + 1, :]
                weights = (scores[b] * jnp.exp(jnp.minimum(gap, 0.0))).astype(BF16)
                scaled = (values[:, at] * step[:, h : h + 1]).astype(BF16)
                parts.append(mm(weights, scaled))
            core = jnp.concatenate(parts, axis=1) + values * tx[6:7]
            core_r[0, blocks[b], :] = core
            zed = z_r[0, blocks[b], :]
            gated = core * (zed * jax.nn.sigmoid(zed))
            gained = gated * tx[5:6]
            gated_s[blocks[b], :] = gained.astype(BF16)
            squares = jnp.sum(gated * gated, axis=1, keepdims=True)
            dots = jnp.sum(dm_r[0, blocks[b], :] * gained, axis=1, keepdims=True)
            sums[blocks[b], :] += jnp.where(lane == 0, squares, jnp.where(lane == 1, dots, 0.0))
        acc[...] += mm(gated_s[...], wo[...])

        @pl.when(c == PARTS - 1)
        def _():
            own_r[...] = acc[blocks[0], :]
            for j in range(1, S):
                sends[j - 1][...] = acc[blocks[j], :].astype(BF16)
            for b in range(S):
                turned = sums[blocks[b], :].T[0:8]
                sums_r[:, blocks[b]] = turned
                for j in range(1, S):
                    sum_sends[j - 1][:, blocks[b ^ j]] = turned

    outs = run(
        scan_forward,
        "scan_forward",
        device,
        [
            whole(map_a),
            whole(map_b),
            whole(mask),
            chunked(pre),
            chunked(y),
            chunked(cum),
            chunked(cum_t),
            columns(taps_x, CH),
            chunked(z),
            chunked(d_mixed),
            rows(w_out, CH),
        ],
        [
            out_chunked((PARTS, R, CH), F32),
            out_whole((8, R), F32),
            out_whole((T, D), F32),
        ]
        + [out_whole((8, R), F32) for _ in range(1, S)]
        + [out_whole((T, D), BF16) for _ in range(1, S)],
        PARTS,
        scratch=[
            pltpu.VMEM((S, T, T), F32),
            pltpu.VMEM((R, D), F32),
            pltpu.VMEM((R, 128), F32),
            pltpu.VMEM((R, CH), BF16),
        ],
        flops=2 * R * D * C + 4 * R * T * C,
    )
    core, sums_own, out_own = outs[:3]
    sums_all = [sums_own] + [exchange(outs[2 + j], "shard", j) for j in range(1, S)]
    out_other = [exchange(outs[1 + S + j], "shard", j) for j in range(1, S)]

    def gate_backward(dev, core_r, z_r, dm_r, tx, cols_r, *refs):
        parts, refs = refs[:S], refs[S:]
        mixed_r, cotz_r = refs[:PARTS], refs[PARTS : 2 * PARTS]
        cotz_c, dcore_r, gg_r, rows_r = refs[2 * PARTS :]
        c = pl.program_id(0)
        lane = iota((T, 128), 1)

        @pl.when(c == 0)
        def _():
            for b in range(S):
                total = parts[0][:, blocks[b]]
                for j in range(1, S):
                    total = total + parts[j][:, blocks[b]]
                turned = jnp.concatenate([total, jnp.zeros((T - 8, 128), F32)], axis=0).T
                inverse = lax.rsqrt(turned[:, 0:1] / inner + epsilon)
                factor = inverse * inverse * inverse * turned[:, 1:2] / inner
                rows_r[blocks[b], :] = jnp.where(
                    lane == 0, inverse, jnp.where(lane == 1, factor, 0.0)
                )

        gate_sum = jnp.zeros((1, CH), F32)
        mixed_parts, cot_parts = [], []
        for b in range(S):
            inverse = rows_r[blocks[b], 0:1]
            factor = rows_r[blocks[b], 1:2]
            used = cols_r[blocks[b], 0:1]
            core = core_r[0, blocks[b], :]
            zed = z_r[0, blocks[b], :]
            sig = jax.nn.sigmoid(zed)
            gated = core * (zed * sig)
            d_mixed = dm_r[0, blocks[b], :]
            scaled = gated * inverse
            gate_sum = gate_sum + jnp.sum(d_mixed * scaled, axis=0, keepdims=True)
            d_gated = inverse * (d_mixed * tx[5:6]) - gated * factor
            dcore_r[0, blocks[b], :] = (d_gated * (zed * sig)).astype(BF16)
            d_z = d_gated * core * sig * (1.0 + zed * (1.0 - sig))
            mixed_parts.append((scaled * tx[5:6] * used).astype(BF16))
            cot_parts.append(d_z.astype(BF16))
            cotz_c[0, blocks[b], :] = cot_parts[b]
        gg_r[0] = jnp.broadcast_to(gate_sum, (8, CH))
        mine = part_of(dev)
        for r in range(PARTS):

            @pl.when((c ^ mine) == r)
            def _():
                for b in range(S):
                    mixed_r[r][blocks[b], :] = mixed_parts[b]
                    cotz_r[r][blocks[b], :] = cot_parts[b]

    outs = run(
        gate_backward,
        "gate_backward",
        device,
        [chunked(core), chunked(z), chunked(d_mixed), columns(taps_x, CH), whole(cols)]
        + [whole(s) for s in sums_all],
        [out_whole((R, CH), BF16) for _ in range(2 * PARTS)]
        + [
            out_chunked((PARTS, R, CH), BF16),
            out_chunked((PARTS, R, CH), BF16),
            out_chunked((PARTS, 8, CH), F32),
            out_whole((R, 128), F32),
        ],
        PARTS,
        flops=40 * R * C,
    )
    mixed_parts, cotz_parts = outs[:PARTS], outs[PARTS : 2 * PARTS]
    cotz, d_core, gate_grads, row_scale = outs[2 * PARTS :]

    def quarter(parts):
        return [parts[0]] + [exchange(parts[r], "rep", r) for r in range(1, PARTS)]

    mixed_q = quarter(mixed_parts)
    cotz_q = quarter(cotz_parts)

    def scan_backward(
        dev, a_r, b_r, mask_r, pre_r, px_r, y_r, cum_r, cumt_r, hp, tx, core_r, dcore_r, cols_r, *refs
    ):
        cotx_r, refs = refs[:PARTS], refs[PARTS:]
        cotx_c, cdt_r, cg_r, hg_r, own_r = refs[:5]
        sends = refs[5 : 4 + S]
        scores, d_scores = refs[4 + S :]
        c = pl.program_id(0)

        @pl.when(c == 0)
        def _():
            fill_scores(dev, a_r, b_r, mask_r, scores)
            d_scores[...] = jnp.zeros_like(d_scores)

        lane = iota((T, 128), 1)
        row = iota((T, 128), 0)
        lane1 = iota((1, 128), 1)
        tap_grads = [jnp.zeros((1, CH), F32) for _ in range(5)]
        bias_grad = jnp.zeros((1, 128), F32)
        rate_grad = jnp.zeros((1, 128), F32)
        skip_grad = jnp.zeros((1, 128), F32)
        cot_parts = []
        rate = jnp.exp(hp[0, 1:2, :])
        for b in range(S):
            before = pre_r[0, blocks[b], :]
            sig = jax.nn.sigmoid(before)
            values = before * sig
            raw = y_r[0, blocks[b], :]
            step = softplus(raw)
            d_core_b = dcore_r[0, blocks[b], :]
            d_core_f = d_core_b.astype(F32)
            skip = values * tx[6:7]
            plain = core_r[0, blocks[b], :] - skip
            d_cum = jnp.zeros((T, 128), F32)
            d_step = jnp.zeros((T, 128), F32)
            d_values = []
            for h in range(HC):
                at = slice(h * HS, (h + 1) * HS)
                gap = cum_r[0, blocks[b], h : h + 1] - cumt_r[0, b, h : h + 1, :]
                decay = jnp.exp(jnp.minimum(gap, 0.0))
                weights = (scores[b] * decay).astype(BF16)
                v = values[:, at]
                scaled = (v * step[:, h : h + 1]).astype(BF16)
                d_out = d_core_b[:, at]
                d_out_f = d_core_f[:, at]
                d_scores[b] += mm_rt(d_out, scaled) * decay
                d_scaled = mm_lt(weights, d_out)
                change = jnp.sum(
                    d_out_f * plain[:, at] - d_scaled * scaled.astype(F32), axis=1, keepdims=True
                )
                d_cum = jnp.where(lane == h, change, d_cum)
                d_step = jnp.where(
                    lane == h, jnp.sum(d_scaled * v, axis=1, keepdims=True), d_step
                )
                d_values.append(d_scaled * step[:, h : h + 1])
                skip_grad = skip_grad + jnp.where(lane1 == h, jnp.sum(d_out_f * v), 0.0)
            shift = 1
            while shift < T:
                d_cum = d_cum + jnp.where(row < T - shift, pltpu.roll(d_cum, T - shift, 0), 0.0)
                shift *= 2
            rate_grad = rate_grad - jnp.sum(d_cum * step, axis=0, keepdims=True) * rate
            d_raw = (d_step - d_cum * rate) * jax.nn.sigmoid(raw)
            d_raw = jnp.where(lane < HC, d_raw, 0.0)
            bias_grad = bias_grad + jnp.sum(d_raw, axis=0, keepdims=True)
            cdt_r[0, blocks[b], :] = d_raw
            d_val = jnp.concatenate(d_values, axis=1) + d_core_f * tx[6:7]
            d_pre = d_val * sig * (1.0 + before * (1.0 - sig))
            d_in, grads, total = conv_back(
                d_pre, px_r[0, blocks[b], :], tx[...], cols_r[blocks[b], :]
            )
            for i, grad in enumerate(grads + [total]):
                tap_grads[i] = tap_grads[i] + grad
            cot_parts.append(d_in.astype(BF16))
            cotx_c[0, blocks[b], :] = cot_parts[b]
        cg_r[0] = jnp.concatenate(tap_grads + [jnp.zeros((3, CH), F32)], axis=0)
        hg_r[0] = jnp.concatenate(
            [bias_grad, rate_grad, skip_grad, jnp.zeros((5, 128), F32)], axis=0
        )
        mine = part_of(dev)
        for r in range(PARTS):

            @pl.when((c ^ mine) == r)
            def _():
                for b in range(S):
                    cotx_r[r][blocks[b], :] = cot_parts[b]

        @pl.when(c == PARTS - 1)
        def _():
            a_is_key = me_of(dev) < S // 2

            def finish(key_first):
                for b in range(S):
                    d_s = (d_scores[b] * mask_r[blocks[b], :]).astype(BF16)
                    a, bb = a_r[blocks[b], :], b_r[blocks[b], :]
                    if key_first:
                        both = (mm_lt(d_s, bb), mm(d_s, a))
                    else:
                        both = (mm(d_s, bb), mm_lt(d_s, a))
                    for j in range(S):
                        half = both[0] if j < S // 2 else both[1]
                        at = (j % (S // 2)) * NB
                        piece = half[:, at : at + NB]
                        if j == 0:
                            own_r[blocks[b], :] = piece
                        else:
                            sends[j - 1][blocks[b ^ j], :] = piece.astype(BF16)

            @pl.when(a_is_key)
            def _():
                finish(True)

            @pl.when(jnp.logical_not(a_is_key))
            def _():
                finish(False)

    outs = run(
        scan_backward,
        "scan_backward",
        device,
        [
            whole(map_a),
            whole(map_b),
            whole(mask),
            chunked(pre),
            chunked(px),
            chunked(y),
            chunked(cum),
            chunked(cum_t),
            chunked(head_rows),
            columns(taps_x, CH),
            chunked(core),
            chunked(d_core),
            whole(cols),
        ],
        [out_whole((R, CH), BF16) for _ in range(PARTS)]
        + [
            out_chunked((PARTS, R, CH), BF16),
            out_chunked((PARTS, R, 128), F32),
            out_chunked((PARTS, 8, CH), F32),
            out_chunked((PARTS, 8, 128), F32),
            out_whole((R, NB), F32),
        ]
        + [out_whole((R, NB), BF16) for _ in range(1, S)],
        PARTS,
        scratch=[pltpu.VMEM((S, T, T), F32), pltpu.VMEM((S, T, T), F32)],
        flops=8 * R * T * C,
    )
    cotx_parts = outs[:PARTS]
    cotx, cot_dt, tap_grads, head_grads, d_map_own = outs[PARTS : PARTS + 5]
    d_map_other = [exchange(outs[PARTS + 4 + j], "shard", j) for j in range(1, S)]
    cotx_q = quarter(cotx_parts)

    def input_backward(dev, cz, cx, cdt, wz, wx, wdt, dn_r, dt_r):
        c = pl.program_id(0)

        @pl.when(c == 0)
        def _():
            joined = cdt[0]
            for i in range(1, PARTS):
                joined = joined + pltpu.roll(cdt[i], i * HC, 1)
            joined = joined.astype(BF16)
            dt_r[...] = joined
            dn_r[...] = mm_rt(joined[:, 0:H], wdt[...])

        dn_r[...] += mm_rt(cz[0], wz[...]) + mm_rt(cx[0], wx[...])

    d_normed, cot_dt_all = run(
        input_backward,
        "input_backward",
        device,
        [
            chunked(cotz),
            chunked(cotx),
            whole(cot_dt),
            columns(w_z, CH),
            columns(w_x, CH),
            whole(w_dt),
        ],
        [out_whole((R, D), F32), out_whole((R, 128), BF16)],
        PARTS,
        flops=4 * R * D * C,
    )

    small_rows = -(-(NB + H + 16) // 16) * 16

    def maps_backward(
        dev, own, pre_r, pbc_r, cols_r, tbc, n_r, wbc, dn_r, cdt, cg, hg, gg, *refs
    ):
        others, hid, refs = refs[: S - 1], refs[S - 1 : 2 * S - 1], refs[2 * S - 1 :]
        dn_own, pack_r = refs[0], refs[1]
        sends = refs[2 : 1 + S]
        cot_s, dn_s = refs[1 + S :]
        pack_r[...] = jnp.zeros_like(pack_r)
        grads = [jnp.zeros((1, NB), F32) for _ in range(5)]
        for b in range(S):
            d_map = own[blocks[b], :]
            for other in others:
                d_map = d_map + other[blocks[b], :].astype(F32)
            before = pre_r[blocks[b], :]
            sig = jax.nn.sigmoid(before)
            d_pre = d_map * sig * (1.0 + before * (1.0 - sig))
            d_in, taps, total = conv_back(d_pre, pbc_r[blocks[b], :], tbc[...], cols_r[blocks[b], :])
            for i, grad in enumerate(taps + [total]):
                grads[i] = grads[i] + grad
            cot_s[blocks[b], :] = d_in.astype(BF16)
        dn_s[...] = dn_r[...] + mm_rt(cot_s[...], wbc[...])
        dn_own[...] = dn_s[blocks[0], :]
        gain_sum = jnp.zeros((1, D), F32)
        for b in range(S):
            x = hid[b][...].astype(F32)
            scale = lax.rsqrt(jnp.mean(x * x, axis=1, keepdims=True) + epsilon)
            part = dn_s[blocks[b], :]
            gain_sum = gain_sum + jnp.sum(part * (x * scale), axis=0, keepdims=True)
            if b > 0:
                sends[b - 1][...] = part.astype(BF16)
        pack_r[0:NB, :] = mm_lt(cot_s[...], n_r[...])
        pack_r[NB : NB + H, :] = mm_lt(cdt[...], n_r[...])[0:H]
        at = NB + H
        for i in range(PARTS):
            pack_r[at : at + 5, i * CH : (i + 1) * CH] = cg[i, 0:5]
            pack_r[at + 5 : at + 6, i * CH : (i + 1) * CH] = gg[i, 0:1]
            pack_r[at + 6 : at + 9, i * 128 : (i + 1) * 128] = hg[i, 0:3]
        for i in range(5):
            pack_r[at + 9 + i : at + 10 + i, 0:NB] = grads[i]
        pack_r[at + 14 : at + 15, :] = gain_sum

    outs = run(
        maps_backward,
        "maps_backward",
        device,
        [
            whole(a)
            for a in (
                d_map_own,
                pre_bc,
                proj_bc,
                cols,
                taps_bc,
                normed,
                w_bc,
                d_normed,
                cot_dt_all,
                tap_grads,
                head_grads,
                gate_grads,
                *d_map_other,
                *hidden,
            )
        ],
        [out_whole((T, D), F32), out_whole((small_rows, D), F32)]
        + [out_whole((T, D), BF16) for _ in range(1, S)],
        1,
        scratch=[pltpu.VMEM((R, NB), BF16), pltpu.VMEM((R, D), F32)],
        flops=2 * R * D * (2 * NB + 128),
    )
    dn_own, pack = outs[:2]
    dn_other = [exchange(outs[1 + j], "shard", j) for j in range(1, S)]

    def own_rows(dev, hid, cot, cols_r, rows_r, gain_r, dn_r, out_r, *refs):
        dns, outs_o, refs = refs[: S - 1], refs[S - 1 : 2 * S - 2], refs[2 * S - 2 :]
        hidden_r, grad_r = refs
        used = cols_r[:, 0:1]
        x = hid[...].astype(F32)
        added = out_r[...]
        for other in outs_o:
            added = added + other[...].astype(F32)
        hidden_r[...] = used * (x + rows_r[:, 0:1] * added)
        d_n = dn_r[...]
        for other in dns:
            d_n = d_n + other[...].astype(F32)
        scale = lax.rsqrt(jnp.mean(x * x, axis=1, keepdims=True) + epsilon)
        u = d_n * gain_r[...]
        dot = jnp.mean(u * x, axis=1, keepdims=True)
        grad_r[...] = used * cot[...].astype(F32) + scale * u - x * (scale * scale * scale * dot)

    hidden_out, grad_hidden = run(
        own_rows,
        "own_rows",
        device,
        [
            whole(hidden_in),
            whole(cotangent),
            (cols, pl.BlockSpec((T, 128), lambda *_: (0, 0))),
            (row_scale, pl.BlockSpec((T, 128), lambda *_: (0, 0))),
        ]
        + [whole(a) for a in (gain, dn_own, out_own, *dn_other, *out_other)],
        [out_whole((T, D), F32), out_whole((T, D), F32)],
        1,
    )

    def split_specs(shape):
        half = spans // 2
        send = pl.BlockSpec((1,) + shape, lambda i, dev: (jnp.minimum(i, half - 1), 0, 0))
        keep = pl.BlockSpec((1,) + shape, lambda i, dev: (jnp.maximum(i - half, 0), 0, 0))
        return [
            (jax.ShapeDtypeStruct((half,) + shape, BF16), send),
            (jax.ShapeDtypeStruct((half,) + shape, F32), keep),
        ]

    def relative(i):
        half = spans // 2
        return jnp.where(i < half, 2 * i + 1, 2 * (i - half))

    def by_span(array):
        height = array.shape[0]
        return (array, pl.BlockSpec((height, DCH), lambda i, dev: (0, span_of(dev) ^ relative(i))))

    def store_split(value, send_r, keep_r):
        i = pl.program_id(0)

        @pl.when(i < spans // 2)
        def _():
            send_r[0] = value.astype(BF16)

        @pl.when(i >= spans // 2)
        def _():
            keep_r[0] = value

    def in_weight_grad(dev, *refs):
        value = mm_lt(refs[0][...], refs[PARTS][...])
        for r in range(1, PARTS):
            value = value + mm_lt(refs[r][...], refs[PARTS + r][...])
        store_split(value, *refs[2 * PARTS :])

    def out_weight_grad(dev, *refs):
        value = jnp.zeros((CH, DCH), F32)
        for r in range(PARTS):
            for b in range(S):
                value = value + mm_lt(refs[r][blocks[b], :], refs[PARTS + r * S + b][...])
        store_split(value, *refs[PARTS + PARTS * S :])

    def sum_spans(send, keep):
        bit = PARTS
        total = keep + exchange(send, "rep", bit).astype(F32)
        while total.shape[0] > 1:
            bit *= 2
            send = total[1::2].astype(BF16)
            total = total[0::2] + exchange(send, "rep", bit).astype(F32)
        held = total.astype(BF16)
        while bit >= PARTS:
            held = jnp.concatenate([held, exchange(held, "rep", bit)], axis=0)
            bit //= 2
        far = exchange(held, "rep", 2)
        return [held, exchange(held, "rep", 1), far, exchange(far, "rep", 1)]

    def reversed_bits(i):
        result = jnp.int32(0) * i
        width = spans.bit_length() - 1
        for b in range(width):
            result = result | (((i >> b) & 1) << (width - 1 - b))
        return result

    def join_in(dev, *refs):
        mine = part_of(dev)
        for m in range(PARTS):

            @pl.when(mine == m)
            def _():
                for r in range(PARTS):
                    refs[PARTS][:, (m ^ r) * CH : ((m ^ r) + 1) * CH] = refs[r][0].astype(F32)

    def join_out(dev, *refs):
        mine = part_of(dev)
        for m in range(PARTS):

            @pl.when(mine == m)
            def _():
                for r in range(PARTS):
                    refs[PARTS][(m ^ r) * CH : ((m ^ r) + 1) * CH, :] = refs[r][0].astype(F32)

    def joined_in(pieces, name):
        return run(
            join_in,
            name,
            device,
            [chunked(p) for p in pieces],
            [
                (
                    jax.ShapeDtypeStruct((D, C), F32),
                    pl.BlockSpec((DCH, C), lambda i, dev: (span_of(dev) ^ reversed_bits(i), 0)),
                )
            ],
            spans,
        )[0]

    def joined_out(pieces, name):
        return run(
            join_out,
            name,
            device,
            [chunked(p) for p in pieces],
            [
                (
                    jax.ShapeDtypeStruct((C, D), F32),
                    pl.BlockSpec((C, DCH), lambda i, dev: (0, span_of(dev) ^ reversed_bits(i))),
                )
            ],
            spans,
        )[0]

    grad_flops = 2 * PARTS * R * D * CH
    send, keep = run(
        out_weight_grad,
        "out_weight_grad",
        device,
        [whole(m) for m in mixed_q] + [by_span(c) for group in cots_all for c in group],
        split_specs((CH, DCH)),
        spans,
        flops=grad_flops,
    )
    grad_out = joined_out(sum_spans(send, keep), "join_out")
    send, keep = run(
        in_weight_grad,
        "z_weight_grad",
        device,
        [by_span(n) for n in normed_all] + [whole(c) for c in cotz_q],
        split_specs((DCH, CH)),
        spans,
        flops=grad_flops,
    )
    grad_z = joined_in(sum_spans(send, keep), "join_z")
    send, keep = run(
        in_weight_grad,
        "x_weight_grad",
        device,
        [by_span(n) for n in normed_all] + [whole(c) for c in cotx_q],
        split_specs((DCH, CH)),
        spans,
        flops=grad_flops,
    )
    grad_x = joined_in(sum_spans(send, keep), "join_x")

    bit = 1
    while bit < replicas:
        rounded = pack.astype(BF16)
        pack = rounded.astype(F32) + exchange(rounded, "rep", bit).astype(F32)
        bit *= 2
    at = NB + H
    grad_bc = pack[0:NB].T
    grad_dt = pack[NB:at].T
    grad_conv_x = pack[at : at + 4, 0:C]
    grad_bias_x = pack[at + 4 : at + 5, 0:C]
    grad_gate = pack[at + 5 : at + 6, 0:C]
    heads = pack[at + 6 : at + 9, 0 : PARTS * 128].reshape(3, PARTS, 128)[:, :, 0:HC].reshape(3, H)
    grad_conv_bc = pack[at + 9 : at + 13, 0:NB]
    grad_bias_bc = pack[at + 13 : at + 14, 0:NB]
    gain_row = pack[at + 14].reshape(S, D // S)
    grad_gain = lax.dynamic_index_in_dim(gain_row, shard_at, 0, keepdims=True)
    for j in range(1, S):
        theirs = lax.dynamic_index_in_dim(gain_row, shard_at ^ j, 0, keepdims=True)
        grad_gain = grad_gain + exchange(theirs, "shard", j)
    return (
        hidden_out,
        grad_hidden,
        grad_gain,
        grad_z[None],
        grad_x[None],
        grad_bc[None],
        grad_dt[None],
        grad_conv_x[None],
        grad_conv_bc[None],
        grad_bias_x,
        grad_bias_bc,
        heads[0:1],
        heads[1:2],
        heads[2:3],
        grad_gate,
        grad_out[None],
    )
```

time: 443 us -> 233 us (0.53)
  blocking collectives: 117 us -> 0 us
  Pallas kernels: 0 us -> 82.2 us
  other arithmetic: 83 us -> 7.98 us
  matrix products: 74.7 us -> 0 us
  starting transfers between devices: 0.2 us -> 47.9 us
  local copies, waits for them, and re-layouts: 57.6 us -> 16.6 us
  between operations: 16.5 us -> 1.2 us
  waiting for transfers between devices: 87.5 us -> 75.5 us
    psum x1 -> x0, waiting for transfers between devices: 87.4 us -> none  [sum_replicas(): lax.psum(parts[1].astype(jnp.bfloat16), 'rep').astype(jnp.float32)]
    pallas_call x0 -> x14, Pallas kernels: none -> 82.2 us  [run(): pl.pallas_call(body, name=name, out_shape=[shape for shape, _ in outs], g...]
    ppermute x0 -> x52, waiting for transfers between devices: none -> 75.5 us  [exchange(): return lax.ppermute(array, axis, [(i, i ^ bit) for i in range(count)])]
    dot_general x27 -> x0, matrix products: 74.7 us -> none  [the longest x3 18.2 us: mixer_core(): jnp.einsum('bhts,bshp->bthp', mixing, head_values, precision=HIGHEST)]
    psum x3 -> x0, blocking collectives: 71.1 us -> none  [the longest x1 60.9 us: sum_replicas(): lax.psum(parts[0].astype(jnp.bfloat16), 'rep').astype(jnp.float32)]
    ppermute x0 -> x52, starting transfers between devices: none -> 47.9 us  [exchange(): return lax.ppermute(array, axis, [(i, i ^ bit) for i in range(count)])]
    all_gather x6 -> x0, blocking collectives: 36 us -> none  [the longest x1 7.87 us: on_device(): normed = lax.all_gather(normed_own, 'shard', axis=0, tiled=True)]
    reduce_sum x15 -> x0, other arithmetic: 20.3 us -> none  [the longest x2 5.82 us: causal_conv(): kernel[kernel_len - 1 - offset][None, :] * shifted * same_seq[:, None]]
  transfers between devices with their start and end apart: 5 -> 52, of which waited for: 1 -> 16; matrix products, arithmetic and copies ran while one was open for 13% -> 9% of each run, Pallas kernels for 0% -> 32%
where the time goes in v1:
time: 233 us; the launch traced here: 231 us
  Pallas kernels  82.2 us (35%)
  waiting for transfers between devices  75.5 us (32%)
  starting transfers between devices  47.9 us (21%)
  local copies, waits for them, and re-layouts  16.6 us (7%)
  other arithmetic  7.98 us (3%)
    pallas_call x14, Pallas kernels, run(): pl.pallas_call(body, name=name, out_shape=[shape for shape, _ in outs], g...  82.2 us
    ppermute x52, waiting for transfers between devices, exchange(): return lax.ppermute(array, axis, [(i, i ^ bit) for i in range(count)])  75.5 us
    ppermute x52, starting transfers between devices, exchange(): return lax.ppermute(array, axis, [(i, i ^ bit) for i in range(count)])  47.9 us
    unnamed x70, local copies, waits for them, and re-layouts  6.33 us
  transfers between devices with their start and end apart: 52, of which 16 were waited for; matrix products, arithmetic and copies ran while one was open for 9% of the time, Pallas kernels for 32%

profile of v1, /device:TPU:0, one launch (start us, length us, event | category | flops | bytes accessed | tf_op | source)
XLA Modules:
  0.0 231.4 jit_solution(3608132457489115053)
XLA Ops:
  1.2 2.6 %collective-permute-start.3 = (bf16[128,1024]{1,0:T(8,128)(2,1)}, bf16[128,1024]{1,0:T(8,128)(2,1)S(1)}, u32[]{:S(2)}, u32[]{:S(2)}) collective-permute-start(bf16[128,1024]{1,0:T(8,128)(2,1)} %refs_4_.1), channel_id=1, source_target_pairs={{0,1},{1,0},{2,3},{3,2},{4,5},{5,4},{6,7},{7,6},{8,9},{9,8},{10,11... | collective-permute-start | bytes 786440 | tf_op jit(solution)/shard_map/ppermute | solution.py:20
  3.8 1.5 collective-permute-start.41
  5.8 1.5 collective-permute-start.1
  13.4 1.4 concatenate.36.tx
  17.4 2.7 %norm_and_maps.1 = (bf16[256,1024]{1,0:T(8,128)(2,1)}, f32[256,128]{1,0:T(8,128)}, f32[256,128]{1,0:T(8,128)}, f32[256,128]{1,0:T(8,128)}, f32[256,128]{1,0:T(8,...) custom-call(s32[1]{0:T(128)} %bitcast.dev, s32[1,256]{1,0:T(1,128)} %bitcast.49, s32[1,256]{1,0:T(1,128)} %bitcast.50, ...), custom_call_target="tpu_custom_call" | custom-call | flops 67108864 | bytes 1977344 | tf_op jit(solution)/shard_map/norm_and_maps/pallas_call | solution.py:70
  20.1 1.6 collective-permute-start.2
  21.7 7.8 %projections.1 = (f32[4,256,256]{2,1,0:T(8,128)}, f32[4,256,256]{2,1,0:T(8,128)}, f32[4,256,256]{2,1,0:T(8,128)}, f32[4,256,128]{2,1,0:T(8,128)}, f32[4,256,128]...) custom-call(s32[1]{0:T(128)} %bitcast.dev, bf16[256,1024]{1,0:T(8,128)(2,1)} %get-tuple-element.74.n_r.refs_0_, ...), custom_call_target="tpu_custom_call" | custom-call | flops 1610612736 | bytes 13844480 | tf_op jit(solution)/shard_map/projections/pallas_call | solution.py:70
  30.2 7.6 %scan_forward.1 = (f32[4,256,256]{2,1,0:T(8,128)}, f32[8,256]{1,0:T(8,128)}, f32[128,1024]{1,0:T(8,128)}, f32[8,256]{1,0:T(8,128)}, bf16[128,1024]{1,0:T(8,128)(2,1)}) custom-call(s32[1]{0:T(128)} %bitcast.dev, bf16[256,128]{1,0:T(8,128)(2,1)} %get-tuple-element.71.a_r, bf16[256,128]{1,0:T(8,128)(2,1)} %copy-done.14, f32[256,128]{1,0:T(8,128)} %get-tuple-element.73.mask_r, ...), custom_call_target="tpu_custom_call" | custom-call | flops 671088640 | bytes 8470528 | tf_op jit(solution)/shard_map/scan_forward/pallas_call | solution.py:70
  38.3 3.5 %collective-permute-done.4.refs_1_ = f32[8,256]{1,0:T(8,128)S(1)} collective-permute-done((f32[8,256]{1,0:T(8,128)}, f32[8,256]{1,0:T(8,128)S(1)}, u32[]{:S(2)}, u32[]{:S(2)}) %collective-permute-start.4) | collective-permute-done | bytes 8224 | tf_op jit(solution)/shard_map/ppermute | solution.py:20
  42.3 5.2 %gate_backward.1 = (bf16[256,256]{1,0:T(8,128)(2,1)}, bf16[256,256]{1,0:T(8,128)(2,1)}, bf16[256,256]{1,0:T(8,128)(2,1)}, bf16[256,256]{1,0:T(8,128)(2,1)}, bf16...) custom-call(s32[1]{0:T(128)} %bitcast.dev, ...), custom_call_target="tpu_custom_call" | custom-call | flops 10485760 | bytes 5586944 | tf_op jit(solution)/shard_map/gate_backward/pallas_call | solution.py:70
  48.6 1.5 collective-permute-start.37
  50.4 4.8 %collective-permute-done.37.refs_2_ = bf16[256,256]{1,0:T(8,128)(2,1)S(1)} collective-permute-done((bf16[256,256]{1,0:T(8,128)(2,1)}, bf16[256,256]{1,0:T(8,128)(2,1)S(1)}, u32[]{:S(2)}, u32[]{:S(2)}) %collective-permute-start.37) | collective-permute-done | bytes 131104 | tf_op jit(solution)/shard_map/ppermute | solution.py:20
  57.2 5.0 %out_weight_grad.1 = (bf16[2,256,256]{2,1,0:T(8,128)(2,1)}, f32[2,256,256]{2,1,0:T(8,128)}) custom-call(s32[1]{0:T(128)} %bitcast.dev, bf16[256,256]{1,0:T(8,128)(2,1)} %get-tuple-element.118.refs_0_, bf16[256,256]{1,0:T(8,128)(2,1)} %copy-done.25, bf16[256,256]{1,0:T(8,128)(2,1)} %copy-done.26, bf16[256,256]{1,0:T(8,128)(2,1)} %copy-done.27, ...), custom_call_target="tpu_custom_call" | custom-call | flops 536870912 | bytes 3407872 | tf_op jit(solution)/shard_map/out_weight_grad/pallas_call | solution.py:70
  62.1 1.7 collective-permute-start.45
  64.7 19.5 %scan_backward.1 = (bf16[256,256]{1,0:T(8,128)(2,1)}, bf16[256,256]{1,0:T(8,128)(2,1)}, bf16[256,256]{1,0:T(8,128)(2,1)}, bf16[256,256]{1,0:T(8,128)(2,1)}, bf16...) custom-call(s32[1]{0:T(128)} %bitcast.dev, ...), custom_call_target="tpu_custom_call" | custom-call | flops 268435456 | bytes 7012352 | tf_op jit(solution)/shard_map/scan_backward/pallas_call | solution.py:70
  84.8 5.9 %input_backward.1 = (f32[256,1024]{1,0:T(8,128)}, bf16[256,128]{1,0:T(8,128)(2,1)}) custom-call(s32[1]{0:T(128)} %bitcast.dev, bf16[4,256,256]{2,1,0:T(8,128)(2,1)} %get-tuple-element.90.cz, bf16[4,256,256]{2,1,0:T(8,128)(2,1)} %get-tuple-element.91.cx, f32[4,256,128]{2,1,0:T(8,128)} %get-tuple-element.92.cdt, bf16[1024,1024]{1,0:T(8,128)(2,1)} %bitcast.34, ...), custom_call_target="tpu_custom_call" | custom-call | flops 1073741824 | bytes 6914048 | tf_op jit(solution)/shard_map/input_backward/pallas_call | solution.py:70
  91.3 3.5 %maps_backward.1 = (f32[128,1024]{1,0:T(8,128)}, f32[160,1024]{1,0:T(8,128)}, bf16[128,1024]{1,0:T(8,128)(2,1)}) custom-call(s32[1]{0:T(128)} %bitcast.dev, f32[256,128]{1,0:T(8,128)} %get-tuple-element.87.own, f32[256,128]{1,0:T(8,128)} %get-tuple-element.88.pre_r, f32[256,128]{1,0:T(8,128)} %get-tuple-element.89.pbc_r, ...), custom_call_target="tpu_custom_call" | custom-call | flops 201326592 | bytes 4542464 | tf_op jit(solution)/shard_map/maps_backward/pallas_call | solution.py:70
  96.2 1.5 collective-permute-start.14
  98.4 2.7 %collective-permute-start.46 = (bf16[1,256,256]{2,1,0:T(8,128)(2,1)S(1)}, bf16[1,256,256]{2,1,0:T(8,128)(2,1)S(1)}, u32[]{:S(2)}, u32[]{:S(2)}) collective-permute-start(bf16[1,256,256]{2,1,0:T(8,128)(2,1)S(1)} %slice.132), channel_id=1, source_target_pairs={{0,16},{2,18},{4,20},{6,22},{8,24},{10,26},{12,28},{14,30},{16,0},... | collective-permute-start | bytes 393224 | tf_op jit(solution)/shard_map/ppermute | solution.py:20
  102.2 1.6 collective-permute-start.9
  103.8 1.6 collective-permute-start.7
  105.3 8.4 %collective-permute-done.17.refs_6_ = bf16[256,256]{1,0:T(8,128)(2,1)S(1)} collective-permute-done((bf16[256,256]{1,0:T(8,128)(2,1)S(1)}, bf16[256,256]{1,0:T(8,128)(2,1)S(1)}, u32[]{:S(2)}, u32[]{:S(2)}) %collective-permute-start.17) | collective-permute-done | bytes 131104 | tf_op jit(solution)/shard_map/ppermute | solution.py:20
  113.7 1.6 collective-permute-start.6
  115.5 1.5 collective-permute-start.18
  117.0 3.7 %collective-permute-done.9 = bf16[160,1024]{1,0:T(8,128)(2,1)S(1)} collective-permute-done((bf16[160,1024]{1,0:T(8,128)(2,1)S(1)}, bf16[160,1024]{1,0:T(8,128)(2,1)S(1)}, u32[]{:S(2)}, u32[]{:S(2)}) %collective-permute-start.9) | collective-permute-done | bytes 327712 | tf_op jit(solution)/shard_map/ppermute | solution.py:20
  120.7 2.6 %collective-permute-start.47 = (bf16[1,256,256]{2,1,0:T(8,128)(2,1)S(1)}, bf16[1,256,256]{2,1,0:T(8,128)(2,1)S(1)}, u32[]{:S(2)}, u32[]{:S(2)}) collective-permute-start(bf16[1,256,256]{2,1,0:T(8,128)(2,1)S(1)} %fusion), channel_id=1, source_target_pairs={{0,16},{2,18},{4,20},{6,22},{8,24},{10,26},{12,28},{14,30},{16,0},... | collective-permute-start | bytes 393224 | tf_op jit(solution)/shard_map/ppermute | solution.py:20
  124.2 2.9 %own_rows.1 = (f32[128,1024]{1,0:T(8,128)}, f32[128,1024]{1,0:T(8,128)}) custom-call(s32[1]{0:T(128)} %bitcast.dev, bf16[128,1024]{1,0:T(8,128)(2,1)} %hid.1, bf16[128,1024]{1,0:T(8,128)(2,1)} %refs_4_.1, f32[256,128]{1,0:T(8,128)} %get-tuple-element.70.cols_r, f32[256,128]{1,0:T(8,128)} %get-tuple-element.84.rows_r, f32[1,1024]{1,0:T(1,128)} %pad_maximum_fusion.6.gain_r, ...), custom_call_target="tpu_custom_call" | custom-call | bytes 3411968 | tf_op jit(solution)/shard_map/own_rows/pallas_call | solution.py:70
  127.1 1.6 collective-permute-start.27
  130.5 4.6 %z_weight_grad.1 = (bf16[2,256,256]{2,1,0:T(8,128)(2,1)}, f32[2,256,256]{2,1,0:T(8,128)}) custom-call(s32[1]{0:T(128)} %bitcast.dev, bf16[256,1024]{1,0:T(8,128)(2,1)} %get-tuple-element.74.n_r.refs_0_, bf16[256,1024]{1,0:T(8,128)(2,1)} %copy-done.5, bf16[256,1024]{1,0:T(8,128)(2,1)} %copy-done.4, bf16[256,1024]{1,0:T(8,128)(2,1)} %copy-done.6, ...), custom_call_target="tpu_custom_call" | custom-call | flops 536870912 | bytes 3407872 | tf_op jit(solution)/shard_map/z_weight_grad/pallas_call | solution.py:70
  136.0 4.6 %x_weight_grad.1 = (bf16[2,256,256]{2,1,0:T(8,128)(2,1)}, f32[2,256,256]{2,1,0:T(8,128)}) custom-call(s32[1]{0:T(128)} %bitcast.dev, bf16[256,1024]{1,0:T(8,128)(2,1)} %get-tuple-element.74.n_r.refs_0_, bf16[256,1024]{1,0:T(8,128)(2,1)} %copy-done.5, bf16[256,1024]{1,0:T(8,128)(2,1)} %copy-done.4, bf16[256,1024]{1,0:T(8,128)(2,1)} %copy-done.6, ...), custom_call_target="tpu_custom_call" | custom-call | flops 536870912 | bytes 3407872 | tf_op jit(solution)/shard_map/x_weight_grad/pallas_call | solution.py:70
  142.0 1.8 collective-permute-start.11
  143.8 1.6 collective-permute-start.50
  145.4 7.3 %collective-permute-done.19 = bf16[2,256,256]{2,1,0:T(8,128)(2,1)S(1)} collective-permute-done((bf16[2,256,256]{2,1,0:T(8,128)(2,1)}, bf16[2,256,256]{2,1,0:T(8,128)(2,1)S(1)}, u32[]{:S(2)}, u32[]{:S(2)}) %collective-permute-start.19) | collective-permute-done | bytes 262176 | tf_op jit(solution)/shard_map/ppermute | solution.py:20
  152.8 4.2 %collective-permute-done.29 = bf16[2,256,256]{2,1,0:T(8,128)(2,1)S(1)} collective-permute-done((bf16[2,256,256]{2,1,0:T(8,128)(2,1)}, bf16[2,256,256]{2,1,0:T(8,128)(2,1)S(1)}, u32[]{:S(2)}, u32[]{:S(2)}) %collective-permute-start.29) | collective-permute-done | bytes 262176 | tf_op jit(solution)/shard_map/ppermute | solution.py:20
  158.2 10.8 %collective-permute-done.20 = bf16[1,256,256]{2,1,0:T(8,128)(2,1)S(1)} collective-permute-done((bf16[1,256,256]{2,1,0:T(8,128)(2,1)S(1)}, bf16[1,256,256]{2,1,0:T(8,128)(2,1)S(1)}, u32[]{:S(2)}, u32[]{:S(2)}) %collective-permute-start.20) | collective-permute-done | bytes 131104 | tf_op jit(solution)/shard_map/ppermute | solution.py:20
  169.1 1.8 collective-permute-done.30
  172.8 7.9 %collective-permute-done.31 = bf16[1,256,256]{2,1,0:T(8,128)(2,1)S(1)} collective-permute-done((bf16[1,256,256]{2,1,0:T(8,128)(2,1)S(1)}, bf16[1,256,256]{2,1,0:T(8,128)(2,1)S(1)}, u32[]{:S(2)}, u32[]{:S(2)}) %collective-permute-start.31) | collective-permute-done | bytes 131104 | tf_op jit(solution)/shard_map/ppermute | solution.py:20
  180.8 2.1 collective-permute-start.32
  183.6 6.5 %collective-permute-done.32 = bf16[2,256,256]{2,1,0:T(8,128)(2,1)S(1)} collective-permute-done((bf16[2,256,256]{2,1,0:T(8,128)(2,1)S(1)}, bf16[2,256,256]{2,1,0:T(8,128)(2,1)S(1)}, u32[]{:S(2)}, u32[]{:S(2)}) %collective-permute-start.32) | collective-permute-done | bytes 262176 | tf_op jit(solution)/shard_map/ppermute | solution.py:20
  190.2 2.9 %collective-permute-start.34 = (bf16[4,256,256]{2,1,0:T(8,128)(2,1)S(1)}, bf16[4,256,256]{2,1,0:T(8,128)(2,1)}, u32[]{:S(2)}, u32[]{:S(2)}) collective-permute-start(bf16[4,256,256]{2,1,0:T(8,128)(2,1)S(1)} %pad_maximum_fusion.1.refs_0_), channel_id=1, source_target_pairs={{0,4},{2,6},{4,0},{6,2},{8,12},{10,14},{12,8},{14,10},{16,20},{18,... | collective-permute-start | bytes 1572872 | tf_op jit(solution)/shard_map/ppermute | solution.py:20
  194.3 1.8 collective-permute-start.24
  196.1 1.6 collective-permute-start.12
  197.8 2.0 collective-permute-done.12
  200.4 5.7 %collective-permute-done.34.refs_2_ = bf16[4,256,256]{2,1,0:T(8,128)(2,1)} collective-permute-done((bf16[4,256,256]{2,1,0:T(8,128)(2,1)S(1)}, bf16[4,256,256]{2,1,0:T(8,128)(2,1)}, u32[]{:S(2)}, u32[]{:S(2)}) %collective-permute-start.34) | collective-permute-done | bytes 524320 | tf_op jit(solution)/shard_map/ppermute | solution.py:20
  206.0 6.5 %collective-permute-done.24.refs_2_ = bf16[4,256,256]{2,1,0:T(8,128)(2,1)} collective-permute-done((bf16[4,256,256]{2,1,0:T(8,128)(2,1)S(1)}, bf16[4,256,256]{2,1,0:T(8,128)(2,1)}, u32[]{:S(2)}, u32[]{:S(2)}) %collective-permute-start.24) | collective-permute-done | bytes 524320 | tf_op jit(solution)/shard_map/ppermute | solution.py:20
  217.7 4.3 %join_out.1 = f32[1024,1024]{1,0:T(8,128)} custom-call(s32[1]{0:T(128)} %bitcast.dev, bf16[4,256,256]{2,1,0:T(8,128)(2,1)} %copy-done.1, bf16[4,256,256]{2,1,0:T(8,128)(2,1)} %collective-permute-done.49.refs_1_, bf16[4,256,256]{2,1,0:T(8,128)(2,1)} %copy-done.10, bf16[4,256,256]{2,1,0:T(8,128)(2,1)} %collective-permute-done.51.refs_3_), custom_call_target="tpu_custom_call" | custom-call | bytes 6291456 | tf_op jit(solution)/shard_map/join_out/pallas_call | solution.py:70
  222.0 4.3 %join_z.1 = f32[1024,1024]{1,0:T(8,128)} custom-call(s32[1]{0:T(128)} %bitcast.dev, bf16[4,256,256]{2,1,0:T(8,128)(2,1)} %copy-done.3, bf16[4,256,256]{2,1,0:T(8,128)(2,1)} %collective-permute-done.23.refs_1_, bf16[4,256,256]{2,1,0:T(8,128)(2,1)} %collective-permute-done.24.refs_2_, bf16[4,256,256]{2,1,0:T(8,128)(2,1)} %collective-permute-done.25.refs_3_), custom_call_target="tpu_custom_call" | custom-call | bytes 6291456 | tf_op jit(solution)/shard_map/join_z/pallas_call | solution.py:70
  227.1 4.3 %join_x.1 = f32[1024,1024]{1,0:T(8,128)} custom-call(s32[1]{0:T(128)} %bitcast.dev, bf16[4,256,256]{2,1,0:T(8,128)(2,1)} %copy-done.2, bf16[4,256,256]{2,1,0:T(8,128)(2,1)} %collective-permute-done.33.refs_1_, bf16[4,256,256]{2,1,0:T(8,128)(2,1)} %collective-permute-done.34.refs_2_, bf16[4,256,256]{2,1,0:T(8,128)(2,1)} %copy-done.11), custom_call_target="tpu_custom_call" | custom-call | bytes 6291456 | tf_op jit(solution)/shard_map/join_x/pallas_call | solution.py:70
  (191 shorter events, 37.0 us)
Async XLA Ops:
  0.6 48.0 %collective-permute-start.39 = (bf16[128,1024]{1,0:T(8,128)(2,1)}, bf16[128,1024]{1,0:T(8,128)(2,1)S(1)}, u32[]{:S(2)}, u32[]{:S(2)}) collective-permute-start(bf16[128,1024]{1,0:T(8,128)(2,1)} %refs_4_.1), channel_id=1, source_target_pairs={{0,2},{2,0},{4,6},{6,4},{8,10},{10,8},{12,14},{14,12},{16,18},{18,... | collective-permute-start | bytes 786440 | tf_op jit(solution)/shard_map/ppermute | solution.py:20
  1.2 14.3 %collective-permute-start.3 = (bf16[128,1024]{1,0:T(8,128)(2,1)}, bf16[128,1024]{1,0:T(8,128)(2,1)S(1)}, u32[]{:S(2)}, u32[]{:S(2)}) collective-permute-start(bf16[128,1024]{1,0:T(8,128)(2,1)} %refs_4_.1), channel_id=1, source_target_pairs={{0,1},{1,0},{2,3},{3,2},{4,5},{5,4},{6,7},{7,6},{8,9},{9,8},{10,11... | collective-permute-start | bytes 786440 | tf_op jit(solution)/shard_map/ppermute | solution.py:20
  3.8 44.3 %collective-permute-start.41 = (bf16[128,1024]{1,0:T(8,128)(2,1)}, bf16[128,1024]{1,0:T(8,128)(2,1)S(1)}, u32[]{:S(2)}, u32[]{:S(2)}) collective-permute-start(bf16[128,1024]{1,0:T(8,128)(2,1)} %refs_4_.1), channel_id=1, source_target_pairs={{0,4},{2,6},{4,0},{6,2},{8,12},{10,14},{12,8},{14,10},{16,20},{18,... | collective-permute-start | bytes 786440 | tf_op jit(solution)/shard_map/ppermute | solution.py:20
  5.3 9.5 %collective-permute-start = (f32[1,512]{1,0:T(1,128)}, f32[1,512]{1,0:T(1,128)S(1)}, u32[]{:S(2)}, u32[]{:S(2)}) collective-permute-start(f32[1,512]{1,0:T(1,128)} %param.21), channel_id=1, source_target_pairs={{0,1},{1,0},{2,3},{3,2},{4,5},{5,4},{6,7},{7,6},{8,9},{9,8},{10,11... | collective-permute-start | bytes 6152 | tf_op jit(solution)/shard_map/ppermute | solution.py:20
  5.8 10.9 %collective-permute-start.1 = (bf16[128,1024]{1,0:T(8,128)(2,1)}, bf16[128,1024]{1,0:T(8,128)(2,1)S(1)}, u32[]{:S(2)}, u32[]{:S(2)}) collective-permute-start(bf16[128,1024]{1,0:T(8,128)(2,1)} %hid.1), channel_id=1, source_target_pairs={{0,1},{1,0},{2,3},{3,2},{4,5},{5,4},{6,7},{7,6},{8,9},{9,8},{10,11... | collective-permute-start | bytes 786440 | tf_op jit(solution)/shard_map/ppermute | solution.py:20
  15.4 32.7 %collective-permute-start.42 = (bf16[128,1024]{1,0:T(8,128)(2,1)S(1)}, bf16[128,1024]{1,0:T(8,128)(2,1)S(1)}, u32[]{:S(2)}, u32[]{:S(2)}) collective-permute-start(bf16[128,1024]{1,0:T(8,128)(2,1)S(1)} %collective-permute-done.3.refs_1_.refs_5_), channel_id=1, source_target_pairs={{0,4},{2,6},{4,0},{6,2},{8,12},{10,14},{12,8},{14,10},{16,20},{18,... | collective-permute-start | bytes 786440 | tf_op jit(solution)/shard_map/ppermute | solution.py:20
  20.1 9.5 %collective-permute-start.2 = (bf16[256,128]{1,0:T(8,128)(2,1)}, bf16[256,128]{1,0:T(8,128)(2,1)S(1)}, u32[]{:S(2)}, u32[]{:S(2)}) collective-permute-start(bf16[256,128]{1,0:T(8,128)(2,1)} %get-tuple-element.72), channel_id=1, source_target_pairs={{0,1},{1,0},{2,3},{3,2},{4,5},{5,4},{6,7},{7,6},{8,9},{9,8},{10,11... | collective-permute-start | bytes 196616 | tf_op jit(solution)/shard_map/ppermute | solution.py:20
  47.6 8.7 %collective-permute-start.40 = (bf16[128,1024]{1,0:T(8,128)(2,1)S(1)}, bf16[128,1024]{1,0:T(8,128)(2,1)S(1)}, u32[]{:S(2)}, u32[]{:S(2)}) collective-permute-start(bf16[128,1024]{1,0:T(8,128)(2,1)S(1)} %copy-done.9), channel_id=1, source_target_pairs={{0,2},{2,0},{4,6},{6,4},{8,10},{10,8},{12,14},{14,12},{16,18},{18,... | collective-permute-start | bytes 786440 | tf_op jit(solution)/shard_map/ppermute | solution.py:20
  48.1 8.2 %collective-permute-start.43 = (bf16[128,1024]{1,0:T(8,128)(2,1)S(1)}, bf16[128,1024]{1,0:T(8,128)(2,1)S(1)}, u32[]{:S(2)}, u32[]{:S(2)}) collective-permute-start(bf16[128,1024]{1,0:T(8,128)(2,1)S(1)} %collective-permute-done.41.refs_8_), channel_id=1, source_target_pairs={{0,2},{2,0},{4,6},{6,4},{8,10},{10,8},{12,14},{14,12},{16,18},{18,... | collective-permute-start | bytes 786440 | tf_op jit(solution)/shard_map/ppermute | solution.py:20
  48.2 8.1 %collective-permute-start.44 = (bf16[128,1024]{1,0:T(8,128)(2,1)S(1)}, bf16[128,1024]{1,0:T(8,128)(2,1)S(1)}, u32[]{:S(2)}, u32[]{:S(2)}) collective-permute-start(bf16[128,1024]{1,0:T(8,128)(2,1)S(1)} %collective-permute-done.42.refs_9_), channel_id=1, source_target_pairs={{0,2},{2,0},{4,6},{6,4},{8,10},{10,8},{12,14},{14,12},{16,18},{18,... | collective-permute-start | bytes 786440 | tf_op jit(solution)/shard_map/ppermute | solution.py:20
  48.6 6.6 %collective-permute-start.37 = (bf16[256,256]{1,0:T(8,128)(2,1)}, bf16[256,256]{1,0:T(8,128)(2,1)S(1)}, u32[]{:S(2)}, u32[]{:S(2)}) collective-permute-start(bf16[256,256]{1,0:T(8,128)(2,1)} %get-tuple-element.120), channel_id=1, source_target_pairs={{0,4},{2,6},{4,0},{6,2},{8,12},{10,14},{12,8},{14,10},{16,20},{18,... | collective-permute-start | bytes 393224 | tf_op jit(solution)/shard_map/ppermute | solution.py:20
  50.1 6.1 %collective-permute-start.38 = (bf16[256,256]{1,0:T(8,128)(2,1)}, bf16[256,256]{1,0:T(8,128)(2,1)S(1)}, u32[]{:S(2)}, u32[]{:S(2)}) collective-permute-start(bf16[256,256]{1,0:T(8,128)(2,1)} %get-tuple-element.121), channel_id=1, source_target_pairs={{0,6},{2,4},{4,2},{6,0},{8,14},{10,12},{12,10},{14,8},{16,22},{18,... | collective-permute-start | bytes 393224 | tf_op jit(solution)/shard_map/ppermute | solution.py:20
  62.1 36.1 %collective-permute-start.45 = (bf16[2,256,256]{2,1,0:T(8,128)(2,1)}, bf16[2,256,256]{2,1,0:T(8,128)(2,1)S(1)}, u32[]{:S(2)}, u32[]{:S(2)}) collective-permute-start(bf16[2,256,256]{2,1,0:T(8,128)(2,1)} %get-tuple-element.123), channel_id=1, source_target_pairs={{0,8},{2,10},{4,12},{6,14},{8,0},{10,2},{12,4},{14,6},{16,24},{18,... | collective-permute-start | bytes 786440 | tf_op jit(solution)/shard_map/ppermute | solution.py:20
  84.2 6.5 %collective-permute-start.5 = (bf16[256,128]{1,0:T(8,128)(2,1)}, bf16[256,128]{1,0:T(8,128)(2,1)S(1)}, u32[]{:S(2)}, u32[]{:S(2)}) collective-permute-start(bf16[256,128]{1,0:T(8,128)(2,1)} %get-tuple-element.98), channel_id=1, source_target_pairs={{0,1},{1,0},{2,3},{3,2},{4,5},{5,4},{6,7},{7,6},{8,9},{9,8},{10,11... | collective-permute-start | bytes 196616 | tf_op jit(solution)/shard_map/ppermute | solution.py:20
  96.2 17.6 %collective-permute-start.14 = (bf16[256,1024]{1,0:T(8,128)(2,1)S(1)}, bf16[256,1024]{1,0:T(8,128)(2,1)S(1)}, u32[]{:S(2)}, u32[]{:S(2)}) collective-permute-start(bf16[256,1024]{1,0:T(8,128)(2,1)S(1)} %copy-done), channel_id=1, source_target_pairs={{0,4},{2,6},{4,0},{6,2},{8,12},{10,14},{12,8},{14,10},{16,20},{18,... | collective-permute-start | bytes 1572872 | tf_op jit(solution)/shard_map/ppermute | solution.py:20
  97.6 6.1 %collective-permute-start.16 = (bf16[256,256]{1,0:T(8,128)(2,1)S(1)}, bf16[256,256]{1,0:T(8,128)(2,1)S(1)}, u32[]{:S(2)}, u32[]{:S(2)}) collective-permute-start(bf16[256,256]{1,0:T(8,128)(2,1)S(1)} %copy-done.33), channel_id=1, source_target_pairs={{0,2},{2,0},{4,6},{6,4},{8,10},{10,8},{12,14},{14,12},{16,18},{18,... | collective-permute-start | bytes 393224 | tf_op jit(solution)/shard_map/ppermute | solution.py:20
  97.7 16.0 %collective-permute-start.17 = (bf16[256,256]{1,0:T(8,128)(2,1)S(1)}, bf16[256,256]{1,0:T(8,128)(2,1)S(1)}, u32[]{:S(2)}, u32[]{:S(2)}) collective-permute-start(bf16[256,256]{1,0:T(8,128)(2,1)S(1)} %copy-done.32), channel_id=1, source_target_pairs={{0,4},{2,6},{4,0},{6,2},{8,12},{10,14},{12,8},{14,10},{16,20},{18,... | collective-permute-start | bytes 393224 | tf_op jit(solution)/shard_map/ppermute | solution.py:20
  98.4 17.0 %collective-permute-start.46 = (bf16[1,256,256]{2,1,0:T(8,128)(2,1)S(1)}, bf16[1,256,256]{2,1,0:T(8,128)(2,1)S(1)}, u32[]{:S(2)}, u32[]{:S(2)}) collective-permute-start(bf16[1,256,256]{2,1,0:T(8,128)(2,1)S(1)} %slice.132), channel_id=1, source_target_pairs={{0,16},{2,18},{4,20},{6,22},{8,24},{10,26},{12,28},{14,30},{16,0},... | collective-permute-start | bytes 393224 | tf_op jit(solution)/shard_map/ppermute | solution.py:20
  102.2 18.5 %collective-permute-start.9 = (bf16[160,1024]{1,0:T(8,128)(2,1)S(1)}, bf16[160,1024]{1,0:T(8,128)(2,1)S(1)}, u32[]{:S(2)}, u32[]{:S(2)}) collective-permute-start(bf16[160,1024]{1,0:T(8,128)(2,1)S(1)} %add_convert_fusion.2), channel_id=1, source_target_pairs={{0,4},{2,6},{4,0},{6,2},{8,12},{10,14},{12,8},{14,10},{16,20},{18,... | collective-permute-start | bytes 983048 | tf_op jit(solution)/shard_map/ppermute | solution.py:20
  103.8 11.7 %collective-permute-start.7 = (bf16[128,1024]{1,0:T(8,128)(2,1)S(1)}, bf16[128,1024]{1,0:T(8,128)(2,1)S(1)}, u32[]{:S(2)}, u32[]{:S(2)}) collective-permute-start(bf16[128,1024]{1,0:T(8,128)(2,1)S(1)} %copy-done.31), channel_id=1, source_target_pairs={{0,1},{1,0},{2,3},{3,2},{4,5},{5,4},{6,7},{7,6},{8,9},{9,8},{10,11... | collective-permute-start | bytes 786440 | tf_op jit(solution)/shard_map/ppermute | solution.py:20
  113.7 13.4 %collective-permute-start.13 = (bf16[256,1024]{1,0:T(8,128)(2,1)S(1)}, bf16[256,1024]{1,0:T(8,128)(2,1)S(1)}, u32[]{:S(2)}, u32[]{:S(2)}) collective-permute-start(bf16[256,1024]{1,0:T(8,128)(2,1)S(1)} %copy-done), channel_id=1, source_target_pairs={{0,2},{2,0},{4,6},{6,4},{8,10},{10,8},{12,14},{14,12},{16,18},{18,... | collective-permute-start | bytes 1572872 | tf_op jit(solution)/shard_map/ppermute | solution.py:20
  113.7 9.7 %collective-permute-start.6 = (bf16[128,1024]{1,0:T(8,128)(2,1)}, bf16[128,1024]{1,0:T(8,128)(2,1)S(1)}, u32[]{:S(2)}, u32[]{:S(2)}) collective-permute-start(bf16[128,1024]{1,0:T(8,128)(2,1)} %get-tuple-element.101), channel_id=1, source_target_pairs={{0,1},{1,0},{2,3},{3,2},{4,5},{5,4},{6,7},{7,6},{8,9},{9,8},{10,11... | collective-permute-start | bytes 786440 | tf_op jit(solution)/shard_map/ppermute | solution.py:20
  115.3 13.9 %collective-permute-start.15 = (bf16[256,1024]{1,0:T(8,128)(2,1)S(1)}, bf16[256,1024]{1,0:T(8,128)(2,1)S(1)}, u32[]{:S(2)}, u32[]{:S(2)}) collective-permute-start(bf16[256,1024]{1,0:T(8,128)(2,1)S(1)} %collective-permute-done.14.refs_2_), channel_id=1, source_target_pairs={{0,2},{2,0},{4,6},{6,4},{8,10},{10,8},{12,14},{14,12},{16,18},{18,... | collective-permute-start | bytes 1572872 | tf_op jit(solution)/shard_map/ppermute | solution.py:20
  115.5 11.6 %collective-permute-start.18 = (bf16[256,256]{1,0:T(8,128)(2,1)}, bf16[256,256]{1,0:T(8,128)(2,1)}, u32[]{:S(2)}, u32[]{:S(2)}) collective-permute-start(bf16[256,256]{1,0:T(8,128)(2,1)} %get-tuple-element.109), channel_id=1, source_target_pairs={{0,6},{2,4},{4,2},{6,0},{8,14},{10,12},{12,10},{14,8},{16,22},{18,... | collective-permute-start | bytes 393224 | tf_op jit(solution)/shard_map/ppermute | solution.py:20
  120.7 8.2 %collective-permute-start.47 = (bf16[1,256,256]{2,1,0:T(8,128)(2,1)S(1)}, bf16[1,256,256]{2,1,0:T(8,128)(2,1)S(1)}, u32[]{:S(2)}, u32[]{:S(2)}) collective-permute-start(bf16[1,256,256]{2,1,0:T(8,128)(2,1)S(1)} %fusion), channel_id=1, source_target_pairs={{0,16},{2,18},{4,20},{6,22},{8,24},{10,26},{12,28},{14,30},{16,0},... | collective-permute-start | bytes 393224 | tf_op jit(solution)/shard_map/ppermute | solution.py:20
  123.5 18.4 %collective-permute-start.10 = (bf16[160,1024]{1,0:T(8,128)(2,1)S(1)}, bf16[160,1024]{1,0:T(8,128)(2,1)S(1)}, u32[]{:S(2)}, u32[]{:S(2)}) collective-permute-start(bf16[160,1024]{1,0:T(8,128)(2,1)S(1)} %add_convert_fusion.1), channel_id=1, source_target_pairs={{0,8},{2,10},{4,12},{6,14},{8,0},{10,2},{12,4},{14,6},{16,24},{18,... | collective-permute-start | bytes 983048 | tf_op jit(solution)/shard_map/ppermute | solution.py:20
  127.1 8.0 %collective-permute-start.26 = (bf16[256,256]{1,0:T(8,128)(2,1)}, bf16[256,256]{1,0:T(8,128)(2,1)}, u32[]{:S(2)}, u32[]{:S(2)}) collective-permute-start(bf16[256,256]{1,0:T(8,128)(2,1)} %get-tuple-element.113), channel_id=1, source_target_pairs={{0,2},{2,0},{4,6},{6,4},{8,10},{10,8},{12,14},{14,12},{16,18},{18,... | collective-permute-start | bytes 393224 | tf_op jit(solution)/shard_map/ppermute | solution.py:20
  127.1 8.9 %collective-permute-start.27 = (bf16[256,256]{1,0:T(8,128)(2,1)}, bf16[256,256]{1,0:T(8,128)(2,1)}, u32[]{:S(2)}, u32[]{:S(2)}) collective-permute-start(bf16[256,256]{1,0:T(8,128)(2,1)} %get-tuple-element.114), channel_id=1, source_target_pairs={{0,4},{2,6},{4,0},{6,2},{8,12},{10,14},{12,8},{14,10},{16,20},{18,... | collective-permute-start | bytes 393224 | tf_op jit(solution)/shard_map/ppermute | solution.py:20
  128.9 7.1 %collective-permute-start.28 = (bf16[256,256]{1,0:T(8,128)(2,1)}, bf16[256,256]{1,0:T(8,128)(2,1)}, u32[]{:S(2)}, u32[]{:S(2)}) collective-permute-start(bf16[256,256]{1,0:T(8,128)(2,1)} %get-tuple-element.115), channel_id=1, source_target_pairs={{0,6},{2,4},{4,2},{6,0},{8,14},{10,12},{12,10},{14,8},{16,22},{18,... | collective-permute-start | bytes 393224 | tf_op jit(solution)/shard_map/ppermute | solution.py:20
  129.3 14.5 %collective-permute-start.48 = (bf16[2,256,256]{2,1,0:T(8,128)(2,1)S(1)}, bf16[2,256,256]{2,1,0:T(8,128)(2,1)S(1)}, u32[]{:S(2)}, u32[]{:S(2)}) collective-permute-start(bf16[2,256,256]{2,1,0:T(8,128)(2,1)S(1)} %pad_maximum_fusion.5), channel_id=1, source_target_pairs={{0,8},{2,10},{4,12},{6,14},{8,0},{10,2},{12,4},{14,6},{16,24},{18,... | collective-permute-start | bytes 786440 | tf_op jit(solution)/shard_map/ppermute | solution.py:20
  135.2 17.5 %collective-permute-start.19 = (bf16[2,256,256]{2,1,0:T(8,128)(2,1)}, bf16[2,256,256]{2,1,0:T(8,128)(2,1)S(1)}, u32[]{:S(2)}, u32[]{:S(2)}) collective-permute-start(bf16[2,256,256]{2,1,0:T(8,128)(2,1)} %get-tuple-element.111), channel_id=1, source_target_pairs={{0,8},{2,10},{4,12},{6,14},{8,0},{10,2},{12,4},{14,6},{16,24},{18,... | collective-permute-start | bytes 786440 | tf_op jit(solution)/shard_map/ppermute | solution.py:20
  140.6 16.3 %collective-permute-start.29 = (bf16[2,256,256]{2,1,0:T(8,128)(2,1)}, bf16[2,256,256]{2,1,0:T(8,128)(2,1)S(1)}, u32[]{:S(2)}, u32[]{:S(2)}) collective-permute-start(bf16[2,256,256]{2,1,0:T(8,128)(2,1)} %get-tuple-element.117), channel_id=1, source_target_pairs={{0,8},{2,10},{4,12},{6,14},{8,0},{10,2},{12,4},{14,6},{16,24},{18,... | collective-permute-start | bytes 786440 | tf_op jit(solution)/shard_map/ppermute | solution.py:20
  142.0 30.1 %collective-permute-start.11 = (bf16[160,1024]{1,0:T(8,128)(2,1)S(1)}, bf16[160,1024]{1,0:T(8,128)(2,1)S(1)}, u32[]{:S(2)}, u32[]{:S(2)}) collective-permute-start(bf16[160,1024]{1,0:T(8,128)(2,1)S(1)} %add_convert_fusion), channel_id=1, source_target_pairs={{0,16},{2,18},{4,20},{6,22},{8,24},{10,26},{12,28},{14,30},{16,0},... | collective-permute-start | bytes 983048 | tf_op jit(solution)/shard_map/ppermute | solution.py:20
  143.8 56.0 %collective-permute-start.50 = (bf16[4,256,256]{2,1,0:T(8,128)(2,1)S(1)}, bf16[4,256,256]{2,1,0:T(8,128)(2,1)S(1)}, u32[]{:S(2)}, u32[]{:S(2)}) collective-permute-start(bf16[4,256,256]{2,1,0:T(8,128)(2,1)S(1)} %pad_maximum_fusion.2.refs_0_), channel_id=1, source_target_pairs={{0,4},{2,6},{4,0},{6,2},{8,12},{10,14},{12,8},{14,10},{16,20},{18,... | collective-permute-start | bytes 1572872 | tf_op jit(solution)/shard_map/ppermute | solution.py:20
  145.4 54.9 %collective-permute-start.49 = (bf16[4,256,256]{2,1,0:T(8,128)(2,1)S(1)}, bf16[4,256,256]{2,1,0:T(8,128)(2,1)}, u32[]{:S(2)}, u32[]{:S(2)}) collective-permute-start(bf16[4,256,256]{2,1,0:T(8,128)(2,1)S(1)} %pad_maximum_fusion.2.refs_0_), channel_id=1, source_target_pairs={{0,2},{2,0},{4,6},{6,4},{8,10},{10,8},{12,14},{14,12},{16,18},{18,... | collective-permute-start | bytes 1572872 | tf_op jit(solution)/shard_map/ppermute | solution.py:20
  152.8 16.3 %collective-permute-start.20 = (bf16[1,256,256]{2,1,0:T(8,128)(2,1)S(1)}, bf16[1,256,256]{2,1,0:T(8,128)(2,1)S(1)}, u32[]{:S(2)}, u32[]{:S(2)}) collective-permute-start(bf16[1,256,256]{2,1,0:T(8,128)(2,1)S(1)} %slice.134), channel_id=1, source_target_pairs={{0,16},{2,18},{4,20},{6,22},{8,24},{10,26},{12,28},{14,30},{16,0},... | collective-permute-start | bytes 393224 | tf_op jit(solution)/shard_map/ppermute | solution.py:20
  158.1 12.8 %collective-permute-start.30 = (bf16[1,256,256]{2,1,0:T(8,128)(2,1)S(1)}, bf16[1,256,256]{2,1,0:T(8,128)(2,1)S(1)}, u32[]{:S(2)}, u32[]{:S(2)}) collective-permute-start(bf16[1,256,256]{2,1,0:T(8,128)(2,1)S(1)} %slice.133), channel_id=1, source_target_pairs={{0,16},{2,18},{4,20},{6,22},{8,24},{10,26},{12,28},{14,30},{16,0},... | collective-permute-start | bytes 393224 | tf_op jit(solution)/shard_map/ppermute | solution.py:20
  169.0 13.9 %collective-permute-start.21 = (bf16[1,256,256]{2,1,0:T(8,128)(2,1)S(1)}, bf16[1,256,256]{2,1,0:T(8,128)(2,1)S(1)}, u32[]{:S(2)}, u32[]{:S(2)}) collective-permute-start(bf16[1,256,256]{2,1,0:T(8,128)(2,1)S(1)} %fusion.2), channel_id=1, source_target_pairs={{0,16},{2,18},{4,20},{6,22},{8,24},{10,26},{12,28},{14,30},{16,0},... | collective-permute-start | bytes 393224 | tf_op jit(solution)/shard_map/ppermute | solution.py:20
  171.0 9.8 %collective-permute-start.31 = (bf16[1,256,256]{2,1,0:T(8,128)(2,1)S(1)}, bf16[1,256,256]{2,1,0:T(8,128)(2,1)S(1)}, u32[]{:S(2)}, u32[]{:S(2)}) collective-permute-start(bf16[1,256,256]{2,1,0:T(8,128)(2,1)S(1)} %fusion.1), channel_id=1, source_target_pairs={{0,16},{2,18},{4,20},{6,22},{8,24},{10,26},{12,28},{14,30},{16,0},... | collective-permute-start | bytes 393224 | tf_op jit(solution)/shard_map/ppermute | solution.py:20
  180.8 9.3 %collective-permute-start.32 = (bf16[2,256,256]{2,1,0:T(8,128)(2,1)S(1)}, bf16[2,256,256]{2,1,0:T(8,128)(2,1)S(1)}, u32[]{:S(2)}, u32[]{:S(2)}) collective-permute-start(bf16[2,256,256]{2,1,0:T(8,128)(2,1)S(1)} %pad_maximum_fusion.4), channel_id=1, source_target_pairs={{0,8},{2,10},{4,12},{6,14},{8,0},{10,2},{12,4},{14,6},{16,24},{18,... | collective-permute-start | bytes 786440 | tf_op jit(solution)/shard_map/ppermute | solution.py:20
  182.9 11.3 %collective-permute-start.22 = (bf16[2,256,256]{2,1,0:T(8,128)(2,1)S(1)}, bf16[2,256,256]{2,1,0:T(8,128)(2,1)S(1)}, u32[]{:S(2)}, u32[]{:S(2)}) collective-permute-start(bf16[2,256,256]{2,1,0:T(8,128)(2,1)S(1)} %pad_maximum_fusion.3), channel_id=1, source_target_pairs={{0,8},{2,10},{4,12},{6,14},{8,0},{10,2},{12,4},{14,6},{16,24},{18,... | collective-permute-start | bytes 786440 | tf_op jit(solution)/shard_map/ppermute | solution.py:20
  190.2 15.8 %collective-permute-start.34 = (bf16[4,256,256]{2,1,0:T(8,128)(2,1)S(1)}, bf16[4,256,256]{2,1,0:T(8,128)(2,1)}, u32[]{:S(2)}, u32[]{:S(2)}) collective-permute-start(bf16[4,256,256]{2,1,0:T(8,128)(2,1)S(1)} %pad_maximum_fusion.1.refs_0_), channel_id=1, source_target_pairs={{0,4},{2,6},{4,0},{6,2},{8,12},{10,14},{12,8},{14,10},{16,20},{18,... | collective-permute-start | bytes 1572872 | tf_op jit(solution)/shard_map/ppermute | solution.py:20
  194.3 18.2 %collective-permute-start.24 = (bf16[4,256,256]{2,1,0:T(8,128)(2,1)S(1)}, bf16[4,256,256]{2,1,0:T(8,128)(2,1)}, u32[]{:S(2)}, u32[]{:S(2)}) collective-permute-start(bf16[4,256,256]{2,1,0:T(8,128)(2,1)S(1)} %pad_maximum_fusion.refs_0_), channel_id=1, source_target_pairs={{0,4},{2,6},{4,0},{6,2},{8,12},{10,14},{12,8},{14,10},{16,20},{18,... | collective-permute-start | bytes 1572872 | tf_op jit(solution)/shard_map/ppermute | solution.py:20
  199.8 26.5 %collective-permute-start.33 = (bf16[4,256,256]{2,1,0:T(8,128)(2,1)S(1)}, bf16[4,256,256]{2,1,0:T(8,128)(2,1)}, u32[]{:S(2)}, u32[]{:S(2)}) collective-permute-start(bf16[4,256,256]{2,1,0:T(8,128)(2,1)S(1)} %pad_maximum_fusion.1.refs_0_), channel_id=1, source_target_pairs={{0,2},{2,0},{4,6},{6,4},{8,10},{10,8},{12,14},{14,12},{16,18},{18,... | collective-permute-start | bytes 1572872 | tf_op jit(solution)/shard_map/ppermute | solution.py:20
  199.8 22.2 %collective-permute-start.23 = (bf16[4,256,256]{2,1,0:T(8,128)(2,1)S(1)}, bf16[4,256,256]{2,1,0:T(8,128)(2,1)}, u32[]{:S(2)}, u32[]{:S(2)}) collective-permute-start(bf16[4,256,256]{2,1,0:T(8,128)(2,1)S(1)} %pad_maximum_fusion.refs_0_), channel_id=1, source_target_pairs={{0,2},{2,0},{4,6},{6,4},{8,10},{10,8},{12,14},{14,12},{16,18},{18,... | collective-permute-start | bytes 1572872 | tf_op jit(solution)/shard_map/ppermute | solution.py:20
  200.3 17.4 %collective-permute-start.51 = (bf16[4,256,256]{2,1,0:T(8,128)(2,1)S(1)}, bf16[4,256,256]{2,1,0:T(8,128)(2,1)}, u32[]{:S(2)}, u32[]{:S(2)}) collective-permute-start(bf16[4,256,256]{2,1,0:T(8,128)(2,1)S(1)} %collective-permute-done.50.refs_2_), channel_id=1, source_target_pairs={{0,2},{2,0},{4,6},{6,4},{8,10},{10,8},{12,14},{14,12},{16,18},{18,... | collective-permute-start | bytes 1572872 | tf_op jit(solution)/shard_map/ppermute | solution.py:20
  206.0 20.3 %collective-permute-start.35 = (bf16[4,256,256]{2,1,0:T(8,128)(2,1)}, bf16[4,256,256]{2,1,0:T(8,128)(2,1)S(1)}, u32[]{:S(2)}, u32[]{:S(2)}) collective-permute-start(bf16[4,256,256]{2,1,0:T(8,128)(2,1)} %collective-permute-done.34.refs_2_), channel_id=1, source_target_pairs={{0,2},{2,0},{4,6},{6,4},{8,10},{10,8},{12,14},{14,12},{16,18},{18,... | collective-permute-start | bytes 1572872 | tf_op jit(solution)/shard_map/ppermute | solution.py:20
  212.6 9.4 %collective-permute-start.25 = (bf16[4,256,256]{2,1,0:T(8,128)(2,1)}, bf16[4,256,256]{2,1,0:T(8,128)(2,1)}, u32[]{:S(2)}, u32[]{:S(2)}) collective-permute-start(bf16[4,256,256]{2,1,0:T(8,128)(2,1)} %collective-permute-done.24.refs_2_), channel_id=1, source_target_pairs={{0,2},{2,0},{4,6},{6,4},{8,10},{10,8},{12,14},{14,12},{16,18},{18,... | collective-permute-start | bytes 1572872 | tf_op jit(solution)/shard_map/ppermute | solution.py:20
  (38 other events, 364.0 us)

commit v2 on v1

v2 whole, which is shorter than its diff:
```python
from functools import partial

import jax
import jax.numpy as jnp
import numpy as np
from jax import lax
from jax.experimental import pallas as pl
from jax.experimental.pallas import tpu as pltpu
from jax.sharding import PartitionSpec as P

epsilon = 1e-05
PARTS = 4
F32 = jnp.float32
BF16 = jnp.bfloat16
VM = 1.5
UNIT = 1.1e9


def exchange(array, axis, bit):
    count = lax.axis_size(axis)
    return lax.ppermute(array, axis, [(i, i ^ bit) for i in range(count)])


def mm(left, right):
    return lax.dot_general(left, right, (((1,), (0,)), ((), ())), preferred_element_type=F32)


def mm_rt(left, right):
    return lax.dot_general(left, right, (((1,), (1,)), ((), ())), preferred_element_type=F32)


def mm_lt(left, right):
    return lax.dot_general(left, right, (((0,), (0,)), ((), ())), preferred_element_type=F32)


def whole(array):
    zeros = (0,) * array.ndim
    return (array, pl.BlockSpec(array.shape, lambda *_: zeros))


def chunked(array, start=0):
    tail = (0,) * (array.ndim - 1)
    return (array, pl.BlockSpec((1,) + array.shape[1:], lambda c, dev: (c + start,) + tail))


def columns(array, width, at):
    if width % 128 == 0:
        return (array, pl.BlockSpec((array.shape[0], width), lambda c, dev: (0, at(c, dev))))
    pieces = array.reshape(array.shape[0], -1, width).transpose(1, 0, 2)
    spec = pl.BlockSpec((None, array.shape[0], width), lambda c, dev: (at(c, dev), 0, 0))
    return (pieces, spec)


def rows(array, height, at):
    return (array, pl.BlockSpec((height, array.shape[1]), lambda c, dev: (at(c, dev), 0)))


def split(value):
    high = value.astype(BF16)
    return high, (value - high.astype(F32)).astype(BF16)


def spread(value, pattern):
    high, low = split(value)
    return mm(high, pattern) + mm(low, pattern)


def out_whole(shape, dtype):
    zeros = (0,) * len(shape)
    return (jax.ShapeDtypeStruct(shape, dtype), pl.BlockSpec(shape, lambda *_: zeros))


def out_chunked(shape, dtype):
    tail = (0,) * (len(shape) - 1)
    spec = pl.BlockSpec((1,) + shape[1:], lambda c, dev: (c,) + tail)
    return (jax.ShapeDtypeStruct(shape, dtype), spec)


def run(body, name, device, ins, outs, steps, scratch=(), us=1.0):
    total = sum(a.size * a.dtype.itemsize for a, _ in ins)
    total += sum(s.size * s.dtype.itemsize for s, _ in outs)
    held = 0
    for array, spec in list(ins) + list(outs):
        size = array.dtype.itemsize
        for extent in spec.block_shape:
            size *= extent or 1
        held += size * (1 if size == array.size * array.dtype.itemsize else 2)
    for buffer in scratch:
        held += buffer.dtype.itemsize * int(np.prod(buffer.shape))
    return pl.pallas_call(
        body,
        name=name,
        out_shape=[shape for shape, _ in outs],
        grid_spec=pltpu.PrefetchScalarGridSpec(
            num_scalar_prefetch=1,
            grid=(steps,),
            in_specs=[spec for _, spec in ins],
            out_specs=[spec for _, spec in outs],
            scratch_shapes=list(scratch),
        ),
        compiler_params=pltpu.CompilerParams(
            dimension_semantics=("arbitrary",),
            vmem_limit_bytes=int(held * VM) + (3 << 20),
        ),
        cost_estimate=pl.CostEstimate(
            flops=int(us * UNIT), bytes_accessed=total, transcendentals=0
        ),
    )(device, *[a for a, _ in ins])


def iota(shape, dim):
    return lax.broadcasted_iota(jnp.int32, shape, dim)


def roll_rows(array, shift):
    if array.shape[1] % 128 == 0:
        return pltpu.roll(array, shift % array.shape[0], 0)
    return jnp.roll(array, shift, 0)


def conv_rows(inputs, taps, bias, marks):
    result = bias + taps[3:4] * inputs
    for offset in range(1, 4):
        shifted = roll_rows(inputs, offset) * marks[:, offset : offset + 1]
        result = result + taps[3 - offset : 4 - offset] * shifted
    return result


def conv_back(d_out, inputs, taps, marks):
    d_in = taps[3:4] * d_out
    grads = [None] * 4
    grads[3] = jnp.sum(d_out * inputs, axis=0, keepdims=True)
    for offset in range(1, 4):
        kept = d_out * marks[:, offset : offset + 1]
        d_in = d_in + taps[3 - offset : 4 - offset] * roll_rows(kept, -offset)
        grads[3 - offset] = jnp.sum(kept * roll_rows(inputs, offset), axis=0, keepdims=True)
    return d_in, grads, jnp.sum(d_out, axis=0, keepdims=True)


def softplus(value):
    return jnp.maximum(value, 0.0) + jnp.log1p(jnp.exp(-jnp.abs(value)))


def solution(mesh):
    members = mesh.shape["shard"]
    replicas = mesh.shape["rep"]
    assert replicas % PARTS == 0 and replicas // PARTS >= 2
    assert replicas & (replicas - 1) == 0 and members & (members - 1) == 0
    return jax.shard_map(
        partial(on_device, members, replicas),
        mesh=mesh,
        in_specs=(
            P(("rep", "shard"), None),
            P(("rep", "shard"), None),
            P(None, "shard"),
            P(None, None, "shard"),
            P(None, None, "shard"),
            P(None, None, "shard"),
            P(None, None, "shard"),
            P(None, None, "shard"),
            P(None, None, "shard"),
            P(None, "shard"),
            P(None, "shard"),
            P(None, "shard"),
            P(None, "shard"),
            P(None, "shard"),
            P(None, "shard"),
            P(None, "shard", None),
            P(),
            P(),
            P(),
        ),
        out_specs=(
            P(("rep", "shard"), None),
            P(("rep", "shard"), None),
            P(None, "shard"),
            P(None, None, "shard"),
            P(None, None, "shard"),
            P(None, None, "shard"),
            P(None, None, "shard"),
            P(None, None, "shard"),
            P(None, None, "shard"),
            P(None, "shard"),
            P(None, "shard"),
            P(None, "shard"),
            P(None, "shard"),
            P(None, "shard"),
            P(None, "shard"),
            P(None, "shard", None),
        ),
        check_vma=False,
    )


def on_device(
    members,
    replicas,
    hidden_in,
    cotangent,
    norm_gain,
    w_z,
    w_x,
    w_bc,
    w_dt,
    conv_x,
    conv_bc,
    bias_x,
    bias_bc,
    dt_bias,
    a_log,
    d_skip,
    gate_gain,
    w_out,
    seq_len,
    seq_owner,
    seq_start,
):
    S = members
    T, D = hidden_in.shape
    R = S * T
    C = w_z.shape[2]
    H = w_dt.shape[2]
    NB = w_bc.shape[2]
    CH = C // PARTS
    HC = H // PARTS
    HS = C // H
    inner = C * S
    spans = replicas // PARTS
    DCH = D // spans
    w_z, w_x, w_bc, w_dt, w_out = w_z[0], w_x[0], w_bc[0], w_dt[0], w_out[0]

    shard_at = lax.axis_index("shard")
    device = (lax.axis_index("rep") * S + shard_at).astype(jnp.int32).reshape(1)

    def me_of(dev):
        return lax.rem(dev[0], S)

    def part_of(dev):
        return lax.rem(lax.div(dev[0], S), PARTS)

    def span_of(dev):
        return lax.div(dev[0], S * PARTS)

    blocks = [slice(b * T, (b + 1) * T) for b in range(S)]

    if S == 2:
        gains = [norm_gain, exchange(norm_gain, "shard", 1)]
    else:
        gains = [lax.all_gather(norm_gain, "shard", axis=1, tiled=True)]
    hidden = [hidden_in] + [exchange(hidden_in, "shard", j) for j in range(1, S)]
    cots = [cotangent] + [exchange(cotangent, "shard", j) for j in range(1, S)]

    lens = seq_len.reshape(1, -1)
    owners = seq_owner.reshape(1, -1)
    starts = seq_start.reshape(1, -1)
    records = lens.shape[1]
    wdt_t = w_dt.T
    conv_x, conv_bc = conv_x[0], conv_bc[0]

    def chunk(c, dev):
        return part_of(dev) ^ c

    def to_part(value, c, dev):
        return pltpu.roll(value, lax.rem(128 - chunk(c, dev) * HC, 128), 1)

    def from_part(value, c, dev):
        return pltpu.roll(value, chunk(c, dev) * HC, 1)

    def head_pattern():
        return jnp.where(iota((128, CH), 0) == iota((128, CH), 1) // HS, 1.0, 0.0).astype(BF16)

    def head_pattern_t():
        return jnp.where(iota((CH, 128), 0) // HS == iota((CH, 128), 1), 1.0, 0.0).astype(BF16)

    def pad_lanes(value):
        gap = jnp.zeros((value.shape[0], 128 - value.shape[1]), F32)
        return jnp.concatenate([value, gap], axis=1)

    group = min(2, HC)
    width = group * HS

    def head_masks():
        lane = iota((1, width), 1) // HS
        return [jnp.where(lane == g, 1.0, 0.0) for g in range(group)]

    def prepare(dev, ln, ow, st, wbc, tbc, bbc, *refs):
        parts, refs = refs[: len(gains)], refs[len(gains) :]
        hid, refs = refs[:S], refs[S:]
        gain_r, normed_r, mask_r, cols_r, pbc_r, pre_r, map_r = refs[:7]
        sends = refs[7:]
        me = me_of(dev)
        base = dev[0] - me
        if S == 2:
            low, high = parts[0][...], parts[1][...]
            first = me == 0
            gain_r[...] = jnp.concatenate(
                [jnp.where(first, low, high), jnp.where(first, high, low)], axis=1
            )
        else:
            gain_r[...] = parts[0][...]
        lane = iota((T, 128), 1)
        row = iota((T, 128), 0)
        for b in range(S):
            x = hid[b][...].astype(F32)
            scale = lax.rsqrt(jnp.mean(x * x, axis=1, keepdims=True) + epsilon)
            normed_r[blocks[b], :] = (x * scale * gain_r[...]).astype(BF16)
            slot = iota((T, records), 0)
            covers = (
                (ow[...] == base + (me ^ b)) & (slot >= st[...]) & (slot < st[...] + ln[...])
            )
            ids = iota((T, records), 1).astype(F32)
            used = jnp.sum(jnp.where(covers, 1.0, 0.0), axis=1, keepdims=True)
            found = jnp.sum(jnp.where(covers, ids, 0.0), axis=1, keepdims=True)
            lone = (records + row).astype(F32)
            seg = jnp.where(used > 0.5, found, lone)
            seg_t = seg.T
            same = (seg == seg_t) & (row >= lane)
            mask_r[blocks[b], :] = jnp.where(same, 1.0, 0.0)
            cols = jnp.where(lane == 0, used, 0.0)
            for offset in range(1, 4):
                mark = (pltpu.roll(seg, offset, 0) == seg) & (row >= offset)
                cols = jnp.where(lane == offset, jnp.where(mark, 1.0, 0.0), cols)
            cols_r[blocks[b], :] = cols
        pbc_r[...] = mm(normed_r[...], wbc[...])
        for b in range(S):
            marks = cols_r[blocks[b], :]
            pre = conv_rows(pbc_r[blocks[b], :], tbc[...], bbc[...], marks)
            pre_r[blocks[b], :] = pre
            out = (pre * jax.nn.sigmoid(pre)).astype(BF16)
            map_r[blocks[b], :] = out
            for j in range(1, S):
                sends[j - 1][blocks[b ^ j], :] = out

    outs = run(
        prepare,
        "norm_and_maps",
        device,
        [whole(a) for a in (lens, owners, starts, w_bc, conv_bc, bias_bc, *gains, *hidden)],
        [
            out_whole((1, D), F32),
            out_whole((R, D), BF16),
            out_whole((R, 128), F32),
            out_whole((R, 128), F32),
            out_whole((R, NB), F32),
            out_whole((R, NB), F32),
            out_whole((R, NB), BF16),
        ]
        + [out_whole((R, NB), BF16) for _ in range(1, S)],
        1,
        us=2.5,
    )
    gain, normed, mask, cols, proj_bc, pre_bc, map_own = outs[:7]
    maps = [map_own] + [exchange(outs[6 + j], "shard", j) for j in range(1, S)]
    if S == 2:
        map_a, map_b = maps
    else:
        map_a = jnp.concatenate(maps[: S // 2], axis=1)
        map_b = jnp.concatenate(maps[S // 2 :], axis=1)

    normed_far = exchange(normed, "rep", 2)
    normed_all = [normed, exchange(normed, "rep", 1), normed_far, exchange(normed_far, "rep", 1)]

    def project(dev, n_r, wz, wx, wdt, dtb, alog, dsk, tx, bx, cols_r, wo, *refs):
        cot, refs = refs[:S], refs[S:]
        z_r, x_r, pre_r, y_r, cum_r, cumt_r, hp_r, sk_r, dm_r, cg_r = refs[:10]
        y_s, cum_s = refs[10:]
        c = pl.program_id(0)
        n = n_r[...]

        @pl.when(c == 0)
        def _():
            y_s[...] = pad_lanes(mm_rt(n, wdt[...]) + dtb[...])
            row = iota((T, 128), 0)
            rate = jnp.exp(pad_lanes(alog[...]))
            for b in range(S):
                total = -softplus(y_s[blocks[b], :]) * rate
                shift = 1
                while shift < T:
                    total = total + jnp.where(row >= shift, pltpu.roll(total, shift, 0), 0.0)
                    shift *= 2
                cum_s[blocks[b], :] = total
                cg_r[blocks[b], :] = cot[b][...]

        z_r[0] = mm(n, wz[...])
        x_r[0] = mm(n, wx[...])
        y_r[0] = to_part(y_s[...], c, dev)
        turned = to_part(cum_s[...], c, dev)
        cum_r[0] = turned
        pair = jnp.concatenate(
            [pad_lanes(alog[...]), pad_lanes(dsk[...]), jnp.zeros((6, 128), F32)], axis=0
        )
        pair = to_part(pair, c, dev)
        hp_r[0] = jnp.exp(pair)
        skips = [jnp.broadcast_to(pair[1:2, h : h + 1], (1, HS)) for h in range(HC)]
        sk_r[0] = jnp.broadcast_to(jnp.concatenate(skips, axis=1), (8, CH))
        dm_r[0] = mm_rt(cg_r[...], wo[...]) * cols_r[:, 0:1]
        for b in range(S):
            marks = cols_r[blocks[b], :]
            pre_r[0, blocks[b], :] = conv_rows(x_r[0, blocks[b], :], tx[...], bx[...], marks)
            cumt_r[0, b] = turned[blocks[b]].T[0:8]

    z, px, pre, y, cum, cum_t, head_rows, skip_rows, d_mixed, cot_group = run(
        project,
        "projections",
        device,
        [
            whole(normed),
            columns(w_z, CH, chunk),
            columns(w_x, CH, chunk),
            whole(wdt_t),
            whole(dt_bias),
            whole(a_log),
            whole(d_skip),
            columns(conv_x, CH, chunk),
            columns(bias_x, CH, chunk),
            whole(cols),
            rows(w_out, CH, chunk),
        ]
        + [whole(c) for c in cots],
        [
            out_chunked((PARTS, R, CH), F32),
            out_chunked((PARTS, R, CH), F32),
            out_chunked((PARTS, R, CH), F32),
            out_chunked((PARTS, R, 128), F32),
            out_chunked((PARTS, R, 128), F32),
            out_chunked((PARTS, S, 8, 128), F32),
            out_chunked((PARTS, 8, 128), F32),
            out_chunked((PARTS, 8, CH), F32),
            out_chunked((PARTS, R, CH), F32),
            out_whole((R, D), BF16),
        ],
        PARTS,
        scratch=[pltpu.VMEM((R, 128), F32), pltpu.VMEM((R, 128), F32)],
        us=4.0,
    )
    cots_far = exchange(cot_group, "rep", 2)
    cots_all = [
        cot_group,
        exchange(cot_group, "rep", 1),
        cots_far,
        exchange(cots_far, "rep", 1),
    ]

    def decays(cum_r, cumt_r, b, h):
        gap = cum_r[0, blocks[b], h : h + 1] - cumt_r[0, b, h : h + 1, :]
        return gap

    def fill_scores(dev, a_r, b_r, mask_r, scores):
        a_is_key = me_of(dev) < S // 2
        for b in range(S):

            @pl.when(a_is_key)
            def _():
                scores[b] = mm_rt(b_r[blocks[b], :], a_r[blocks[b], :]) * mask_r[blocks[b], :]

            @pl.when(jnp.logical_not(a_is_key))
            def _():
                scores[b] = mm_rt(a_r[blocks[b], :], b_r[blocks[b], :]) * mask_r[blocks[b], :]

    def scan_forward(
        dev, a_r, b_r, mask_r, pre_r, y_r, cum_r, cumt_r, sk, gg, z_r, dm_r, wo, *refs
    ):
        core_r, sums_r, own_r = refs[0], refs[1], refs[2]
        sum_sends = refs[3 : 2 + S]
        sends = refs[2 + S : 1 + 2 * S]
        scores, acc, sums, gated_s = refs[1 + 2 * S :]
        c = pl.program_id(0)

        @pl.when(c == 0)
        def _():
            fill_scores(dev, a_r, b_r, mask_r, scores)
            acc[...] = jnp.zeros_like(acc)
            sums[...] = jnp.zeros_like(sums)

        lane = iota((T, 128), 1)
        pattern = head_pattern()
        masks = head_masks()
        for b in range(S):
            before = pre_r[0, blocks[b], :]
            values = before * jax.nn.sigmoid(before)
            step = spread(softplus(y_r[0, blocks[b], :]), pattern)
            scaled = (values * step).astype(BF16)
            parts = []
            for first in range(0, HC, group):
                at = slice(first * HS, first * HS + width)
                weights = []
                for h in range(first, first + group):
                    gap = cum_r[0, blocks[b], h : h + 1] - cumt_r[0, b, h : h + 1, :]
                    weights.append(
                        (scores[b] * jnp.exp(jnp.minimum(gap, 0.0))).astype(BF16)
                    )
                stacked = [scaled[:, at] * m.astype(BF16) for m in masks]
                parts.append(
                    mm(jnp.concatenate(weights, axis=1), jnp.concatenate(stacked, axis=0))
                )
            core = jnp.concatenate(parts, axis=1) + values * sk[0, 0:1]
            core_r[0, blocks[b], :] = core
            zed = z_r[0, blocks[b], :]
            gated = core * (zed * jax.nn.sigmoid(zed))
            gained = gated * gg[...]
            gated_s[blocks[b], :] = gained.astype(BF16)
            squares = jnp.sum(gated * gated, axis=1, keepdims=True)
            dots = jnp.sum(dm_r[0, blocks[b], :] * gained, axis=1, keepdims=True)
            sums[blocks[b], :] += jnp.where(lane == 0, squares, jnp.where(lane == 1, dots, 0.0))
        acc[...] += mm(gated_s[...], wo[...])

        @pl.when(c == PARTS - 1)
        def _():
            own_r[...] = acc[blocks[0], :]
            for j in range(1, S):
                sends[j - 1][...] = acc[blocks[j], :].astype(BF16)
            for b in range(S):
                turned = sums[blocks[b], :].T[0:8]
                sums_r[:, blocks[b]] = turned
                for j in range(1, S):
                    sum_sends[j - 1][:, blocks[b ^ j]] = turned

    outs = run(
        scan_forward,
        "scan_forward",
        device,
        [
            whole(map_a),
            whole(map_b),
            whole(mask),
            chunked(pre),
            chunked(y),
            chunked(cum),
            chunked(cum_t),
            chunked(skip_rows),
            columns(gate_gain, CH, chunk),
            chunked(z),
            chunked(d_mixed),
            rows(w_out, CH, chunk),
        ],
        [
            out_chunked((PARTS, R, CH), F32),
            out_whole((8, R), F32),
            out_whole((T, D), F32),
        ]
        + [out_whole((8, R), F32) for _ in range(1, S)]
        + [out_whole((T, D), BF16) for _ in range(1, S)],
        PARTS,
        scratch=[
            pltpu.VMEM((S, T, T), F32),
            pltpu.VMEM((R, D), F32),
            pltpu.VMEM((R, 128), F32),
            pltpu.VMEM((R, CH), BF16),
        ],
        us=4.0,
    )
    core, sums_own, out_own = outs[:3]
    sums_all = [sums_own] + [exchange(outs[2 + j], "shard", j) for j in range(1, S)]
    out_sends = [outs[1 + S + j] for j in range(1, S)]

    def gate_backward(dev, core_r, z_r, dm_r, gg, cols_r, *refs):
        parts, refs = refs[:S], refs[S:]
        both_r = refs[:PARTS]
        cotz_c, dcore_r, gg_r, rows_r = refs[PARTS:]
        c = pl.program_id(0)
        lane = iota((T, 128), 1)

        @pl.when(c == 0)
        def _():
            for b in range(S):
                total = parts[0][:, blocks[b]]
                for j in range(1, S):
                    total = total + parts[j][:, blocks[b]]
                turned = jnp.concatenate([total, jnp.zeros((T - 8, 128), F32)], axis=0).T
                inverse = lax.rsqrt(turned[:, 0:1] / inner + epsilon)
                factor = inverse * inverse * inverse * turned[:, 1:2] / inner
                rows_r[blocks[b], :] = jnp.where(
                    lane == 0, inverse, jnp.where(lane == 1, factor, 0.0)
                )

        gate_sum = jnp.zeros((1, CH), F32)
        mixed_parts, cot_parts = [], []
        for b in range(S):
            inverse = rows_r[blocks[b], 0:1]
            factor = rows_r[blocks[b], 1:2]
            used = cols_r[blocks[b], 0:1]
            core = core_r[0, blocks[b], :]
            zed = z_r[0, blocks[b], :]
            sig = jax.nn.sigmoid(zed)
            gated = core * (zed * sig)
            d_mixed = dm_r[0, blocks[b], :]
            scaled = gated * inverse
            gate_sum = gate_sum + jnp.sum(d_mixed * scaled, axis=0, keepdims=True)
            d_gated = inverse * (d_mixed * gg[...]) - gated * factor
            dcore_r[0, blocks[b], :] = (d_gated * (zed * sig)).astype(BF16)
            d_z = d_gated * core * sig * (1.0 + zed * (1.0 - sig))
            mixed_parts.append((scaled * gg[...] * used).astype(BF16))
            cot_parts.append(d_z.astype(BF16))
            cotz_c[0, blocks[b], :] = cot_parts[b]
        gg_r[0] = jnp.broadcast_to(gate_sum, (8, CH))
        for r in range(PARTS):

            @pl.when(c == r)
            def _():
                for b in range(S):
                    both_r[r][blocks[b], 0:CH] = mixed_parts[b]
                    both_r[r][blocks[b], CH : 2 * CH] = cot_parts[b]

    outs = run(
        gate_backward,
        "gate_backward",
        device,
        [chunked(core), chunked(z), chunked(d_mixed), columns(gate_gain, CH, chunk), whole(cols)]
        + [whole(s) for s in sums_all],
        [out_whole((R, 2 * CH), BF16) for _ in range(PARTS)]
        + [
            out_chunked((PARTS, R, CH), BF16),
            out_chunked((PARTS, R, CH), BF16),
            out_chunked((PARTS, 8, CH), F32),
            out_whole((R, 128), F32),
        ],
        PARTS,
        us=2.2,
    )
    cotz, d_core, gate_grads, row_scale = outs[PARTS:]
    both_q = [outs[0]] + [exchange(outs[r], "rep", r) for r in range(1, PARTS)]

    half_parts = PARTS // 2

    def scan_backward(
        last, dev, a_r, b_r, mask_r, pre_r, px_r, y_r, cum_r, cumt_r, hp, sk, tx, core_r, dcore_r,
        cols_r, *refs
    ):
        if last:
            d_before, refs = refs[0], refs[1:]
        cotx_r, refs = refs[:half_parts], refs[half_parts:]
        cotx_c, cdt_r, cg_r, hg_r = refs[:4]
        if last:
            own_r, sends = refs[4], refs[5 : 4 + S]
            scores, scores_t, d_scores = refs[4 + S :]
        else:
            d_scores, scores, scores_t = refs[4:]
        c = pl.program_id(0)

        @pl.when(c == 0)
        def _():
            fill_scores(dev, a_r, b_r, mask_r, scores)
            for b in range(S):
                scores_t[b] = scores[b].T
            d_scores[...] = d_before[...] if last else jnp.zeros_like(d_scores)

        row = iota((T, 128), 0)
        lane = iota((T, 128), 1)
        pattern = head_pattern()
        pattern_t = head_pattern_t()
        masks = [m.astype(BF16) for m in head_masks()]
        tap_grads = [jnp.zeros((1, CH), F32) for _ in range(6)]
        bias_grad = jnp.zeros((1, 128), F32)
        rate_grad = jnp.zeros((1, 128), F32)
        cot_parts = []
        rate = hp[0, 0:1, :]
        for b in range(S):
            before = pre_r[0, blocks[b], :]
            sig = jax.nn.sigmoid(before)
            values = before * sig
            raw = y_r[0, blocks[b], :]
            step = softplus(raw)
            step_full = spread(step, pattern)
            scaled = (values * step_full).astype(BF16)
            d_out = dcore_r[0, blocks[b], :]
            d_scaled = []
            for first in range(0, HC, group):
                at = slice(first * HS, first * HS + width)
                stacked = jnp.concatenate([d_out[:, at] * m for m in masks], axis=0)
                d_weights = mm_rt(stacked, scaled[:, at])
                turned, change = [], None
                for g in range(group):
                    h = first + g
                    gap = cum_r[0, blocks[b], h : h + 1] - cumt_r[0, b, h : h + 1, :]
                    turned.append((scores_t[b] * jnp.exp(jnp.minimum(-gap, 0.0))).astype(BF16))
                    term = d_weights[g * T : (g + 1) * T] * jnp.exp(jnp.minimum(gap, 0.0))
                    change = term if change is None else change + term
                d_scores[b] += change
                d_scaled.append(mm(jnp.concatenate(turned, axis=1), stacked))
            d_scaled = jnp.concatenate(d_scaled, axis=1)
            d_out = d_out.astype(F32)
            plain = core_r[0, blocks[b], :] - values * sk[0, 0:1]
            d_cum = spread(d_out * plain - d_scaled * scaled.astype(F32), pattern_t)
            d_step = spread(d_scaled * values, pattern_t)
            shift = 1
            while shift < T:
                d_cum = d_cum + jnp.where(row < T - shift, pltpu.roll(d_cum, T - shift, 0), 0.0)
                shift *= 2
            rate_grad = rate_grad - jnp.sum(d_cum * step, axis=0, keepdims=True) * rate
            d_raw = (d_step - d_cum * rate) * jax.nn.sigmoid(raw)
            d_raw = jnp.where(lane < HC, d_raw, 0.0)
            bias_grad = bias_grad + jnp.sum(d_raw, axis=0, keepdims=True)
            cdt_r[0, blocks[b], :] = d_raw
            d_val = d_scaled * step_full + d_out * sk[0, 0:1]
            d_pre = d_val * sig * (1.0 + before * (1.0 - sig))
            d_in, grads, total = conv_back(
                d_pre, px_r[0, blocks[b], :], tx[...], cols_r[blocks[b], :]
            )
            skip = jnp.sum(d_out * values, axis=0, keepdims=True)
            for i, grad in enumerate(grads + [total, skip]):
                tap_grads[i] = tap_grads[i] + grad
            cot_parts.append(d_in.astype(BF16))
            cotx_c[0, blocks[b], :] = cot_parts[b]
        cg_r[0] = jnp.concatenate(tap_grads + [jnp.zeros((2, CH), F32)], axis=0)
        high, low = split(jnp.broadcast_to(tap_grads[5], (8, CH)))
        skip_grad = mm(high, pattern_t) + mm(low, pattern_t)
        hg_r[0] = jnp.concatenate(
            [bias_grad, rate_grad, skip_grad[0:1], jnp.zeros((5, 128), F32)], axis=0
        )
        for r in range(half_parts):

            @pl.when(c == r)
            def _():
                for b in range(S):
                    cotx_r[r][blocks[b], :] = cot_parts[b]

        if last:

            @pl.when(c == half_parts - 1)
            def _():
                a_is_key = me_of(dev) < S // 2

                def finish(key_first):
                    for b in range(S):
                        d_s = (d_scores[b] * mask_r[blocks[b], :]).astype(BF16)
                        a, bb = a_r[blocks[b], :], b_r[blocks[b], :]
                        if key_first:
                            both = (mm_lt(d_s, bb), mm(d_s, a))
                        else:
                            both = (mm(d_s, bb), mm_lt(d_s, a))
                        for j in range(S):
                            half = both[0] if j < S // 2 else both[1]
                            at = (j % (S // 2)) * NB
                            piece = half[:, at : at + NB]
                            if j == 0:
                                own_r[blocks[b], :] = piece
                            else:
                                sends[j - 1][blocks[b ^ j], :] = piece.astype(BF16)

                @pl.when(a_is_key)
                def _():
                    finish(True)

                @pl.when(jnp.logical_not(a_is_key))
                def _():
                    finish(False)

    def half_backward(last, carried):
        start = 0 if last else half_parts
        ins = [whole(map_a), whole(map_b), whole(mask)]
        for array in (pre, px, y, cum, cum_t, head_rows, skip_rows):
            ins.append(chunked(array, start))
        ins.append(columns(conv_x, CH, lambda c, dev: chunk(c + start, dev)))
        ins += [chunked(core, start), chunked(d_core, start), whole(cols)]
        outs = [out_whole((R, CH), BF16) for _ in range(half_parts)] + [
            out_chunked((half_parts, R, CH), BF16),
            out_chunked((half_parts, R, 128), F32),
            out_chunked((half_parts, 8, CH), F32),
            out_chunked((half_parts, 8, 128), F32),
        ]
        square = pltpu.VMEM((S, T, T), F32)
        if last:
            ins.append(whole(carried))
            outs += [out_whole((R, NB), F32)]
            outs += [out_whole((R, NB), BF16) for _ in range(1, S)]
            scratch = [square, square, square]
        else:
            outs += [out_whole((S, T, T), F32)]
            scratch = [square, square]
        return run(
            partial(scan_backward, last),
            "scan_backward_near" if last else "scan_backward_far",
            device,
            ins,
            outs,
            half_parts,
            scratch=scratch,
            us=5.0,
        )

    far = half_backward(False, None)
    cotx_far = [exchange(far[r], "rep", half_parts + r) for r in range(half_parts)]
    near = half_backward(True, far[half_parts + 4])
    cotx_q = [near[0], exchange(near[1], "rep", 1)] + cotx_far
    halves = [near[half_parts : half_parts + 4], far[half_parts : half_parts + 4]]
    d_map_own = near[half_parts + 4]
    d_map_other = [exchange(near[half_parts + 4 + j], "shard", j) for j in range(1, S)]

    def input_backward(dev, cz, near_x, far_x, near_dt, far_dt, wz, wx, wdt, dn_r, dt_r):
        c = pl.program_id(0)

        @pl.when(c == 0)
        def _():
            joined = jnp.zeros((R, 128), F32)
            for i in range(PARTS):
                held = (near_dt, far_dt)[i // half_parts]
                joined = joined + from_part(held[i % half_parts], i, dev)
            joined = joined.astype(BF16)
            dt_r[...] = joined
            dn_r[...] = mm(joined[:, 0:H], wdt[...])

        @pl.when(c < half_parts)
        def _():
            dn_r[...] += mm_rt(cz[0], wz[...]) + mm_rt(near_x[0], wx[...])

        @pl.when(c >= half_parts)
        def _():
            dn_r[...] += mm_rt(cz[0], wz[...]) + mm_rt(far_x[0], wx[...])

    def half_spec(array, first):
        def at(c, dev):
            if first:
                return (jnp.minimum(c, half_parts - 1), 0, 0)
            return (jnp.maximum(c - half_parts, 0), 0, 0)

        return (array, pl.BlockSpec((1,) + array.shape[1:], at))

    d_normed, cot_dt_all = run(
        input_backward,
        "input_backward",
        device,
        [
            chunked(cotz),
            half_spec(halves[0][0], True),
            half_spec(halves[1][0], False),
            whole(halves[0][1]),
            whole(halves[1][1]),
            columns(w_z, CH, chunk),
            columns(w_x, CH, chunk),
            whole(wdt_t),
        ],
        [out_whole((R, D), F32), out_whole((R, 128), BF16)],
        PARTS,
        us=3.0,
    )

    small_rows = -(-(NB + H + 16) // 16) * 16

    def maps_backward(
        dev, own, pre_r, pbc_r, cols_r, tbc, n_r, wbc, dn_r, cdt, cg0, cg1, hg0, hg1, gg, *refs
    ):
        others, hid, refs = refs[: S - 1], refs[S - 1 : 2 * S - 1], refs[2 * S - 1 :]
        kept, refs = refs[: S - 1], refs[S - 1 :]
        dn_own, pack_r = refs[0], refs[1]
        sends = refs[2 : 1 + S]
        cot_s, dn_s = refs[1 + S :]
        pack_r[...] = jnp.zeros_like(pack_r)
        grads = [jnp.zeros((1, NB), F32) for _ in range(5)]
        for b in range(S):
            d_map = own[blocks[b], :]
            for other in others:
                d_map = d_map + other[blocks[b], :].astype(F32)
            before = pre_r[blocks[b], :]
            sig = jax.nn.sigmoid(before)
            d_pre = d_map * sig * (1.0 + before * (1.0 - sig))
            d_in, taps, total = conv_back(d_pre, pbc_r[blocks[b], :], tbc[...], cols_r[blocks[b], :])
            for i, grad in enumerate(taps + [total]):
                grads[i] = grads[i] + grad
            cot_s[blocks[b], :] = d_in.astype(BF16)
        dn_s[...] = dn_r[...] + mm_rt(cot_s[...], wbc[...])
        dn_own[...] = dn_s[blocks[0], :]
        gain_sum = jnp.zeros((1, D), F32)
        for b in range(S):
            x = hid[b][...].astype(F32)
            scale = lax.rsqrt(jnp.mean(x * x, axis=1, keepdims=True) + epsilon)
            part = dn_s[blocks[b], :]
            gain_sum = gain_sum + jnp.sum(part * (x * scale), axis=0, keepdims=True)
            if b > 0:
                sends[b - 1][:, 0:D] = part.astype(BF16)
                sends[b - 1][:, D : 2 * D] = kept[b - 1][...]
        pack_r[0:NB, :] = mm_lt(cot_s[...], n_r[...])
        pack_r[NB : NB + H, :] = mm_lt(cdt[...], n_r[...])[0:H]
        at = NB + H
        heads = jnp.zeros((8, 128), F32)
        for i in range(PARTS):
            heads = heads + from_part((hg0, hg1)[i // half_parts][i % half_parts], i, dev)
        pack_r[at + 6 : at + 9, 0:128] = heads[0:3]
        mine = part_of(dev)
        for m in range(PARTS):

            @pl.when(mine == m)
            def _():
                for i in range(PARTS):
                    cg = (cg0, cg1)[i // half_parts]
                    lanes = slice((m ^ i) * CH, ((m ^ i) + 1) * CH)
                    pack_r[at : at + 5, lanes] = cg[i % half_parts, 0:5]
                    pack_r[at + 5 : at + 6, lanes] = gg[i, 0:1]

        for i in range(5):
            pack_r[at + 9 + i : at + 10 + i, 0:NB] = grads[i]
        pack_r[at + 14 : at + 15, :] = gain_sum

    outs = run(
        maps_backward,
        "maps_backward",
        device,
        [
            whole(a)
            for a in (
                d_map_own,
                pre_bc,
                proj_bc,
                cols,
                conv_bc,
                normed,
                w_bc,
                d_normed,
                cot_dt_all,
                halves[0][2],
                halves[1][2],
                halves[0][3],
                halves[1][3],
                gate_grads,
                *d_map_other,
                *hidden,
                *out_sends,
            )
        ],
        [out_whole((T, D), F32), out_whole((small_rows, D), F32)]
        + [out_whole((T, 2 * D), BF16) for _ in range(1, S)],
        1,
        scratch=[pltpu.VMEM((R, NB), BF16), pltpu.VMEM((R, D), F32)],
        us=3.0,
    )
    dn_own, pack = outs[:2]
    dn_other = [exchange(outs[1 + j], "shard", j) for j in range(1, S)]

    def own_rows(dev, hid, cot, cols_r, rows_r, gain_r, dn_r, out_r, *refs):
        others, refs = refs[: S - 1], refs[S - 1 :]
        hidden_r, grad_r = refs
        used = cols_r[:, 0:1]
        x = hid[...].astype(F32)
        added = out_r[...]
        for other in others:
            added = added + other[:, D : 2 * D].astype(F32)
        hidden_r[...] = used * (x + rows_r[:, 0:1] * added)
        d_n = dn_r[...]
        for other in others:
            d_n = d_n + other[:, 0:D].astype(F32)
        scale = lax.rsqrt(jnp.mean(x * x, axis=1, keepdims=True) + epsilon)
        u = d_n * gain_r[...]
        dot = jnp.mean(u * x, axis=1, keepdims=True)
        grad_r[...] = used * cot[...].astype(F32) + scale * u - x * (scale * scale * scale * dot)

    hidden_out, grad_hidden = run(
        own_rows,
        "own_rows",
        device,
        [
            whole(hidden_in),
            whole(cotangent),
            (cols, pl.BlockSpec((T, 128), lambda *_: (0, 0))),
            (row_scale, pl.BlockSpec((T, 128), lambda *_: (0, 0))),
        ]
        + [whole(a) for a in (gain, dn_own, out_own, *dn_other)],
        [out_whole((T, D), F32), out_whole((T, D), F32)],
        1,
    )

    def split_specs(shape):
        half = spans // 2
        send = pl.BlockSpec((1,) + shape, lambda i, dev: (jnp.minimum(i, half - 1), 0, 0, 0))
        keep = pl.BlockSpec((1,) + shape, lambda i, dev: (jnp.maximum(i - half, 0), 0, 0, 0))
        return [
            (jax.ShapeDtypeStruct((half,) + shape, BF16), send),
            (jax.ShapeDtypeStruct((half,) + shape, F32), keep),
        ]

    def relative(i):
        half = spans // 2
        return jnp.where(i < half, 2 * i + 1, 2 * (i - half))

    def by_span(array):
        height = array.shape[0]
        return (array, pl.BlockSpec((height, DCH), lambda i, dev: (0, span_of(dev) ^ relative(i))))

    def store_split(value, slot, send_r, keep_r):
        i = pl.program_id(0)

        @pl.when(i < spans // 2)
        def _():
            send_r[0, slot] = value.astype(BF16)

        @pl.when(i >= spans // 2)
        def _():
            keep_r[0, slot] = value

    def pair_weight_grad(dev, *refs):
        both, cot, norm = refs[:PARTS], refs[PARTS : 2 * PARTS], refs[2 * PARTS : 3 * PARTS]
        value = jnp.zeros((CH, DCH), F32)
        other = jnp.zeros((CH, DCH), F32)
        for r in range(PARTS):
            value = value + mm_lt(both[r][:, 0:CH], cot[r][...])
            other = other + mm_lt(both[r][:, CH : 2 * CH], norm[r][...])
        store_split(value, 0, *refs[3 * PARTS :])
        store_split(other, 1, *refs[3 * PARTS :])

    def x_weight_grad(dev, *refs):
        value = jnp.zeros((CH, DCH), F32)
        for r in range(PARTS):
            value = value + mm_lt(refs[r][...], refs[PARTS + r][...])
        store_split(value, 0, *refs[2 * PARTS :])

    def sum_spans(send, keep):
        bit = PARTS
        total = keep + exchange(send, "rep", bit).astype(F32)
        while total.shape[0] > 1:
            bit *= 2
            send = total[1::2].astype(BF16)
            total = total[0::2] + exchange(send, "rep", bit).astype(F32)
        held = total.astype(BF16)
        while bit >= PARTS:
            held = jnp.concatenate([held, exchange(held, "rep", bit)], axis=0)
            bit //= 2
        far = exchange(held, "rep", 2)
        return [held, exchange(held, "rep", 1), far, exchange(far, "rep", 1)]

    def reversed_bits(i):
        result = jnp.int32(0) * i
        count = spans.bit_length() - 1
        for b in range(count):
            result = result | (((i >> b) & 1) << (count - 1 - b))
        return result

    def in_spec(name=None):
        def at(i, dev):
            return (span_of(dev) ^ reversed_bits(i), 0)

        return (jax.ShapeDtypeStruct((D, C), F32), pl.BlockSpec((DCH, C), at))

    def out_spec():
        def at(i, dev):
            return (0, span_of(dev) ^ reversed_bits(i))

        return (jax.ShapeDtypeStruct((C, D), F32), pl.BlockSpec((C, DCH), at))

    def join_pair(dev, *refs):
        mine = part_of(dev)
        for m in range(PARTS):

            @pl.when(mine == m)
            def _():
                for r in range(PARTS):
                    at = slice((m ^ r) * CH, ((m ^ r) + 1) * CH)
                    refs[PARTS][at, :] = refs[r][0, 0].astype(F32)
                    refs[PARTS + 1][:, at] = refs[r][0, 1].astype(F32).T

    def join_x(dev, *refs):
        mine = part_of(dev)
        for m in range(PARTS):

            @pl.when(mine == m)
            def _():
                for r in range(PARTS):
                    at = slice((m ^ r) * CH, ((m ^ r) + 1) * CH)
                    refs[PARTS][:, at] = refs[r][0, 0].astype(F32).T

    send, keep = run(
        pair_weight_grad,
        "pair_weight_grad",
        device,
        [whole(b) for b in both_q]
        + [by_span(c) for c in cots_all]
        + [by_span(n) for n in normed_all],
        split_specs((2, CH, DCH)),
        spans,
        us=5.0,
    )
    pieces = sum_spans(send, keep)
    grad_out, grad_z = run(
        join_pair,
        "join_pair",
        device,
        [chunked(p) for p in pieces],
        [out_spec(), in_spec()],
        spans,
        us=6.0,
    )
    send, keep = run(
        x_weight_grad,
        "x_weight_grad",
        device,
        [whole(c) for c in cotx_q] + [by_span(n) for n in normed_all],
        split_specs((1, CH, DCH)),
        spans,
        us=2.5,
    )
    pieces = sum_spans(send, keep)
    (grad_x,) = run(
        join_x,
        "join_x",
        device,
        [chunked(p) for p in pieces],
        [in_spec()],
        spans,
        us=4.0,
    )

    bit = 1
    while bit < replicas:
        rounded = pack.astype(BF16)
        pack = rounded.astype(F32) + exchange(rounded, "rep", bit).astype(F32)
        bit *= 2

    def unpack(dev, pack_r, *refs):
        at = NB + H
        refs[0][...] = pack_r[0:NB, :].T
        refs[1][...] = pack_r[NB:at, :]
        refs[2][...] = pack_r[at : at + 4, 0:C]
        refs[3][...] = pack_r[at + 9 : at + 13, 0:NB]
        refs[4][...] = pack_r[at + 4 : at + 5, 0:C]
        refs[5][...] = pack_r[at + 13 : at + 14, 0:NB]
        for i in range(3):
            refs[6 + i][...] = pack_r[at + 6 + i : at + 7 + i, 0:H]
        refs[9][...] = pack_r[at + 5 : at + 6, 0:C]
        me = me_of(dev)
        for m in range(S):

            @pl.when(me == m)
            def _():
                for j in range(S):
                    lanes = slice((m ^ j) * (D // S), ((m ^ j) + 1) * (D // S))
                    refs[10 + j][...] = pack_r[at + 14 : at + 15, lanes]

    outs = run(
        unpack,
        "unpack",
        device,
        [whole(pack)],
        [
            out_whole(shape, F32)
            for shape in [(D, NB), (H, D), (4, C), (4, NB), (1, C), (1, NB)]
            + [(1, H)] * 3
            + [(1, C)]
            + [(1, D // S)] * S
        ],
        1,
        us=1.5,
    )
    grad_bc, grad_dt, grad_conv_x, grad_conv_bc, grad_bias_x, grad_bias_bc = outs[:6]
    heads, grad_gate = outs[6:9], outs[9]
    grad_gain = outs[10]
    for j in range(1, S):
        grad_gain = grad_gain + exchange(outs[10 + j], "shard", j)
    return (
        hidden_out,
        grad_hidden,
        grad_gain,
        grad_z[None],
        grad_x[None],
        grad_bc[None],
        grad_dt.T[None],
        grad_conv_x[None],
        grad_conv_bc[None],
        grad_bias_x,
        grad_bias_bc,
        *heads,
        grad_gate,
        grad_out[None],
    )
```

time: 233 us -> 176 us (0.76)
  Pallas kernels: 82.2 us -> 35.2 us
  waiting for transfers between devices: 75.5 us -> 98.1 us
  starting transfers between devices: 47.9 us -> 33.7 us
  local copies, waits for them, and re-layouts: 16.6 us -> 6.07 us
  other arithmetic: 7.98 us -> 1.52 us
    pallas_call x14, Pallas kernels: 82.2 us -> 35.2 us  [run(): pl.pallas_call(body, name=name, out_shape=[shape for shape, _ in outs], g...]
    ppermute x52 -> x38, waiting for transfers between devices: 75.5 us -> 98.1 us  [exchange(): return lax.ppermute(array, axis, [(i, i ^ bit) for i in range(count)])]
    ppermute x52 -> x38, starting transfers between devices: 47.9 us -> 33.7 us  [exchange(): return lax.ppermute(array, axis, [(i, i ^ bit) for i in range(count)])]
    slice x7 -> x0, local copies, waits for them, and re-layouts: 2.91 us -> none  [the longest x1 0.61 us: on_device(): grad_gate = pack[at + 5:at + 6, 0:C]]
    broadcast_in_dim x8 -> x0, local copies, waits for them, and re-layouts: 2.67 us -> none  [the longest x2 0.81 us: on_device(): jnp.repeat(d_skip, HS, axis=1)]
    concatenate x3 -> x0, other arithmetic: 2.64 us -> none  [the longest x1 1.36 us: on_device(): jnp.concatenate([conv_bc[0], bias_bc, jnp.zeros((3, NB), F32)], axis=0)]
    unnamed x70 -> x44, local copies, waits for them, and re-layouts: 6.33 us -> 6.03 us
  transfers between devices with their start and end apart: 52 -> 38, of which waited for: 16 -> 17; matrix products, arithmetic and copies ran while one was open for 9% -> 1% of each run, Pallas kernels for 32% -> 16%
where the time goes in v2:
time: 176 us
  waiting for transfers between devices  98.1 us (56%)
  Pallas kernels  35.2 us (20%)
  starting transfers between devices  33.7 us (19%)
  local copies, waits for them, and re-layouts  6.07 us (3%)
    ppermute x38, waiting for transfers between devices, exchange(): return lax.ppermute(array, axis, [(i, i ^ bit) for i in range(count)])  98.1 us
    pallas_call x14, Pallas kernels, run(): pl.pallas_call(body, name=name, out_shape=[shape for shape, _ in outs], g...  35.2 us
    ppermute x38, starting transfers between devices, exchange(): return lax.ppermute(array, axis, [(i, i ^ bit) for i in range(count)])  33.7 us
    unnamed x44, local copies, waits for them, and re-layouts  6.03 us
  transfers between devices with their start and end apart: 38, of which 17 were waited for; matrix products, arithmetic and copies ran while one was open for 1% of the time, Pallas kernels for 16%

profile of v2, /device:TPU:0, one launch (start us, length us, event | category | flops | bytes accessed | tf_op | source)
XLA Modules:
  0.0 175.7 jit_solution(7114891384644435561)
XLA Ops:
  0.6 3.0 %collective-permute-start.1 = (bf16[128,1024]{1,0:T(8,128)(2,1)}, bf16[128,1024]{1,0:T(8,128)(2,1)S(1)}, u32[]{:S(2)}, u32[]{:S(2)}) collective-permute-start(bf16[128,1024]{1,0:T(8,128)(2,1)} %hid.1), channel_id=1, source_target_pairs={{0,1},{1,0},{2,3},{3,2},{4,5},{5,4},{6,7},{7,6},{8,9},{9,8},{10,11... | collective-permute-start | bytes 786440 | tf_op jit(solution)/shard_map/ppermute | solution.py:21
  3.8 1.9 %collective-permute-start = (f32[1,512]{1,0:T(1,128)}, f32[1,512]{1,0:T(1,128)S(1)}, u32[]{:S(2)}, u32[]{:S(2)}) collective-permute-start(f32[1,512]{1,0:T(1,128)} %refs_0_.2), channel_id=1, source_target_pairs={{0,1},{1,0},{2,3},{3,2},{4,5},{5,4},{6,7},{7,6},{8,9},{9,8},{10,11... | collective-permute-start | bytes 6152 | tf_op jit(solution)/shard_map/ppermute | solution.py:21
  5.7 10.2 %collective-permute-done.refs_1_ = f32[1,512]{1,0:T(1,128)S(1)} collective-permute-done((f32[1,512]{1,0:T(1,128)}, f32[1,512]{1,0:T(1,128)S(1)}, u32[]{:S(2)}, u32[]{:S(2)}) %collective-permute-start) | collective-permute-done | bytes 2080 | tf_op jit(solution)/shard_map/ppermute | solution.py:21
  15.9 0.9 copy-done.3
  16.8 0.9 copy-done.5
  17.8 0.7 copy-done.12
  18.5 0.7 copy-done.13
  19.1 0.7 copy-done.15
  22.6 1.8 %collective-permute-start.2 = (bf16[256,128]{1,0:T(8,128)(2,1)S(1)}, bf16[256,128]{1,0:T(8,128)(2,1)S(1)}, u32[]{:S(2)}, u32[]{:S(2)}) collective-permute-start(bf16[256,128]{1,0:T(8,128)(2,1)S(1)} %get-tuple-element.89), channel_id=1, source_target_pairs={{0,1},{1,0},{2,3},{3,2},{4,5},{5,4},{6,7},{7,6},{8,9},{9,8},{10,11... | collective-permute-start | bytes 196616 | tf_op jit(solution)/shard_map/ppermute | solution.py:21
  24.4 1.5 collective-permute-start.19
  26.0 4.0 %projections.1 = (f32[4,256,256]{2,1,0:T(8,128)S(1)}, f32[4,256,256]{2,1,0:T(8,128)S(1)}, f32[4,256,256]{2,1,0:T(8,128)S(1)}, f32[4,256,128]{2,1,0:T(8,128)S(1)}...) custom-call(s32[1]{0:T(128)} %bitcast.dev, ...), custom_call_target="tpu_custom_call" | custom-call | flops 4400000000 | bytes 13373632 | tf_op jit(solution)/shard_map/projections/pallas_call | solution.py:90
  30.6 3.3 %scan_forward.1 = (f32[4,256,256]{2,1,0:T(8,128)S(1)}, f32[8,256]{1,0:T(8,128)S(1)}, f32[128,1024]{1,0:T(8,128)S(1)}, f32[8,256]{1,0:T(8,128)S(1)}, bf16[128,1024]{1,0:T(8,128)(2,1)S(1)}) custom-call(s32[1]{0:T(128)} %bitcast.dev, bf16[256,128]{1,0:T(8,128)(2,1)S(1)} %get-tuple-element.88.a_r, bf16[256,128]{1,0:T(8,128)(2,1)S(1)} %collective-permute-done.2.b_r, ...), custom_call_target="tpu_custom_call" | custom-call | flops 4400000000 | bytes 8474624 | tf_op jit(solution)/shard_map/scan_forward/pallas_call | solution.py:90
  34.0 1.5 collective-permute-start.4
  35.5 2.2 %collective-permute-done.4.refs_1_ = f32[8,256]{1,0:T(8,128)S(1)} collective-permute-done((f32[8,256]{1,0:T(8,128)S(1)}, f32[8,256]{1,0:T(8,128)S(1)}, u32[]{:S(2)}, u32[]{:S(2)}) %collective-permute-start.4) | collective-permute-done | bytes 8224 | tf_op jit(solution)/shard_map/ppermute | solution.py:21
  37.7 1.6 gate_backward.1
  39.9 1.5 collective-permute-start.13
  41.3 9.1 %collective-permute-done.16.refs_6_ = bf16[256,1024]{1,0:T(8,128)(2,1)S(1)} collective-permute-done((bf16[256,1024]{1,0:T(8,128)(2,1)S(1)}, bf16[256,1024]{1,0:T(8,128)(2,1)S(1)}, u32[]{:S(2)}, u32[]{:S(2)}) %collective-permute-start.16) | collective-permute-done | bytes 524320 | tf_op jit(solution)/shard_map/ppermute | solution.py:21
  51.0 2.8 %collective-permute-done.13.refs_2_ = bf16[256,512]{1,0:T(8,128)(2,1)S(1)} collective-permute-done((bf16[256,512]{1,0:T(8,128)(2,1)S(1)}, bf16[256,512]{1,0:T(8,128)(2,1)S(1)}, u32[]{:S(2)}, u32[]{:S(2)}) %collective-permute-start.13) | collective-permute-done | bytes 262176 | tf_op jit(solution)/shard_map/ppermute | solution.py:21
  53.7 8.6 %collective-permute-done.14.refs_3_ = bf16[256,512]{1,0:T(8,128)(2,1)S(1)} collective-permute-done((bf16[256,512]{1,0:T(8,128)(2,1)S(1)}, bf16[256,512]{1,0:T(8,128)(2,1)S(1)}, u32[]{:S(2)}, u32[]{:S(2)}) %collective-permute-start.14) | collective-permute-done | bytes 262176 | tf_op jit(solution)/shard_map/ppermute | solution.py:21
  62.3 3.1 %pair_weight_grad.1 = (bf16[2,2,256,256]{3,2,1,0:T(8,128)(2,1)S(1)}, f32[2,2,256,256]{3,2,1,0:T(8,128)S(1)}) custom-call(s32[1]{0:T(128)} %bitcast.dev, bf16[256,512]{1,0:T(8,128)(2,1)S(1)} %get-tuple-element.133.refs_0_, bf16[256,512]{1,0:T(8,128)(2,1)S(1)} %collective-permute-done.12.refs_1_, bf16[256,512]{1,0:T(8,128)(2,1)S(1)} %collective-permute-done.13.refs_2_, ...), custom_call_target="tpu_custom_call" | custom-call | flops 5500000256 | bytes 6815744 | tf_op jit(solution)/shard_map/pair_weight_grad/pallas_call | solution.py:90
  65.4 1.6 collective-permute-start.21
  67.1 3.5 %scan_backward_far.1 = (bf16[256,256]{1,0:T(8,128)(2,1)S(1)}, bf16[256,256]{1,0:T(8,128)(2,1)S(1)}, bf16[2,256,256]{2,1,0:T(8,128)(2,1)S(1)}, f32[2,256,128]{2,1...) custom-call(s32[1]{0:T(128)} %bitcast.dev, ...), custom_call_target="tpu_custom_call" | custom-call | flops 5500000256 | bytes 6152192 | tf_op jit(solution)/shard_map/scan_backward_far/pallas_call | solution.py:90
  70.6 3.7 %scan_backward_near.1 = (bf16[256,256]{1,0:T(8,128)(2,1)S(1)}, bf16[256,256]{1,0:T(8,128)(2,1)S(1)}, bf16[2,256,256]{2,1,0:T(8,128)(2,1)S(1)}, f32[2,256,128]{2,...) custom-call(s32[1]{0:T(128)} %bitcast.dev, ...), custom_call_target="tpu_custom_call" | custom-call | flops 5500000256 | bytes 6348800 | tf_op jit(solution)/shard_map/scan_backward_near/pallas_call | solution.py:90
  75.5 1.2 collective-permute-start.30
  76.8 2.7 %collective-permute-done.21 = bf16[2,2,256,256]{3,2,1,0:T(8,128)(2,1)S(1)} collective-permute-done((bf16[2,2,256,256]{3,2,1,0:T(8,128)(2,1)S(1)}, bf16[2,2,256,256]{3,2,1,0:T(8,128)(2,1)S(1)}, u32[]{:S(2)}, u32[]{:S(2)}) %collective-permute-start.21) | collective-permute-done | bytes 524320 | tf_op jit(solution)/shard_map/ppermute | solution.py:21
  79.6 2.7 %collective-permute-start.22 = (bf16[1,2,256,256]{3,2,1,0:T(8,128)(2,1)S(1)}, bf16[1,2,256,256]{3,2,1,0:T(8,128)(2,1)S(1)}, u32[]{:S(2)}, u32[]{:S(2)}) collective-permute-start(bf16[1,2,256,256]{3,2,1,0:T(8,128)(2,1)S(1)} %slice.34), channel_id=1, source_target_pairs={{0,16},{2,18},{4,20},{6,22},{8,24},{10,26},{12,28},{14,30},{16,0},... | collective-permute-start | bytes 786440 | tf_op jit(solution)/shard_map/ppermute | solution.py:21
  82.3 3.1 %input_backward.1 = (f32[256,1024]{1,0:T(8,128)S(1)}, bf16[256,128]{1,0:T(8,128)(2,1)S(1)}) custom-call(s32[1]{0:T(128)} %bitcast.dev, bf16[4,256,256]{2,1,0:T(8,128)(2,1)S(1)} %get-tuple-element.111.cz, bf16[2,256,256]{2,1,0:T(8,128)(2,1)S(1)} %get-tuple-element.112.near_x, bf16[2,256,256]{2,1,0:T(8,128)(2,1)S(1)} %get-tuple-element.113.far_x, ...), custom_call_target="tpu_custom_call" | custom-call | flops 3300000000 | bytes 6914048 | tf_op jit(solution)/shard_map/input_backward/pallas_call | solution.py:90
  85.4 2.0 %x_weight_grad.1 = (bf16[2,1,256,256]{3,2,1,0:T(8,128)(2,1)S(1)}, f32[2,1,256,256]{3,2,1,0:T(8,128)S(1)}) custom-call(s32[1]{0:T(128)} %bitcast.dev, bf16[256,256]{1,0:T(8,128)(2,1)S(1)} %get-tuple-element.141.refs_0_, bf16[256,256]{1,0:T(8,128)(2,1)S(1)} %collective-permute-done.28.refs_1_, bf16[256,256]{1,0:T(8,128)(2,1)S(1)} %collective-permute-done.29.refs_2_, ...), custom_call_target="tpu_custom_call" | custom-call | flops 2750000128 | bytes 3407872 | tf_op jit(solution)/shard_map/x_weight_grad/pallas_call | solution.py:90
  87.5 1.6 collective-permute-start.31
  89.1 4.7 %collective-permute-done.22 = bf16[1,2,256,256]{3,2,1,0:T(8,128)(2,1)S(1)} collective-permute-done((bf16[1,2,256,256]{3,2,1,0:T(8,128)(2,1)S(1)}, bf16[1,2,256,256]{3,2,1,0:T(8,128)(2,1)S(1)}, u32[]{:S(2)}, u32[]{:S(2)}) %collective-permute-start.22) | collective-permute-done | bytes 262176 | tf_op jit(solution)/shard_map/ppermute | solution.py:21
  94.0 1.1 maps_backward.1
  95.2 12.4 %collective-permute-done.23 = bf16[1,2,256,256]{3,2,1,0:T(8,128)(2,1)S(1)} collective-permute-done((bf16[1,2,256,256]{3,2,1,0:T(8,128)(2,1)S(1)}, bf16[1,2,256,256]{3,2,1,0:T(8,128)(2,1)S(1)}, u32[]{:S(2)}, u32[]{:S(2)}) %collective-permute-start.23) | collective-permute-done | bytes 262176 | tf_op jit(solution)/shard_map/ppermute | solution.py:21
  107.8 2.4 %collective-permute-start.32 = (bf16[1,1,256,256]{3,2,1,0:T(8,128)(2,1)S(1)}, bf16[1,1,256,256]{3,2,1,0:T(8,128)(2,1)S(1)}, u32[]{:S(2)}, u32[]{:S(2)}) collective-permute-start(bf16[1,1,256,256]{3,2,1,0:T(8,128)(2,1)S(1)} %slice.35), channel_id=1, source_target_pairs={{0,16},{2,18},{4,20},{6,22},{8,24},{10,26},{12,28},{14,30},{16,0},... | collective-permute-start | bytes 393224 | tf_op jit(solution)/shard_map/ppermute | solution.py:21
  110.4 10.5 %collective-permute-done.32 = bf16[1,1,256,256]{3,2,1,0:T(8,128)(2,1)S(1)} collective-permute-done((bf16[1,1,256,256]{3,2,1,0:T(8,128)(2,1)S(1)}, bf16[1,1,256,256]{3,2,1,0:T(8,128)(2,1)S(1)}, u32[]{:S(2)}, u32[]{:S(2)}) %collective-permute-start.32) | collective-permute-done | bytes 131104 | tf_op jit(solution)/shard_map/ppermute | solution.py:21
  120.9 3.4 %collective-permute-start.33 = (bf16[1,1,256,256]{3,2,1,0:T(8,128)(2,1)S(1)}, bf16[1,1,256,256]{3,2,1,0:T(8,128)(2,1)S(1)}, u32[]{:S(2)}, u32[]{:S(2)}) collective-permute-start(bf16[1,1,256,256]{3,2,1,0:T(8,128)(2,1)S(1)} %fusion.1), channel_id=1, source_target_pairs={{0,16},{2,18},{4,20},{6,22},{8,24},{10,26},{12,28},{14,30},{16,0},... | collective-permute-start | bytes 393224 | tf_op jit(solution)/shard_map/ppermute | solution.py:21
  124.5 2.8 %collective-permute-done.33 = bf16[1,1,256,256]{3,2,1,0:T(8,128)(2,1)S(1)} collective-permute-done((bf16[1,1,256,256]{3,2,1,0:T(8,128)(2,1)S(1)}, bf16[1,1,256,256]{3,2,1,0:T(8,128)(2,1)S(1)}, u32[]{:S(2)}, u32[]{:S(2)}) %collective-permute-start.33) | collective-permute-done | bytes 131104 | tf_op jit(solution)/shard_map/ppermute | solution.py:21
  127.3 3.8 %collective-permute-start.34 = (bf16[2,1,256,256]{3,2,1,0:T(8,128)(2,1)S(1)}, bf16[2,1,256,256]{3,2,1,0:T(8,128)(2,1)S(1)}, u32[]{:S(2)}, u32[]{:S(2)}) collective-permute-start(bf16[2,1,256,256]{3,2,1,0:T(8,128)(2,1)S(1)} %pad_maximum_fusion.3), channel_id=1, source_target_pairs={{0,8},{2,10},{4,12},{6,14},{8,0},{10,2},{12,4},{14,6},{16,24},{18,... | collective-permute-start | bytes 786440 | tf_op jit(solution)/shard_map/ppermute | solution.py:21
  131.3 7.0 %collective-permute-done.34 = bf16[2,1,256,256]{3,2,1,0:T(8,128)(2,1)S(1)} collective-permute-done((bf16[2,1,256,256]{3,2,1,0:T(8,128)(2,1)S(1)}, bf16[2,1,256,256]{3,2,1,0:T(8,128)(2,1)S(1)}, u32[]{:S(2)}, u32[]{:S(2)}) %collective-permute-start.34) | collective-permute-done | bytes 262176 | tf_op jit(solution)/shard_map/ppermute | solution.py:21
  138.5 4.7 %collective-permute-done.9 = bf16[160,1024]{1,0:T(8,128)(2,1)S(1)} collective-permute-done((bf16[160,1024]{1,0:T(8,128)(2,1)S(1)}, bf16[160,1024]{1,0:T(8,128)(2,1)S(1)}, u32[]{:S(2)}, u32[]{:S(2)}) %collective-permute-start.9) | collective-permute-done | bytes 327712 | tf_op jit(solution)/shard_map/ppermute | solution.py:21
  143.3 0.7 collective-permute-start.10
  143.9 6.7 %collective-permute-done.26.refs_2_ = bf16[4,2,256,256]{3,2,1,0:T(8,128)(2,1)S(1)} collective-permute-done((bf16[4,2,256,256]{3,2,1,0:T(8,128)(2,1)S(1)}, bf16[4,2,256,256]{3,2,1,0:T(8,128)(2,1)S(1)}, u32[]{:S(2)}, u32[]{:S(2)}) %collective-permute-start.26) | collective-permute-done | bytes 1048608 | tf_op jit(solution)/shard_map/ppermute | solution.py:21
  151.1 7.1 %collective-permute-done.10 = bf16[160,1024]{1,0:T(8,128)(2,1)S(1)} collective-permute-done((bf16[160,1024]{1,0:T(8,128)(2,1)S(1)}, bf16[160,1024]{1,0:T(8,128)(2,1)S(1)}, u32[]{:S(2)}, u32[]{:S(2)}) %collective-permute-start.10) | collective-permute-done | bytes 327712 | tf_op jit(solution)/shard_map/ppermute | solution.py:21
  158.8 1.0 unpack.1
  159.8 5.1 %collective-permute-done.6.refs_0_ = bf16[128,2048]{1,0:T(8,128)(2,1)S(1)} collective-permute-done((bf16[128,2048]{1,0:T(8,128)(2,1)S(1)}, bf16[128,2048]{1,0:T(8,128)(2,1)S(1)}, u32[]{:S(2)}, u32[]{:S(2)}) %collective-permute-start.6) | collective-permute-done | bytes 524320 | tf_op jit(solution)/shard_map/ppermute | solution.py:21
  165.5 1.4 own_rows.1
  166.8 1.7 collective-permute-done.11
  169.1 2.7 %join_x.1 = f32[1024,1024]{1,0:T(8,128)} custom-call(s32[1]{0:T(128)} %bitcast.dev, bf16[4,1,256,256]{3,2,1,0:T(8,128)(2,1)S(1)} %pad_maximum_fusion.2.refs_0_, bf16[4,1,256,256]{3,2,1,0:T(8,128)(2,1)S(1)} %collective-permute-done.35.refs_1_, bf16[4,1,256,256]{3,2,1,0:T(8,128)(2,1)S(1)} %collective-permute-done.36.refs_2_, ...), custom_call_target="tpu_custom_call" | custom-call | flops 4400000000 | bytes 6291456 | tf_op jit(solution)/shard_map/join_x/pallas_call | solution.py:90
  171.9 3.9 %join_pair.1 = (f32[1024,1024]{1,0:T(8,128)}, f32[1024,1024]{1,0:T(8,128)}) custom-call(s32[1]{0:T(128)} %bitcast.dev, bf16[4,2,256,256]{3,2,1,0:T(8,128)(2,1)S(1)} %pad_maximum_fusion.refs_0_, bf16[4,2,256,256]{3,2,1,0:T(8,128)(2,1)S(1)} %collective-permute-done.25.refs_1_, bf16[4,2,256,256]{3,2,1,0:T(8,128)(2,1)S(1)} %collective-permute-done.26.refs_2_, ...), custom_call_target="tpu_custom_call" | custom-call | flops 6600000000 | bytes 12582912 | tf_op jit(solution)/shard_map/join_pair/pallas_call | solution.py:90
  (102 shorter events, 9.4 us)
Async XLA Ops:
  0.6 15.2 %collective-permute-start.1 = (bf16[128,1024]{1,0:T(8,128)(2,1)}, bf16[128,1024]{1,0:T(8,128)(2,1)S(1)}, u32[]{:S(2)}, u32[]{:S(2)}) collective-permute-start(bf16[128,1024]{1,0:T(8,128)(2,1)} %hid.1), channel_id=1, source_target_pairs={{0,1},{1,0},{2,3},{3,2},{4,5},{5,4},{6,7},{7,6},{8,9},{9,8},{10,11... | collective-permute-start | bytes 786440 | tf_op jit(solution)/shard_map/ppermute | solution.py:21
  3.7 22.2 %collective-permute-start.3 = (bf16[128,1024]{1,0:T(8,128)(2,1)}, bf16[128,1024]{1,0:T(8,128)(2,1)S(1)}, u32[]{:S(2)}, u32[]{:S(2)}) collective-permute-start(bf16[128,1024]{1,0:T(8,128)(2,1)} %cot.1), channel_id=1, source_target_pairs={{0,1},{1,0},{2,3},{3,2},{4,5},{5,4},{6,7},{7,6},{8,9},{9,8},{10,11... | collective-permute-start | bytes 786440 | tf_op jit(solution)/shard_map/ppermute | solution.py:21
  3.8 12.1 %collective-permute-start = (f32[1,512]{1,0:T(1,128)}, f32[1,512]{1,0:T(1,128)S(1)}, u32[]{:S(2)}, u32[]{:S(2)}) collective-permute-start(f32[1,512]{1,0:T(1,128)} %refs_0_.2), channel_id=1, source_target_pairs={{0,1},{1,0},{2,3},{3,2},{4,5},{5,4},{6,7},{7,6},{8,9},{9,8},{10,11... | collective-permute-start | bytes 6152 | tf_op jit(solution)/shard_map/ppermute | solution.py:21
  21.8 4.0 %copy-start.7 = (bf16[128,1024]{1,0:T(8,128)(2,1)S(1)}, bf16[128,1024]{1,0:T(8,128)(2,1)}, u32[]{:S(2)}) copy-start(bf16[128,1024]{1,0:T(8,128)(2,1)} %cot.1) | copy-start | bytes 786436
  21.8 4.0 %copy-start.8 = (bf16[1,1024,16]{1,2,0:T(8,128)(2,1)S(1)}, bf16[1,1024,16]{1,2,0:T(8,128)(2,1)}, u32[]{:S(2)}) copy-start(bf16[1,1024,16]{1,2,0:T(8,128)(2,1)} %param.25) | copy-start | bytes 98308
  21.8 4.0 %copy-start.9 = (f32[1,4,1024]{2,1,0:T(4,128)S(1)}, f32[1,4,1024]{2,1,0:T(4,128)}, u32[]{:S(2)}) copy-start(f32[1,4,1024]{2,1,0:T(4,128)} %param.26) | copy-start | bytes 49156
  21.9 4.0 %copy-start.10 = (f32[1,1024]{1,0:T(1,128)S(1)}, f32[1,1024]{1,0:T(1,128)}, u32[]{:S(2)}) copy-start(f32[1,1024]{1,0:T(1,128)} %bx.1) | copy-start | bytes 12292
  21.9 4.0 %copy-start.19 = (f32[1,16]{1,0:T(1,128)S(1)}, f32[1,16]{1,0:T(1,128)}, u32[]{:S(2)}) copy-start(f32[1,16]{1,0:T(1,128)} %dtb.1) | copy-start | bytes 196
  21.9 4.0 %copy-start.20 = (f32[1,16]{1,0:T(1,128)S(1)}, f32[1,16]{1,0:T(1,128)}, u32[]{:S(2)}) copy-start(f32[1,16]{1,0:T(1,128)} %alog.1) | copy-start | bytes 196
  22.6 8.0 %collective-permute-start.2 = (bf16[256,128]{1,0:T(8,128)(2,1)S(1)}, bf16[256,128]{1,0:T(8,128)(2,1)S(1)}, u32[]{:S(2)}, u32[]{:S(2)}) collective-permute-start(bf16[256,128]{1,0:T(8,128)(2,1)S(1)} %get-tuple-element.89), channel_id=1, source_target_pairs={{0,1},{1,0},{2,3},{3,2},{4,5},{5,4},{6,7},{7,6},{8,9},{9,8},{10,11... | collective-permute-start | bytes 196616 | tf_op jit(solution)/shard_map/ppermute | solution.py:21
  24.4 26.1 %collective-permute-start.19 = (bf16[256,1024]{1,0:T(8,128)(2,1)S(1)}, bf16[256,1024]{1,0:T(8,128)(2,1)S(1)}, u32[]{:S(2)}, u32[]{:S(2)}) collective-permute-start(bf16[256,1024]{1,0:T(8,128)(2,1)S(1)} %get-tuple-element.91.n_r.refs_8_.refs_4_), channel_id=1, source_target_pairs={{0,4},{2,6},{4,0},{6,2},{8,12},{10,14},{12,8},{14,10},{16,20},{18,... | collective-permute-start | bytes 1572872 | tf_op jit(solution)/shard_map/ppermute | solution.py:21
  25.9 4.7 %copy-start.11 = (f32[1,1024]{1,0:T(1,128)S(1)}, f32[1,1024]{1,0:T(1,128)}, u32[]{:S(2)}) copy-start(f32[1,1024]{1,0:T(1,128)} %gg.3) | copy-start | bytes 12292
  30.0 20.5 %collective-permute-start.16 = (bf16[256,1024]{1,0:T(8,128)(2,1)S(1)}, bf16[256,1024]{1,0:T(8,128)(2,1)S(1)}, u32[]{:S(2)}, u32[]{:S(2)}) collective-permute-start(bf16[256,1024]{1,0:T(8,128)(2,1)S(1)} %get-tuple-element.137.refs_4_), channel_id=1, source_target_pairs={{0,4},{2,6},{4,0},{6,2},{8,12},{10,14},{12,8},{14,10},{16,20},{18,... | collective-permute-start | bytes 1572872 | tf_op jit(solution)/shard_map/ppermute | solution.py:21
  34.0 3.7 %collective-permute-start.4 = (f32[8,256]{1,0:T(8,128)S(1)}, f32[8,256]{1,0:T(8,128)S(1)}, u32[]{:S(2)}, u32[]{:S(2)}) collective-permute-start(f32[8,256]{1,0:T(8,128)S(1)} %get-tuple-element.101), channel_id=1, source_target_pairs={{0,1},{1,0},{2,3},{3,2},{4,5},{5,4},{6,7},{7,6},{8,9},{9,8},{10,11... | collective-permute-start | bytes 24584 | tf_op jit(solution)/shard_map/ppermute | solution.py:21
  39.3 2.0 %collective-permute-start.12 = (bf16[256,512]{1,0:T(8,128)(2,1)S(1)}, bf16[256,512]{1,0:T(8,128)(2,1)S(1)}, u32[]{:S(2)}, u32[]{:S(2)}) collective-permute-start(bf16[256,512]{1,0:T(8,128)(2,1)S(1)} %get-tuple-element.134), channel_id=1, source_target_pairs={{0,2},{2,0},{4,6},{6,4},{8,10},{10,8},{12,14},{14,12},{16,18},{18,... | collective-permute-start | bytes 786440 | tf_op jit(solution)/shard_map/ppermute | solution.py:21
  39.4 22.9 %collective-permute-start.15 = (bf16[256,1024]{1,0:T(8,128)(2,1)S(1)}, bf16[256,1024]{1,0:T(8,128)(2,1)S(1)}, u32[]{:S(2)}, u32[]{:S(2)}) collective-permute-start(bf16[256,1024]{1,0:T(8,128)(2,1)S(1)} %get-tuple-element.137.refs_4_), channel_id=1, source_target_pairs={{0,2},{2,0},{4,6},{6,4},{8,10},{10,8},{12,14},{14,12},{16,18},{18,... | collective-permute-start | bytes 1572872 | tf_op jit(solution)/shard_map/ppermute | solution.py:21
  39.9 13.9 %collective-permute-start.13 = (bf16[256,512]{1,0:T(8,128)(2,1)S(1)}, bf16[256,512]{1,0:T(8,128)(2,1)S(1)}, u32[]{:S(2)}, u32[]{:S(2)}) collective-permute-start(bf16[256,512]{1,0:T(8,128)(2,1)S(1)} %get-tuple-element.135), channel_id=1, source_target_pairs={{0,4},{2,6},{4,0},{6,2},{8,12},{10,14},{12,8},{14,10},{16,20},{18,... | collective-permute-start | bytes 786440 | tf_op jit(solution)/shard_map/ppermute | solution.py:21
  41.3 21.0 %collective-permute-start.18 = (bf16[256,1024]{1,0:T(8,128)(2,1)S(1)}, bf16[256,1024]{1,0:T(8,128)(2,1)S(1)}, u32[]{:S(2)}, u32[]{:S(2)}) collective-permute-start(bf16[256,1024]{1,0:T(8,128)(2,1)S(1)} %get-tuple-element.91.n_r.refs_8_.refs_4_), channel_id=1, source_target_pairs={{0,2},{2,0},{4,6},{6,4},{8,10},{10,8},{12,14},{14,12},{16,18},{18,... | collective-permute-start | bytes 1572872 | tf_op jit(solution)/shard_map/ppermute | solution.py:21
  50.5 11.8 %collective-permute-start.17 = (bf16[256,1024]{1,0:T(8,128)(2,1)S(1)}, bf16[256,1024]{1,0:T(8,128)(2,1)S(1)}, u32[]{:S(2)}, u32[]{:S(2)}) collective-permute-start(bf16[256,1024]{1,0:T(8,128)(2,1)S(1)} %collective-permute-done.16.refs_6_), channel_id=1, source_target_pairs={{0,2},{2,0},{4,6},{6,4},{8,10},{10,8},{12,14},{14,12},{16,18},{18,... | collective-permute-start | bytes 1572872 | tf_op jit(solution)/shard_map/ppermute | solution.py:21
  50.5 11.8 %collective-permute-start.20 = (bf16[256,1024]{1,0:T(8,128)(2,1)S(1)}, bf16[256,1024]{1,0:T(8,128)(2,1)S(1)}, u32[]{:S(2)}, u32[]{:S(2)}) collective-permute-start(bf16[256,1024]{1,0:T(8,128)(2,1)S(1)} %collective-permute-done.19.refs_10_.refs_6_), channel_id=1, source_target_pairs={{0,2},{2,0},{4,6},{6,4},{8,10},{10,8},{12,14},{14,12},{16,18},{18,... | collective-permute-start | bytes 1572872 | tf_op jit(solution)/shard_map/ppermute | solution.py:21
  53.7 8.6 %collective-permute-start.14 = (bf16[256,512]{1,0:T(8,128)(2,1)S(1)}, bf16[256,512]{1,0:T(8,128)(2,1)S(1)}, u32[]{:S(2)}, u32[]{:S(2)}) collective-permute-start(bf16[256,512]{1,0:T(8,128)(2,1)S(1)} %get-tuple-element.136), channel_id=1, source_target_pairs={{0,6},{2,4},{4,2},{6,0},{8,14},{10,12},{12,10},{14,8},{16,22},{18,... | collective-permute-start | bytes 786440 | tf_op jit(solution)/shard_map/ppermute | solution.py:21
  65.4 14.0 %collective-permute-start.21 = (bf16[2,2,256,256]{3,2,1,0:T(8,128)(2,1)S(1)}, bf16[2,2,256,256]{3,2,1,0:T(8,128)(2,1)S(1)}, u32[]{:S(2)}, u32[]{:S(2)}) collective-permute-start(bf16[2,2,256,256]{3,2,1,0:T(8,128)(2,1)S(1)} %get-tuple-element.139), channel_id=1, source_target_pairs={{0,8},{2,10},{4,12},{6,14},{8,0},{10,2},{12,4},{14,6},{16,24},{18,... | collective-permute-start | bytes 1572872 | tf_op jit(solution)/shard_map/ppermute | solution.py:21
  74.3 19.6 %collective-permute-start.5 = (bf16[256,128]{1,0:T(8,128)(2,1)S(1)}, bf16[256,128]{1,0:T(8,128)(2,1)S(1)}, u32[]{:S(2)}, u32[]{:S(2)}) collective-permute-start(bf16[256,128]{1,0:T(8,128)(2,1)S(1)} %get-tuple-element.123), channel_id=1, source_target_pairs={{0,1},{1,0},{2,3},{3,2},{4,5},{5,4},{6,7},{7,6},{8,9},{9,8},{10,11... | collective-permute-start | bytes 196616 | tf_op jit(solution)/shard_map/ppermute | solution.py:21
  74.9 10.5 %collective-permute-start.28 = (bf16[256,256]{1,0:T(8,128)(2,1)S(1)}, bf16[256,256]{1,0:T(8,128)(2,1)S(1)}, u32[]{:S(2)}, u32[]{:S(2)}) collective-permute-start(bf16[256,256]{1,0:T(8,128)(2,1)S(1)} %get-tuple-element.142), channel_id=1, source_target_pairs={{0,2},{2,0},{4,6},{6,4},{8,10},{10,8},{12,14},{14,12},{16,18},{18,... | collective-permute-start | bytes 393224 | tf_op jit(solution)/shard_map/ppermute | solution.py:21
  74.9 10.5 %collective-permute-start.29 = (bf16[256,256]{1,0:T(8,128)(2,1)S(1)}, bf16[256,256]{1,0:T(8,128)(2,1)S(1)}, u32[]{:S(2)}, u32[]{:S(2)}) collective-permute-start(bf16[256,256]{1,0:T(8,128)(2,1)S(1)} %get-tuple-element.143), channel_id=1, source_target_pairs={{0,4},{2,6},{4,0},{6,2},{8,12},{10,14},{12,8},{14,10},{16,20},{18,... | collective-permute-start | bytes 393224 | tf_op jit(solution)/shard_map/ppermute | solution.py:21
  75.5 9.9 %collective-permute-start.30 = (bf16[256,256]{1,0:T(8,128)(2,1)S(1)}, bf16[256,256]{1,0:T(8,128)(2,1)S(1)}, u32[]{:S(2)}, u32[]{:S(2)}) collective-permute-start(bf16[256,256]{1,0:T(8,128)(2,1)S(1)} %get-tuple-element.144), channel_id=1, source_target_pairs={{0,6},{2,4},{4,2},{6,0},{8,14},{10,12},{12,10},{14,8},{16,22},{18,... | collective-permute-start | bytes 393224 | tf_op jit(solution)/shard_map/ppermute | solution.py:21
  79.6 14.2 %collective-permute-start.22 = (bf16[1,2,256,256]{3,2,1,0:T(8,128)(2,1)S(1)}, bf16[1,2,256,256]{3,2,1,0:T(8,128)(2,1)S(1)}, u32[]{:S(2)}, u32[]{:S(2)}) collective-permute-start(bf16[1,2,256,256]{3,2,1,0:T(8,128)(2,1)S(1)} %slice.34), channel_id=1, source_target_pairs={{0,16},{2,18},{4,20},{6,22},{8,24},{10,26},{12,28},{14,30},{16,0},... | collective-permute-start | bytes 786440 | tf_op jit(solution)/shard_map/ppermute | solution.py:21
  85.4 8.5 %copy-start.4 = (bf16[1,1024,128]{2,1,0:T(8,128)(2,1)S(1)}, bf16[1,1024,128]{2,1,0:T(8,128)(2,1)}, u32[]{:S(2)}) copy-start(bf16[1,1024,128]{2,1,0:T(8,128)(2,1)} %param.24) | copy-start | bytes 786436
  85.4 8.5 %copy-start.6 = (bf16[128,1024]{1,0:T(8,128)(2,1)S(1)}, bf16[128,1024]{1,0:T(8,128)(2,1)}, u32[]{:S(2)}) copy-start(bf16[128,1024]{1,0:T(8,128)(2,1)} %hid.1) | copy-start | bytes 786436
  85.4 8.5 %copy-start.14 = (f32[1,4,128]{2,1,0:T(4,128)S(1)}, f32[1,4,128]{2,1,0:T(4,128)}, u32[]{:S(2)}) copy-start(f32[1,4,128]{2,1,0:T(4,128)} %param.27) | copy-start | bytes 6148
  87.5 20.2 %collective-permute-start.31 = (bf16[2,1,256,256]{3,2,1,0:T(8,128)(2,1)S(1)}, bf16[2,1,256,256]{3,2,1,0:T(8,128)(2,1)S(1)}, u32[]{:S(2)}, u32[]{:S(2)}) collective-permute-start(bf16[2,1,256,256]{3,2,1,0:T(8,128)(2,1)S(1)} %get-tuple-element.146), channel_id=1, source_target_pairs={{0,8},{2,10},{4,12},{6,14},{8,0},{10,2},{12,4},{14,6},{16,24},{18,... | collective-permute-start | bytes 786440 | tf_op jit(solution)/shard_map/ppermute | solution.py:21
  93.9 13.7 %collective-permute-start.23 = (bf16[1,2,256,256]{3,2,1,0:T(8,128)(2,1)S(1)}, bf16[1,2,256,256]{3,2,1,0:T(8,128)(2,1)S(1)}, u32[]{:S(2)}, u32[]{:S(2)}) collective-permute-start(bf16[1,2,256,256]{3,2,1,0:T(8,128)(2,1)S(1)} %fusion), channel_id=1, source_target_pairs={{0,16},{2,18},{4,20},{6,22},{8,24},{10,26},{12,28},{14,30},{16,0},... | collective-permute-start | bytes 786440 | tf_op jit(solution)/shard_map/ppermute | solution.py:21
  95.1 15.1 %collective-permute-start.7 = (bf16[160,1024]{1,0:T(8,128)(2,1)S(1)}, bf16[160,1024]{1,0:T(8,128)(2,1)S(1)}, u32[]{:S(2)}, u32[]{:S(2)}) collective-permute-start(bf16[160,1024]{1,0:T(8,128)(2,1)S(1)} %convert_element_type.56), channel_id=1, source_target_pairs={{0,2},{2,0},{4,6},{6,4},{8,10},{10,8},{12,14},{14,12},{16,18},{18,... | collective-permute-start | bytes 983048 | tf_op jit(solution)/shard_map/ppermute | solution.py:21
  107.6 16.7 %collective-permute-start.24 = (bf16[2,2,256,256]{3,2,1,0:T(8,128)(2,1)S(1)}, bf16[2,2,256,256]{3,2,1,0:T(8,128)(2,1)S(1)}, u32[]{:S(2)}, u32[]{:S(2)}) collective-permute-start(bf16[2,2,256,256]{3,2,1,0:T(8,128)(2,1)S(1)} %pad_maximum_fusion.1), channel_id=1, source_target_pairs={{0,8},{2,10},{4,12},{6,14},{8,0},{10,2},{12,4},{14,6},{16,24},{18,... | collective-permute-start | bytes 1572872 | tf_op jit(solution)/shard_map/ppermute | solution.py:21
  107.8 13.0 %collective-permute-start.32 = (bf16[1,1,256,256]{3,2,1,0:T(8,128)(2,1)S(1)}, bf16[1,1,256,256]{3,2,1,0:T(8,128)(2,1)S(1)}, u32[]{:S(2)}, u32[]{:S(2)}) collective-permute-start(bf16[1,1,256,256]{3,2,1,0:T(8,128)(2,1)S(1)} %slice.35), channel_id=1, source_target_pairs={{0,16},{2,18},{4,20},{6,22},{8,24},{10,26},{12,28},{14,30},{16,0},... | collective-permute-start | bytes 393224 | tf_op jit(solution)/shard_map/ppermute | solution.py:21
  110.3 20.8 %collective-permute-start.8 = (bf16[160,1024]{1,0:T(8,128)(2,1)S(1)}, bf16[160,1024]{1,0:T(8,128)(2,1)S(1)}, u32[]{:S(2)}, u32[]{:S(2)}) collective-permute-start(bf16[160,1024]{1,0:T(8,128)(2,1)S(1)} %add_convert_fusion.2), channel_id=1, source_target_pairs={{0,4},{2,6},{4,0},{6,2},{8,12},{10,14},{12,8},{14,10},{16,20},{18,... | collective-permute-start | bytes 983048 | tf_op jit(solution)/shard_map/ppermute | solution.py:21
  120.9 6.4 %collective-permute-start.33 = (bf16[1,1,256,256]{3,2,1,0:T(8,128)(2,1)S(1)}, bf16[1,1,256,256]{3,2,1,0:T(8,128)(2,1)S(1)}, u32[]{:S(2)}, u32[]{:S(2)}) collective-permute-start(bf16[1,1,256,256]{3,2,1,0:T(8,128)(2,1)S(1)} %fusion.1), channel_id=1, source_target_pairs={{0,16},{2,18},{4,20},{6,22},{8,24},{10,26},{12,28},{14,30},{16,0},... | collective-permute-start | bytes 393224 | tf_op jit(solution)/shard_map/ppermute | solution.py:21
  124.4 26.2 %collective-permute-start.26 = (bf16[4,2,256,256]{3,2,1,0:T(8,128)(2,1)S(1)}, bf16[4,2,256,256]{3,2,1,0:T(8,128)(2,1)S(1)}, u32[]{:S(2)}, u32[]{:S(2)}) collective-permute-start(bf16[4,2,256,256]{3,2,1,0:T(8,128)(2,1)S(1)} %pad_maximum_fusion.refs_0_), channel_id=1, source_target_pairs={{0,4},{2,6},{4,0},{6,2},{8,12},{10,14},{12,8},{14,10},{16,20},{18,... | collective-permute-start | bytes 3145736 | tf_op jit(solution)/shard_map/ppermute | solution.py:21
  127.3 11.0 %collective-permute-start.34 = (bf16[2,1,256,256]{3,2,1,0:T(8,128)(2,1)S(1)}, bf16[2,1,256,256]{3,2,1,0:T(8,128)(2,1)S(1)}, u32[]{:S(2)}, u32[]{:S(2)}) collective-permute-start(bf16[2,1,256,256]{3,2,1,0:T(8,128)(2,1)S(1)} %pad_maximum_fusion.3), channel_id=1, source_target_pairs={{0,8},{2,10},{4,12},{6,14},{8,0},{10,2},{12,4},{14,6},{16,24},{18,... | collective-permute-start | bytes 786440 | tf_op jit(solution)/shard_map/ppermute | solution.py:21
  131.2 11.9 %collective-permute-start.9 = (bf16[160,1024]{1,0:T(8,128)(2,1)S(1)}, bf16[160,1024]{1,0:T(8,128)(2,1)S(1)}, u32[]{:S(2)}, u32[]{:S(2)}) collective-permute-start(bf16[160,1024]{1,0:T(8,128)(2,1)S(1)} %add_convert_fusion.1), channel_id=1, source_target_pairs={{0,8},{2,10},{4,12},{6,14},{8,0},{10,2},{12,4},{14,6},{16,24},{18,... | collective-permute-start | bytes 983048 | tf_op jit(solution)/shard_map/ppermute | solution.py:21
  138.4 19.9 %collective-permute-start.36 = (bf16[4,1,256,256]{3,2,1,0:T(8,128)(2,1)S(1)}, bf16[4,1,256,256]{3,2,1,0:T(8,128)(2,1)S(1)}, u32[]{:S(2)}, u32[]{:S(2)}) collective-permute-start(bf16[4,1,256,256]{3,2,1,0:T(8,128)(2,1)S(1)} %pad_maximum_fusion.2.refs_0_), channel_id=1, source_target_pairs={{0,4},{2,6},{4,0},{6,2},{8,12},{10,14},{12,8},{14,10},{16,20},{18,... | collective-permute-start | bytes 1572872 | tf_op jit(solution)/shard_map/ppermute | solution.py:21
  143.3 14.9 %collective-permute-start.10 = (bf16[160,1024]{1,0:T(8,128)(2,1)S(1)}, bf16[160,1024]{1,0:T(8,128)(2,1)S(1)}, u32[]{:S(2)}, u32[]{:S(2)}) collective-permute-start(bf16[160,1024]{1,0:T(8,128)(2,1)S(1)} %add_convert_fusion), channel_id=1, source_target_pairs={{0,16},{2,18},{4,20},{6,22},{8,24},{10,26},{12,28},{14,30},{16,0},... | collective-permute-start | bytes 983048 | tf_op jit(solution)/shard_map/ppermute | solution.py:21
  143.9 27.9 %collective-permute-start.25 = (bf16[4,2,256,256]{3,2,1,0:T(8,128)(2,1)S(1)}, bf16[4,2,256,256]{3,2,1,0:T(8,128)(2,1)S(1)}, u32[]{:S(2)}, u32[]{:S(2)}) collective-permute-start(bf16[4,2,256,256]{3,2,1,0:T(8,128)(2,1)S(1)} %pad_maximum_fusion.refs_0_), channel_id=1, source_target_pairs={{0,2},{2,0},{4,6},{6,4},{8,10},{10,8},{12,14},{14,12},{16,18},{18,... | collective-permute-start | bytes 3145736 | tf_op jit(solution)/shard_map/ppermute | solution.py:21
  150.6 21.3 %collective-permute-start.27 = (bf16[4,2,256,256]{3,2,1,0:T(8,128)(2,1)S(1)}, bf16[4,2,256,256]{3,2,1,0:T(8,128)(2,1)S(1)}, u32[]{:S(2)}, u32[]{:S(2)}) collective-permute-start(bf16[4,2,256,256]{3,2,1,0:T(8,128)(2,1)S(1)} %collective-permute-done.26.refs_2_), channel_id=1, source_target_pairs={{0,2},{2,0},{4,6},{6,4},{8,10},{10,8},{12,14},{14,12},{16,18},{18,... | collective-permute-start | bytes 3145736 | tf_op jit(solution)/shard_map/ppermute | solution.py:21
  150.6 14.3 %collective-permute-start.6 = (bf16[128,2048]{1,0:T(8,128)(2,1)S(1)}, bf16[128,2048]{1,0:T(8,128)(2,1)S(1)}, u32[]{:S(2)}, u32[]{:S(2)}) collective-permute-start(bf16[128,2048]{1,0:T(8,128)(2,1)S(1)} %get-tuple-element.127), channel_id=1, source_target_pairs={{0,1},{1,0},{2,3},{3,2},{4,5},{5,4},{6,7},{7,6},{8,9},{9,8},{10,11... | collective-permute-start | bytes 1572872 | tf_op jit(solution)/shard_map/ppermute | solution.py:21
  158.2 10.9 %collective-permute-start.35 = (bf16[4,1,256,256]{3,2,1,0:T(8,128)(2,1)S(1)}, bf16[4,1,256,256]{3,2,1,0:T(8,128)(2,1)S(1)}, u32[]{:S(2)}, u32[]{:S(2)}) collective-permute-start(bf16[4,1,256,256]{3,2,1,0:T(8,128)(2,1)S(1)} %pad_maximum_fusion.2.refs_0_), channel_id=1, source_target_pairs={{0,2},{2,0},{4,6},{6,4},{8,10},{10,8},{12,14},{14,12},{16,18},{18,... | collective-permute-start | bytes 1572872 | tf_op jit(solution)/shard_map/ppermute | solution.py:21
  158.3 10.8 %collective-permute-start.37 = (bf16[4,1,256,256]{3,2,1,0:T(8,128)(2,1)S(1)}, bf16[4,1,256,256]{3,2,1,0:T(8,128)(2,1)S(1)}, u32[]{:S(2)}, u32[]{:S(2)}) collective-permute-start(bf16[4,1,256,256]{3,2,1,0:T(8,128)(2,1)S(1)} %collective-permute-done.36.refs_2_), channel_id=1, source_target_pairs={{0,2},{2,0},{4,6},{6,4},{8,10},{10,8},{12,14},{14,12},{16,18},{18,... | collective-permute-start | bytes 1572872 | tf_op jit(solution)/shard_map/ppermute | solution.py:21
  164.9 3.6 %collective-permute-start.11 = (f32[1,512]{1,0:T(1,128)S(1)}, f32[1,512]{1,0:T(1,128)S(1)}, u32[]{:S(2)}, u32[]{:S(2)}) collective-permute-start(f32[1,512]{1,0:T(1,128)S(1)} %get-tuple-element.132), channel_id=1, source_target_pairs={{0,1},{1,0},{2,3},{3,2},{4,5},{5,4},{6,7},{7,6},{8,9},{9,8},{10,11... | collective-permute-start | bytes 6152 | tf_op jit(solution)/shard_map/ppermute | solution.py:21
  (12 other events, 22.1 us)

commit v3 on v2

--- a/solution.py
+++ b/solution.py
@@ -13,7 +13,7 @@
 F32 = jnp.float32
 BF16 = jnp.bfloat16
 VM = 1.5
-UNIT = 1.1e9
+UNIT = 3e9
 
 
 def exchange(array, axis, bit):
@@ -76,7 +76,7 @@
     return (jax.ShapeDtypeStruct(shape, dtype), spec)
 
 
-def run(body, name, device, ins, outs, steps, scratch=(), us=1.0):
+def run(body, name, device, ins, outs, steps, scratch=(), us=1.0, pull=False):
     total = sum(a.size * a.dtype.itemsize for a, _ in ins)
     total += sum(s.size * s.dtype.itemsize for s, _ in outs)
     held = 0
@@ -87,6 +87,26 @@
         held += size * (1 if size == array.size * array.dtype.itemsize else 2)
     for buffer in scratch:
         held += buffer.dtype.itemsize * int(np.prod(buffer.shape))
+    if pull:
+        count, inner = len(ins), body
+        scratch = (
+            [pltpu.VMEM(a.shape, a.dtype) for a, _ in ins]
+            + [pltpu.SemaphoreType.DMA((count,))]
+            + list(scratch)
+        )
+        ins = [(a, pl.BlockSpec(memory_space=pltpu.HBM)) for a, _ in ins]
+
+        def body(dev, *refs):
+            held = refs[count + len(outs) :]
+            copies = [
+                pltpu.make_async_copy(refs[i], held[i], held[count].at[i]) for i in range(count)
+            ]
+            for copy in copies:
+                copy.start()
+            for copy in copies:
+                copy.wait()
+            inner(dev, *held[:count], *refs[count : count + len(outs)], *held[count + 1 :])
+
     return pl.pallas_call(
         body,
         name=name,
@@ -243,12 +263,7 @@
 
     blocks = [slice(b * T, (b + 1) * T) for b in range(S)]
 
-    if S == 2:
-        gains = [norm_gain, exchange(norm_gain, "shard", 1)]
-    else:
-        gains = [lax.all_gather(norm_gain, "shard", axis=1, tiled=True)]
     hidden = [hidden_in] + [exchange(hidden_in, "shard", j) for j in range(1, S)]
-    cots = [cotangent] + [exchange(cotangent, "shard", j) for j in range(1, S)]
 
     lens = seq_len.reshape(1, -1)
     owners = seq_owner.reshape(1, -1)
@@ -283,13 +298,80 @@
         lane = iota((1, width), 1) // HS
         return [jnp.where(lane == g, 1.0, 0.0) for g in range(group)]
 
-    def prepare(dev, ln, ow, st, wbc, tbc, bbc, *refs):
+    def segments(dev, ln, ow, st, hid, cot, *refs):
+        given, refs = refs[:4], refs[4:]
+        mask_r, cols_r, mine_r, cot_r = refs[:4]
+        for source, target in zip(given, refs[4:]):
+            target[...] = source[...]
+        mine_r[:, 0:D] = hid[...]
+        mine_r[:, D : 2 * D] = cot[...]
+        cot_r[...] = cot[...]
+        me = me_of(dev)
+        base = dev[0] - me
+        lane = iota((T, 128), 1)
+        row = iota((T, 128), 0)
+        slot = iota((T, records), 0)
+        ids = iota((T, records), 1).astype(F32)
+        for b in range(S):
+            covers = (
+                (ow[...] == base + (me ^ b)) & (slot >= st[...]) & (slot < st[...] + ln[...])
+            )
+            used = jnp.sum(jnp.where(covers, 1.0, 0.0), axis=1, keepdims=True)
+            found = jnp.sum(jnp.where(covers, ids, 0.0), axis=1, keepdims=True)
+            lone = (records + row).astype(F32)
+            seg = jnp.where(used > 0.5, found, lone)
+            same = (seg == seg.T) & (row >= lane)
+            mask_r[blocks[b], :] = jnp.where(same, 1.0, 0.0)
+            cols = jnp.where(lane == 0, used, 0.0)
+            for offset in range(1, 4):
+                mark = (pltpu.roll(seg, offset, 0) == seg) & (row >= offset)
+                cols = jnp.where(lane == offset, jnp.where(mark, 1.0, 0.0), cols)
+            cols_r[blocks[b], :] = cols
+
+    mask, cols, mine_rows, cot_own, own_gain, bc_weight, bc_taps, bc_bias = run(
+        segments,
+        "segments",
+        device,
+        [
+            whole(a)
+            for a in (
+                lens,
+                owners,
+                starts,
+                hidden_in,
+                cotangent,
+                norm_gain,
+                w_bc,
+                conv_bc,
+                bias_bc,
+            )
+        ],
+        [
+            out_whole((R, 128), F32),
+            out_whole((R, 128), F32),
+            out_whole((T, 2 * D), BF16),
+            out_whole((T, D), BF16),
+            out_whole(norm_gain.shape, F32),
+            out_whole(w_bc.shape, BF16),
+            out_whole(conv_bc.shape, F32),
+            out_whole(bias_bc.shape, F32),
+        ],
+        1,
+        us=1.5,
+        pull=True,
+    )
+    if S == 2:
+        gains = [own_gain, exchange(own_gain, "shard", 1)]
+    else:
+        gains = [lax.all_gather(own_gain, "shard", axis=1, tiled=True)]
+    far_rows = [exchange(mine_rows, "rep", 2)]
+
+    def prepare(dev, wbc, tbc, bbc, cols_r, cot, *refs):
         parts, refs = refs[: len(gains)], refs[len(gains) :]
         hid, refs = refs[:S], refs[S:]
-        gain_r, normed_r, mask_r, cols_r, pbc_r, pre_r, map_r = refs[:7]
-        sends = refs[7:]
+        gain_r, normed_r, pbc_r, pre_r, map_r, cot_r = refs[:6]
+        sends = refs[6:]
         me = me_of(dev)
-        base = dev[0] - me
         if S == 2:
             low, high = parts[0][...], parts[1][...]
             first = me == 0
@@ -298,29 +380,10 @@
             )
         else:
             gain_r[...] = parts[0][...]
-        lane = iota((T, 128), 1)
-        row = iota((T, 128), 0)
         for b in range(S):
             x = hid[b][...].astype(F32)
             scale = lax.rsqrt(jnp.mean(x * x, axis=1, keepdims=True) + epsilon)
             normed_r[blocks[b], :] = (x * scale * gain_r[...]).astype(BF16)
-            slot = iota((T, records), 0)
-            covers = (
-                (ow[...] == base + (me ^ b)) & (slot >= st[...]) & (slot < st[...] + ln[...])
-            )
-            ids = iota((T, records), 1).astype(F32)
-            used = jnp.sum(jnp.where(covers, 1.0, 0.0), axis=1, keepdims=True)
-            found = jnp.sum(jnp.where(covers, ids, 0.0), axis=1, keepdims=True)
-            lone = (records + row).astype(F32)
-            seg = jnp.where(used > 0.5, found, lone)
-            seg_t = seg.T
-            same = (seg == seg_t) & (row >= lane)
-            mask_r[blocks[b], :] = jnp.where(same, 1.0, 0.0)
-            cols = jnp.where(lane == 0, used, 0.0)
-            for offset in range(1, 4):
-                mark = (pltpu.roll(seg, offset, 0) == seg) & (row >= offset)
-                cols = jnp.where(lane == offset, jnp.where(mark, 1.0, 0.0), cols)
-            cols_r[blocks[b], :] = cols
         pbc_r[...] = mm(normed_r[...], wbc[...])
         for b in range(S):
             marks = cols_r[blocks[b], :]
@@ -330,40 +393,37 @@
             map_r[blocks[b], :] = out
             for j in range(1, S):
                 sends[j - 1][blocks[b ^ j], :] = out
+        cot_r[...] = cot[...]
 
     outs = run(
         prepare,
         "norm_and_maps",
         device,
-        [whole(a) for a in (lens, owners, starts, w_bc, conv_bc, bias_bc, *gains, *hidden)],
+        [whole(a) for a in (bc_weight, bc_taps, bc_bias, cols, cot_own, *gains, *hidden)],
         [
             out_whole((1, D), F32),
             out_whole((R, D), BF16),
-            out_whole((R, 128), F32),
-            out_whole((R, 128), F32),
             out_whole((R, NB), F32),
             out_whole((R, NB), F32),
             out_whole((R, NB), BF16),
+            out_whole((T, D), BF16),
         ]
         + [out_whole((R, NB), BF16) for _ in range(1, S)],
         1,
-        us=2.5,
-    )
-    gain, normed, mask, cols, proj_bc, pre_bc, map_own = outs[:7]
-    maps = [map_own] + [exchange(outs[6 + j], "shard", j) for j in range(1, S)]
+        us=1.0,
+    )
+    gain, normed, proj_bc, pre_bc, map_own, cot_own = outs[:6]
+    maps = [map_own] + [exchange(outs[5 + j], "shard", j) for j in range(1, S)]
     if S == 2:
         map_a, map_b = maps
     else:
         map_a = jnp.concatenate(maps[: S // 2], axis=1)
         map_b = jnp.concatenate(maps[S // 2 :], axis=1)
-
-    normed_far = exchange(normed, "rep", 2)
-    normed_all = [normed, exchange(normed, "rep", 1), normed_far, exchange(normed_far, "rep", 1)]
-
-    def project(dev, n_r, wz, wx, wdt, dtb, alog, dsk, tx, bx, cols_r, wo, *refs):
-        cot, refs = refs[:S], refs[S:]
-        z_r, x_r, pre_r, y_r, cum_r, cumt_r, hp_r, sk_r, dm_r, cg_r = refs[:10]
-        y_s, cum_s = refs[10:]
+    cots = [cot_own] + [exchange(cot_own, "shard", j) for j in range(1, S)]
+
+    def project(dev, n_r, wz, wx, wdt, dtb, alog, dsk, tx, bx, cols_r, *refs):
+        z_r, x_r, pre_r, y_r, cum_r, cumt_r, hp_r, sk_r = refs[:8]
+        y_s, cum_s = refs[8:]
         c = pl.program_id(0)
         n = n_r[...]
 
@@ -379,7 +439,6 @@
                     total = total + jnp.where(row >= shift, pltpu.roll(total, shift, 0), 0.0)
                     shift *= 2
                 cum_s[blocks[b], :] = total
-                cg_r[blocks[b], :] = cot[b][...]
 
         z_r[0] = mm(n, wz[...])
         x_r[0] = mm(n, wx[...])
@@ -393,13 +452,12 @@
         hp_r[0] = jnp.exp(pair)
         skips = [jnp.broadcast_to(pair[1:2, h : h + 1], (1, HS)) for h in range(HC)]
         sk_r[0] = jnp.broadcast_to(jnp.concatenate(skips, axis=1), (8, CH))
-        dm_r[0] = mm_rt(cg_r[...], wo[...]) * cols_r[:, 0:1]
         for b in range(S):
             marks = cols_r[blocks[b], :]
             pre_r[0, blocks[b], :] = conv_rows(x_r[0, blocks[b], :], tx[...], bx[...], marks)
             cumt_r[0, b] = turned[blocks[b]].T[0:8]
 
-    z, px, pre, y, cum, cum_t, head_rows, skip_rows, d_mixed, cot_group = run(
+    z, px, pre, y, cum, cum_t, head_rows, skip_rows = run(
         project,
         "projections",
         device,
@@ -414,9 +472,7 @@
             columns(conv_x, CH, chunk),
             columns(bias_x, CH, chunk),
             whole(cols),
-            rows(w_out, CH, chunk),
-        ]
-        + [whole(c) for c in cots],
+        ],
         [
             out_chunked((PARTS, R, CH), F32),
             out_chunked((PARTS, R, CH), F32),
@@ -426,25 +482,11 @@
             out_chunked((PARTS, S, 8, 128), F32),
             out_chunked((PARTS, 8, 128), F32),
             out_chunked((PARTS, 8, CH), F32),
-            out_chunked((PARTS, R, CH), F32),
-            out_whole((R, D), BF16),
         ],
         PARTS,
         scratch=[pltpu.VMEM((R, 128), F32), pltpu.VMEM((R, 128), F32)],
         us=4.0,
     )
-    cots_far = exchange(cot_group, "rep", 2)
-    cots_all = [
-        cot_group,
-        exchange(cot_group, "rep", 1),
-        cots_far,
-        exchange(cots_far, "rep", 1),
-    ]
-
-    def decays(cum_r, cumt_r, b, h):
-        gap = cum_r[0, blocks[b], h : h + 1] - cumt_r[0, b, h : h + 1, :]
-        return gap
-
     def fill_scores(dev, a_r, b_r, mask_r, scores):
         a_is_key = me_of(dev) < S // 2
         for b in range(S):
@@ -458,12 +500,11 @@
                 scores[b] = mm_rt(a_r[blocks[b], :], b_r[blocks[b], :]) * mask_r[blocks[b], :]
 
     def scan_forward(
-        dev, a_r, b_r, mask_r, pre_r, y_r, cum_r, cumt_r, sk, gg, z_r, dm_r, wo, *refs
+        dev, a_r, b_r, mask_r, pre_r, y_r, cum_r, cumt_r, sk, gg, z_r, wo, *refs
     ):
-        core_r, sums_r, own_r = refs[0], refs[1], refs[2]
-        sum_sends = refs[3 : 2 + S]
-        sends = refs[2 + S : 1 + 2 * S]
-        scores, acc, sums, gated_s = refs[1 + 2 * S :]
+        core_r, sums, own_r = refs[0], refs[1], refs[2]
+        sends = refs[3 : 2 + S]
+        scores, acc, gated_s = refs[2 + S :]
         c = pl.program_id(0)
 
         @pl.when(c == 0)
@@ -500,8 +541,7 @@
             gained = gated * gg[...]
             gated_s[blocks[b], :] = gained.astype(BF16)
             squares = jnp.sum(gated * gated, axis=1, keepdims=True)
-            dots = jnp.sum(dm_r[0, blocks[b], :] * gained, axis=1, keepdims=True)
-            sums[blocks[b], :] += jnp.where(lane == 0, squares, jnp.where(lane == 1, dots, 0.0))
+            sums[blocks[b], :] += jnp.where(lane == 0, squares, 0.0)
         acc[...] += mm(gated_s[...], wo[...])
 
         @pl.when(c == PARTS - 1)
@@ -509,11 +549,6 @@
             own_r[...] = acc[blocks[0], :]
             for j in range(1, S):
                 sends[j - 1][...] = acc[blocks[j], :].astype(BF16)
-            for b in range(S):
-                turned = sums[blocks[b], :].T[0:8]
-                sums_r[:, blocks[b]] = turned
-                for j in range(1, S):
-                    sum_sends[j - 1][:, blocks[b ^ j]] = turned
 
     outs = run(
         scan_forward,
@@ -530,28 +565,73 @@
             chunked(skip_rows),
             columns(gate_gain, CH, chunk),
             chunked(z),
-            chunked(d_mixed),
             rows(w_out, CH, chunk),
         ],
         [
             out_chunked((PARTS, R, CH), F32),
-            out_whole((8, R), F32),
+            out_whole((R, 128), F32),
             out_whole((T, D), F32),
         ]
-        + [out_whole((8, R), F32) for _ in range(1, S)]
         + [out_whole((T, D), BF16) for _ in range(1, S)],
         PARTS,
         scratch=[
             pltpu.VMEM((S, T, T), F32),
             pltpu.VMEM((R, D), F32),
-            pltpu.VMEM((R, 128), F32),
             pltpu.VMEM((R, CH), BF16),
         ],
         us=4.0,
     )
-    core, sums_own, out_own = outs[:3]
-    sums_all = [sums_own] + [exchange(outs[2 + j], "shard", j) for j in range(1, S)]
-    out_sends = [outs[1 + S + j] for j in range(1, S)]
+    core, squares, out_own = outs[:3]
+    out_sends = outs[3:]
+
+    def mixed_backward(dev, core_r, z_r, gg, cols_r, squares_r, wo, *refs):
+        cot, refs = refs[:S], refs[S:]
+        dm_r, sums_r = refs[0], refs[1]
+        sends, sums = refs[2 : 1 + S], refs[1 + S]
+        c = pl.program_id(0)
+        lane = iota((T, 128), 1)
+
+        @pl.when(c == 0)
+        def _():
+            sums[...] = squares_r[...]
+
+        for b in range(S):
+            d_mixed = mm_rt(cot[b][...], wo[...]) * cols_r[blocks[b], 0:1]
+            dm_r[0, blocks[b], :] = d_mixed
+            zed = z_r[0, blocks[b], :]
+            gated = core_r[0, blocks[b], :] * (zed * jax.nn.sigmoid(zed))
+            dots = jnp.sum(d_mixed * (gated * gg[...]), axis=1, keepdims=True)
+            sums[blocks[b], :] += jnp.where(lane == 1, dots, 0.0)
+
+        @pl.when(c == PARTS - 1)
+        def _():
+            for b in range(S):
+                turned = sums[blocks[b], :].T[0:8]
+                sums_r[:, blocks[b]] = turned
+                for j in range(1, S):
+                    sends[j - 1][:, blocks[b ^ j]] = turned
+
+    outs = run(
+        mixed_backward,
+        "mixed_backward",
+        device,
+        [
+            chunked(core),
+            chunked(z),
+            columns(gate_gain, CH, chunk),
+            whole(cols),
+            whole(squares),
+            rows(w_out, CH, chunk),
+        ]
+        + [whole(c) for c in cots],
+        [out_chunked((PARTS, R, CH), F32), out_whole((8, R), F32)]
+        + [out_whole((8, R), F32) for _ in range(1, S)],
+        PARTS,
+        scratch=[pltpu.VMEM((R, 128), F32)],
+        us=1.6,
+    )
+    d_mixed, sums_own = outs[:2]
+    sums_all = [sums_own] + [exchange(outs[1 + j], "shard", j) for j in range(1, S)]
 
     def gate_backward(dev, core_r, z_r, dm_r, gg, cols_r, *refs):
         parts, refs = refs[:S], refs[S:]
@@ -619,6 +699,30 @@
     )
     cotz, d_core, gate_grads, row_scale = outs[PARTS:]
     both_q = [outs[0]] + [exchange(outs[r], "rep", r) for r in range(1, PARTS)]
+
+    far_rows = far_rows + [exchange(far_rows[0], "shard", j) for j in range(1, S)]
+
+    def plane_rows(dev, gain_r, n_r, *refs):
+        cot, far, out_r = refs[:S], refs[S : 2 * S], refs[2 * S]
+        out_r[0:R, 0:D] = n_r[...]
+        for b in range(S):
+            out_r[blocks[b], D : 2 * D] = cot[b][...]
+            x = far[b][:, 0:D].astype(F32)
+            scale = lax.rsqrt(jnp.mean(x * x, axis=1, keepdims=True) + epsilon)
+            at = slice(R + b * T, R + (b + 1) * T)
+            out_r[at, 0:D] = (x * scale * gain_r[...]).astype(BF16)
+            out_r[at, D : 2 * D] = far[b][:, D : 2 * D]
+
+    (plane,) = run(
+        plane_rows,
+        "plane_rows",
+        device,
+        [whole(a) for a in (gain, normed, *cots, *far_rows)],
+        [out_whole((2 * R, 2 * D), BF16)],
+        1,
+        us=1.0,
+    )
+    planes = [plane, exchange(plane, "rep", 1)]
 
     half_parts = PARTS // 2
 
@@ -783,6 +887,7 @@
     near = half_backward(True, far[half_parts + 4])
     cotx_q = [near[0], exchange(near[1], "rep", 1)] + cotx_far
     halves = [near[half_parts : half_parts + 4], far[half_parts : half_parts + 4]]
+    token = near[half_parts + 3]
     d_map_own = near[half_parts + 4]
     d_map_other = [exchange(near[half_parts + 4 + j], "shard", j) for j in range(1, S)]
 
@@ -834,16 +939,16 @@
         us=3.0,
     )
 
-    small_rows = -(-(NB + H + 16) // 16) * 16
+    small_half = -(-(NB + H + 15) // 32) * 16
 
     def maps_backward(
         dev, own, pre_r, pbc_r, cols_r, tbc, n_r, wbc, dn_r, cdt, cg0, cg1, hg0, hg1, gg, *refs
     ):
         others, hid, refs = refs[: S - 1], refs[S - 1 : 2 * S - 1], refs[2 * S - 1 :]
         kept, refs = refs[: S - 1], refs[S - 1 :]
-        dn_own, pack_r = refs[0], refs[1]
-        sends = refs[2 : 1 + S]
-        cot_s, dn_s = refs[1 + S :]
+        dn_own, pack_keep, pack_send = refs[0], refs[1], refs[2]
+        sends = refs[3 : 2 + S]
+        cot_s, dn_s, pack_r = refs[2 + S :]
         pack_r[...] = jnp.zeros_like(pack_r)
         grads = [jnp.zeros((1, NB), F32) for _ in range(5)]
         for b in range(S):
@@ -889,6 +994,11 @@
         for i in range(5):
             pack_r[at + 9 + i : at + 10 + i, 0:NB] = grads[i]
         pack_r[at + 14 : at + 15, :] = gain_sum
+        core_at = lax.rem(mine, 2)
+        keep_at = pl.multiple_of(core_at * small_half, 16)
+        send_at = pl.multiple_of((1 - core_at) * small_half, 16)
+        pack_keep[...] = pack_r[pl.ds(keep_at, small_half), :]
+        pack_send[...] = pack_r[pl.ds(send_at, small_half), :].astype(BF16)
 
     outs = run(
         maps_backward,
@@ -916,14 +1026,22 @@
                 *out_sends,
             )
         ],
-        [out_whole((T, D), F32), out_whole((small_rows, D), F32)]
+        [
+            out_whole((T, D), F32),
+            out_whole((small_half, D), F32),
+            out_whole((small_half, D), BF16),
+        ]
         + [out_whole((T, 2 * D), BF16) for _ in range(1, S)],
         1,
-        scratch=[pltpu.VMEM((R, NB), BF16), pltpu.VMEM((R, D), F32)],
+        scratch=[
+            pltpu.VMEM((R, NB), BF16),
+            pltpu.VMEM((R, D), F32),
+            pltpu.VMEM((2 * small_half, D), F32),
+        ],
         us=3.0,
     )
-    dn_own, pack = outs[:2]
-    dn_other = [exchange(outs[1 + j], "shard", j) for j in range(1, S)]
+    dn_own, pack, pack_send = outs[:3]
+    dn_other = [exchange(outs[2 + j], "shard", j) for j in range(1, S)]
 
     def own_rows(dev, hid, cot, cols_r, rows_r, gain_r, dn_r, out_r, *refs):
         others, refs = refs[: S - 1], refs[S - 1 :]
@@ -970,9 +1088,15 @@
         half = spans // 2
         return jnp.where(i < half, 2 * i + 1, 2 * (i - half))
 
-    def by_span(array):
-        height = array.shape[0]
-        return (array, pl.BlockSpec((height, DCH), lambda i, dev: (0, span_of(dev) ^ relative(i))))
+    def by_span(array, side):
+        def at(i, dev):
+            return (0, side * spans + (span_of(dev) ^ relative(i)))
+
+        return (array, pl.BlockSpec((array.shape[0], DCH), at))
+
+    def four(refs):
+        ends = (slice(0, R), slice(R, 2 * R))
+        return [refs[0][ends[0], :], refs[1][ends[0], :], refs[0][ends[1], :], refs[1][ends[1], :]]
 
     def store_split(value, slot, send_r, keep_r):
         i = pl.program_id(0)
@@ -986,20 +1110,21 @@
             keep_r[0, slot] = value
 
     def pair_weight_grad(dev, *refs):
-        both, cot, norm = refs[:PARTS], refs[PARTS : 2 * PARTS], refs[2 * PARTS : 3 * PARTS]
+        both, norm, cot = refs[:PARTS], four(refs[PARTS:]), four(refs[PARTS + 2 :])
         value = jnp.zeros((CH, DCH), F32)
         other = jnp.zeros((CH, DCH), F32)
         for r in range(PARTS):
-            value = value + mm_lt(both[r][:, 0:CH], cot[r][...])
-            other = other + mm_lt(both[r][:, CH : 2 * CH], norm[r][...])
-        store_split(value, 0, *refs[3 * PARTS :])
-        store_split(other, 1, *refs[3 * PARTS :])
+            value = value + mm_lt(both[r][:, 0:CH], cot[r])
+            other = other + mm_lt(both[r][:, CH : 2 * CH], norm[r])
+        store_split(value, 0, *refs[-2:])
+        store_split(other, 1, *refs[-2:])
 
     def x_weight_grad(dev, *refs):
         value = jnp.zeros((CH, DCH), F32)
+        norm = four(refs[PARTS:])
         for r in range(PARTS):
-            value = value + mm_lt(refs[r][...], refs[PARTS + r][...])
-        store_split(value, 0, *refs[2 * PARTS :])
+            value = value + mm_lt(refs[r][...], norm[r])
+        store_split(value, 0, *refs[-2:])
 
     def sum_spans(send, keep):
         bit = PARTS
@@ -1044,6 +1169,7 @@
                     at = slice((m ^ r) * CH, ((m ^ r) + 1) * CH)
                     refs[PARTS][at, :] = refs[r][0, 0].astype(F32)
                     refs[PARTS + 1][:, at] = refs[r][0, 1].astype(F32).T
+        refs[PARTS + 2][...] = jnp.zeros((8, 128), F32)
 
     def join_x(dev, *refs):
         mine = part_of(dev)
@@ -1053,26 +1179,27 @@
             def _():
                 for r in range(PARTS):
                     at = slice((m ^ r) * CH, ((m ^ r) + 1) * CH)
-                    refs[PARTS][:, at] = refs[r][0, 0].astype(F32).T
+                    refs[PARTS + 1][:, at] = refs[r][0, 0].astype(F32).T
 
     send, keep = run(
         pair_weight_grad,
         "pair_weight_grad",
         device,
         [whole(b) for b in both_q]
-        + [by_span(c) for c in cots_all]
-        + [by_span(n) for n in normed_all],
+        + [by_span(p, 0) for p in planes]
+        + [by_span(p, 1) for p in planes]
+        + [whole(token)],
         split_specs((2, CH, DCH)),
         spans,
         us=5.0,
     )
     pieces = sum_spans(send, keep)
-    grad_out, grad_z = run(
+    grad_out, grad_z, joined = run(
         join_pair,
         "join_pair",
         device,
         [chunked(p) for p in pieces],
-        [out_spec(), in_spec()],
+        [out_spec(), in_spec(), out_whole((8, 128), F32)],
         spans,
         us=6.0,
     )
@@ -1080,7 +1207,7 @@
         x_weight_grad,
         "x_weight_grad",
         device,
-        [whole(c) for c in cotx_q] + [by_span(n) for n in normed_all],
+        [whole(c) for c in cotx_q] + [by_span(p, 0) for p in planes],
         split_specs((1, CH, DCH)),
         spans,
         us=2.5,
@@ -1090,19 +1217,29 @@
         join_x,
         "join_x",
         device,
-        [chunked(p) for p in pieces],
+        [chunked(p) for p in pieces] + [whole(joined)],
         [in_spec()],
         spans,
         us=4.0,
     )
 
-    bit = 1
+    pack = pack + exchange(pack_send, "rep", 1).astype(F32)
+    bit = 2
     while bit < replicas:
         rounded = pack.astype(BF16)
         pack = rounded.astype(F32) + exchange(rounded, "rep", bit).astype(F32)
         bit *= 2
 
-    def unpack(dev, pack_r, *refs):
+    pack = pack.astype(BF16)
+    pack_other = exchange(pack, "rep", 1)
+
+    def unpack(dev, own, other, *refs):
+        pack_r = refs[-1]
+        core_at = lax.rem(part_of(dev), 2)
+        own_at = pl.multiple_of(core_at * small_half, 16)
+        other_at = pl.multiple_of((1 - core_at) * small_half, 16)
+        pack_r[pl.ds(own_at, small_half), :] = own[...].astype(F32)
+        pack_r[pl.ds(other_at, small_half), :] = other[...].astype(F32)
         at = NB + H
         refs[0][...] = pack_r[0:NB, :].T
         refs[1][...] = pack_r[NB:at, :]
@@ -1126,7 +1263,7 @@
         unpack,
         "unpack",
         device,
-        [whole(pack)],
+        [whole(pack), whole(pack_other)],
         [
             out_whole(shape, F32)
             for shape in [(D, NB), (H, D), (4, C), (4, NB), (1, C), (1, NB)]
@@ -1135,6 +1272,7 @@
             + [(1, D // S)] * S
         ],
         1,
+        scratch=[pltpu.VMEM((2 * small_half, D), F32)],
         us=1.5,
     )
     grad_bc, grad_dt, grad_conv_x, grad_conv_bc, grad_bias_x, grad_bias_bc = outs[:6]

time: 176 us -> 157 us (0.89)
  waiting for transfers between devices: 98.1 us -> 73.6 us
  starting transfers between devices: 33.7 us -> 36.6 us
  Pallas kernels: 35.2 us -> 37.5 us
    ppermute x38 -> x36, waiting for transfers between devices: 98.1 us -> 73.6 us  [exchange(): return lax.ppermute(array, axis, [(i, i ^ bit) for i in range(count)])]
    ppermute x38 -> x36, starting transfers between devices: 33.7 us -> 36.6 us  [exchange(): return lax.ppermute(array, axis, [(i, i ^ bit) for i in range(count)])]
    pallas_call x14 -> x17, Pallas kernels: 35.2 us -> 37.5 us  [run(): pl.pallas_call(body, name=name, out_shape=[shape for shape, _ in outs], g...]
    unnamed x44 -> x46, local copies, waits for them, and re-layouts: 6.03 us -> 6.98 us
  transfers between devices with their start and end apart: 38 -> 36, of which waited for: 17 -> 14; matrix products, arithmetic and copies ran while one was open for 1% -> 1% of each run, Pallas kernels for 16% -> 20%
where the time goes in v3:
time: 157 us
  waiting for transfers between devices  73.6 us (47%)
  Pallas kernels  37.5 us (24%)
  starting transfers between devices  36.6 us (23%)
  local copies, waits for them, and re-layouts  7.02 us (4%)
    ppermute x36, waiting for transfers between devices, exchange(): return lax.ppermute(array, axis, [(i, i ^ bit) for i in range(count)])  73.6 us
    pallas_call x17, Pallas kernels, run(): pl.pallas_call(body, name=name, out_shape=[shape for shape, _ in outs], g...  37.5 us
    ppermute x36, starting transfers between devices, exchange(): return lax.ppermute(array, axis, [(i, i ^ bit) for i in range(count)])  36.6 us
    unnamed x46, local copies, waits for them, and re-layouts  6.98 us
  transfers between devices with their start and end apart: 36, of which 14 were waited for; matrix products, arithmetic and copies ran while one was open for 1% of the time, Pallas kernels for 20%

profile of v3, /device:TPU:0, one launch (start us, length us, event | category | flops | bytes accessed | tf_op | source)
XLA Modules:
  0.0 157.1 jit_solution(15221067728575880446)
XLA Ops:
  0.6 3.0 %collective-permute-start.1 = (bf16[128,1024]{1,0:T(8,128)(2,1)}, bf16[128,1024]{1,0:T(8,128)(2,1)S(1)}, u32[]{:S(2)}, u32[]{:S(2)}) collective-permute-start(bf16[128,1024]{1,0:T(8,128)(2,1)} %hid.1), channel_id=1, source_target_pairs={{0,1},{1,0},{2,3},{3,2},{4,5},{5,4},{6,7},{7,6},{8,9},{9,8},{10,11... | collective-permute-start | bytes 786440 | tf_op jit(solution)/shard_map/ppermute | solution.py:21
  3.7 0.9 copy-done.3
  11.2 2.0 %collective-permute-start.16 = (bf16[128,2048]{1,0:T(8,128)(2,1)S(1)}, bf16[128,2048]{1,0:T(8,128)(2,1)S(1)}, u32[]{:S(2)}, u32[]{:S(2)}) collective-permute-start(bf16[128,2048]{1,0:T(8,128)(2,1)S(1)} %get-tuple-element.154), channel_id=1, source_target_pairs={{0,4},{2,6},{4,0},{6,2},{8,12},{10,14},{12,8},{14,10},{16,20},{18,... | collective-permute-start | bytes 1572872 | tf_op jit(solution)/shard_map/ppermute | solution.py:21
  13.2 1.6 %collective-permute-done.refs_1_ = f32[1,512]{1,0:T(1,128)S(1)} collective-permute-done((f32[1,512]{1,0:T(1,128)S(1)}, f32[1,512]{1,0:T(1,128)S(1)}, u32[]{:S(2)}, u32[]{:S(2)}) %collective-permute-start) | collective-permute-done | bytes 2080 | tf_op jit(solution)/shard_map/ppermute | solution.py:21
  15.5 2.0 %collective-permute-start.3 = (bf16[128,1024]{1,0:T(8,128)(2,1)S(1)}, bf16[128,1024]{1,0:T(8,128)(2,1)S(1)}, u32[]{:S(2)}, u32[]{:S(2)}) collective-permute-start(bf16[128,1024]{1,0:T(8,128)(2,1)S(1)} %get-tuple-element.114.refs_0_), channel_id=1, source_target_pairs={{0,1},{1,0},{2,3},{3,2},{4,5},{5,4},{6,7},{7,6},{8,9},{9,8},{10,11... | collective-permute-start | bytes 786440 | tf_op jit(solution)/shard_map/ppermute | solution.py:21
  17.6 3.4 %projections.1 = (f32[4,256,256]{2,1,0:T(8,128)S(1)}, f32[4,256,256]{2,1,0:T(8,128)S(1)}, f32[4,256,256]{2,1,0:T(8,128)S(1)}, f32[4,256,128]{2,1,0:T(8,128)S(1)}...) custom-call(s32[1]{0:T(128)} %bitcast.dev, ...), custom_call_target="tpu_custom_call" | custom-call | flops 12000000000 | bytes 9179328 | tf_op jit(solution)/shard_map/projections/pallas_call | solution.py:110
  21.0 3.4 %scan_forward.1 = (f32[4,256,256]{2,1,0:T(8,128)S(1)}, f32[256,128]{1,0:T(8,128)S(1)}, f32[128,1024]{1,0:T(8,128)S(1)}, bf16[128,1024]{1,0:T(8,128)(2,1)S(1)}) custom-call(s32[1]{0:T(128)} %bitcast.dev, bf16[256,128]{1,0:T(8,128)(2,1)S(1)} %get-tuple-element.102.a_r, bf16[256,128]{1,0:T(8,128)(2,1)S(1)} %collective-permute-done.2.b_r, ...), custom_call_target="tpu_custom_call" | custom-call | flops 12000000000 | bytes 7540736 | tf_op jit(solution)/shard_map/scan_forward/pallas_call | solution.py:110
  24.4 2.4 %mixed_backward.1 = (f32[4,256,256]{2,1,0:T(8,128)S(1)}, f32[8,256]{1,0:T(8,128)S(1)}, f32[8,256]{1,0:T(8,128)S(1)}) custom-call(s32[1]{0:T(128)} %bitcast.dev, f32[4,256,256]{2,1,0:T(8,128)S(1)} %get-tuple-element.112.core_r, f32[4,256,256]{2,1,0:T(8,128)S(1)} %get-tuple-element.111.z_r, f32[1,1024]{1,0:T(1,128)S(1)} %copy-done.12, ...), custom_call_target="tpu_custom_call" | custom-call | flops 4800000000 | bytes 6049792 | tf_op jit(solution)/shard_map/mixed_backward/pallas_call | solution.py:110
  26.9 1.9 %collective-permute-start.17 = (bf16[128,2048]{1,0:T(8,128)(2,1)S(1)}, bf16[128,2048]{1,0:T(8,128)(2,1)S(1)}, u32[]{:S(2)}, u32[]{:S(2)}) collective-permute-start(bf16[128,2048]{1,0:T(8,128)(2,1)S(1)} %collective-permute-done.16.refs_2_), channel_id=1, source_target_pairs={{0,1},{1,0},{2,3},{3,2},{4,5},{5,4},{6,7},{7,6},{8,9},{9,8},{10,11... | collective-permute-start | bytes 1572872 | tf_op jit(solution)/shard_map/ppermute | solution.py:21
  28.9 1.8 %collective-permute-done.4.refs_1_ = f32[8,256]{1,0:T(8,128)S(1)} collective-permute-done((f32[8,256]{1,0:T(8,128)S(1)}, f32[8,256]{1,0:T(8,128)S(1)}, u32[]{:S(2)}, u32[]{:S(2)}) %collective-permute-start.4) | collective-permute-done | bytes 8224 | tf_op jit(solution)/shard_map/ppermute | solution.py:21
  30.6 1.6 %gate_backward.1 = (bf16[256,512]{1,0:T(8,128)(2,1)S(1)}, bf16[256,512]{1,0:T(8,128)(2,1)S(1)}, bf16[256,512]{1,0:T(8,128)(2,1)S(1)}, bf16[256,512]{1,0:T(8,128)...) custom-call(s32[1]{0:T(128)} %bitcast.dev, ...), custom_call_target="tpu_custom_call" | custom-call | flops 6600000000 | bytes 5558272 | tf_op jit(solution)/shard_map/gate_backward/pallas_call | solution.py:110
  32.3 1.6 collective-permute-start.14
  34.2 4.8 %collective-permute-done.17.refs_3_ = bf16[128,2048]{1,0:T(8,128)(2,1)S(1)} collective-permute-done((bf16[128,2048]{1,0:T(8,128)(2,1)S(1)}, bf16[128,2048]{1,0:T(8,128)(2,1)S(1)}, u32[]{:S(2)}, u32[]{:S(2)}) %collective-permute-start.17) | collective-permute-done | bytes 524320 | tf_op jit(solution)/shard_map/ppermute | solution.py:21
  39.3 3.5 %scan_backward_far.1 = (bf16[256,256]{1,0:T(8,128)(2,1)S(1)}, bf16[256,256]{1,0:T(8,128)(2,1)S(1)}, bf16[2,256,256]{2,1,0:T(8,128)(2,1)S(1)}, f32[2,256,128]{2,1...) custom-call(s32[1]{0:T(128)} %bitcast.dev, ...), custom_call_target="tpu_custom_call" | custom-call | flops 15000000512 | bytes 6152192 | tf_op jit(solution)/shard_map/scan_backward_far/pallas_call | solution.py:110
  42.9 3.7 %scan_backward_near.1 = (bf16[256,256]{1,0:T(8,128)(2,1)S(1)}, bf16[256,256]{1,0:T(8,128)(2,1)S(1)}, bf16[2,256,256]{2,1,0:T(8,128)(2,1)S(1)}, f32[2,256,128]{2,...) custom-call(s32[1]{0:T(128)} %bitcast.dev, ...), custom_call_target="tpu_custom_call" | custom-call | flops 15000000512 | bytes 6348800 | tf_op jit(solution)/shard_map/scan_backward_near/pallas_call | solution.py:110
  46.6 2.9 %pair_weight_grad.1 = (bf16[2,2,256,256]{3,2,1,0:T(8,128)(2,1)S(1)}, f32[2,2,256,256]{3,2,1,0:T(8,128)S(1)}) custom-call(s32[1]{0:T(128)} %bitcast.dev, bf16[256,512]{1,0:T(8,128)(2,1)S(1)} %get-tuple-element.150.refs_0_, bf16[256,512]{1,0:T(8,128)(2,1)S(1)} %collective-permute-done.13.refs_1_, bf16[256,512]{1,0:T(8,128)(2,1)S(1)} %collective-permute-done.14.refs_2_, ...), custom_call_target="tpu_custom_call" | custom-call | flops 15000000512 | bytes 11018240 | tf_op jit(solution)/shard_map/pair_weight_grad/pallas_call | solution.py:110
  49.5 1.6 %collective-permute-start.19 = (bf16[2,2,256,256]{3,2,1,0:T(8,128)(2,1)S(1)}, bf16[2,2,256,256]{3,2,1,0:T(8,128)(2,1)S(1)}, u32[]{:S(2)}, u32[]{:S(2)}) collective-permute-start(bf16[2,2,256,256]{3,2,1,0:T(8,128)(2,1)S(1)} %get-tuple-element.156), channel_id=1, source_target_pairs={{0,8},{2,10},{4,12},{6,14},{8,0},{10,2},{12,4},{14,6},{16,24},{18,... | collective-permute-start | bytes 1572872 | tf_op jit(solution)/shard_map/ppermute | solution.py:21
  51.2 1.5 collective-permute-start.5
  52.7 1.5 collective-permute-start.27
  54.6 9.3 %collective-permute-done.19 = bf16[2,2,256,256]{3,2,1,0:T(8,128)(2,1)S(1)} collective-permute-done((bf16[2,2,256,256]{3,2,1,0:T(8,128)(2,1)S(1)}, bf16[2,2,256,256]{3,2,1,0:T(8,128)(2,1)S(1)}, u32[]{:S(2)}, u32[]{:S(2)}) %collective-permute-start.19) | collective-permute-done | bytes 524320 | tf_op jit(solution)/shard_map/ppermute | solution.py:21
  64.1 2.7 %collective-permute-start.20 = (bf16[1,2,256,256]{3,2,1,0:T(8,128)(2,1)S(1)}, bf16[1,2,256,256]{3,2,1,0:T(8,128)(2,1)S(1)}, u32[]{:S(2)}, u32[]{:S(2)}) collective-permute-start(bf16[1,2,256,256]{3,2,1,0:T(8,128)(2,1)S(1)} %slice.34), channel_id=1, source_target_pairs={{0,16},{2,18},{4,20},{6,22},{8,24},{10,26},{12,28},{14,30},{16,0},... | collective-permute-start | bytes 786440 | tf_op jit(solution)/shard_map/ppermute | solution.py:21
  66.7 3.1 %input_backward.1 = (f32[256,1024]{1,0:T(8,128)S(1)}, bf16[256,128]{1,0:T(8,128)(2,1)S(1)}) custom-call(s32[1]{0:T(128)} %bitcast.dev, bf16[4,256,256]{2,1,0:T(8,128)(2,1)S(1)} %get-tuple-element.127.cz, bf16[2,256,256]{2,1,0:T(8,128)(2,1)S(1)} %get-tuple-element.128.near_x, bf16[2,256,256]{2,1,0:T(8,128)(2,1)S(1)} %get-tuple-element.129.far_x, ...), custom_call_target="tpu_custom_call" | custom-call | flops 8999999488 | bytes 6914048 | tf_op jit(solution)/shard_map/input_backward/pallas_call | solution.py:110
  69.8 8.7 %collective-permute-done.20 = bf16[1,2,256,256]{3,2,1,0:T(8,128)(2,1)S(1)} collective-permute-done((bf16[1,2,256,256]{3,2,1,0:T(8,128)(2,1)S(1)}, bf16[1,2,256,256]{3,2,1,0:T(8,128)(2,1)S(1)}, u32[]{:S(2)}, u32[]{:S(2)}) %collective-permute-start.20) | collective-permute-done | bytes 262176 | tf_op jit(solution)/shard_map/ppermute | solution.py:21
  78.7 1.1 maps_backward.1
  79.8 12.5 %collective-permute-done.21 = bf16[1,2,256,256]{3,2,1,0:T(8,128)(2,1)S(1)} collective-permute-done((bf16[1,2,256,256]{3,2,1,0:T(8,128)(2,1)S(1)}, bf16[1,2,256,256]{3,2,1,0:T(8,128)(2,1)S(1)}, u32[]{:S(2)}, u32[]{:S(2)}) %collective-permute-start.21) | collective-permute-done | bytes 262176 | tf_op jit(solution)/shard_map/ppermute | solution.py:21
  92.5 1.9 %x_weight_grad.1 = (bf16[2,1,256,256]{3,2,1,0:T(8,128)(2,1)S(1)}, f32[2,1,256,256]{3,2,1,0:T(8,128)S(1)}) custom-call(s32[1]{0:T(128)} %bitcast.dev, bf16[256,256]{1,0:T(8,128)(2,1)S(1)} %get-tuple-element.158.refs_0_, bf16[256,256]{1,0:T(8,128)(2,1)S(1)} %collective-permute-done.26.refs_1_, bf16[256,256]{1,0:T(8,128)(2,1)S(1)} %collective-permute-done.27.refs_2_, ...), custom_call_target="tpu_custom_call" | custom-call | flops 7500000256 | bytes 5505024 | tf_op jit(solution)/shard_map/x_weight_grad/pallas_call | solution.py:110
  94.4 2.1 %collective-permute-start.29 = (bf16[2,1,256,256]{3,2,1,0:T(8,128)(2,1)S(1)}, bf16[2,1,256,256]{3,2,1,0:T(8,128)(2,1)S(1)}, u32[]{:S(2)}, u32[]{:S(2)}) collective-permute-start(bf16[2,1,256,256]{3,2,1,0:T(8,128)(2,1)S(1)} %get-tuple-element.163), channel_id=1, source_target_pairs={{0,8},{2,10},{4,12},{6,14},{8,0},{10,2},{12,4},{14,6},{16,24},{18,... | collective-permute-start | bytes 786440 | tf_op jit(solution)/shard_map/ppermute | solution.py:21
  96.5 1.5 collective-permute-start.8
  98.1 9.1 %collective-permute-done.22 = bf16[2,2,256,256]{3,2,1,0:T(8,128)(2,1)S(1)} collective-permute-done((bf16[2,2,256,256]{3,2,1,0:T(8,128)(2,1)S(1)}, bf16[2,2,256,256]{3,2,1,0:T(8,128)(2,1)S(1)}, u32[]{:S(2)}, u32[]{:S(2)}) %collective-permute-start.22) | collective-permute-done | bytes 524320 | tf_op jit(solution)/shard_map/ppermute | solution.py:21
  107.3 1.5 collective-permute-start.24
  108.8 1.2 collective-permute-done.29
  110.1 2.0 %collective-permute-start.30 = (bf16[1,1,256,256]{3,2,1,0:T(8,128)(2,1)S(1)}, bf16[1,1,256,256]{3,2,1,0:T(8,128)(2,1)S(1)}, u32[]{:S(2)}, u32[]{:S(2)}) collective-permute-start(bf16[1,1,256,256]{3,2,1,0:T(8,128)(2,1)S(1)} %slice.35), channel_id=1, source_target_pairs={{0,16},{2,18},{4,20},{6,22},{8,24},{10,26},{12,28},{14,30},{16,0},... | collective-permute-start | bytes 393224 | tf_op jit(solution)/shard_map/ppermute | solution.py:21
  112.1 1.8 %collective-permute-start.9 = (bf16[80,1024]{1,0:T(8,128)(2,1)S(1)}, bf16[80,1024]{1,0:T(8,128)(2,1)S(1)}, u32[]{:S(2)}, u32[]{:S(2)}) collective-permute-start(bf16[80,1024]{1,0:T(8,128)(2,1)S(1)} %add_convert_fusion.2), channel_id=1, source_target_pairs={{0,8},{2,10},{4,12},{6,14},{8,0},{10,2},{12,4},{14,6},{16,24},{18,... | collective-permute-start | bytes 491528 | tf_op jit(solution)/shard_map/ppermute | solution.py:21
  113.9 4.2 %collective-permute-done.30 = bf16[1,1,256,256]{3,2,1,0:T(8,128)(2,1)S(1)} collective-permute-done((bf16[1,1,256,256]{3,2,1,0:T(8,128)(2,1)S(1)}, bf16[1,1,256,256]{3,2,1,0:T(8,128)(2,1)S(1)}, u32[]{:S(2)}, u32[]{:S(2)}) %collective-permute-start.30) | collective-permute-done | bytes 131104 | tf_op jit(solution)/shard_map/ppermute | solution.py:21
  118.1 1.4 collective-permute-start.31
  119.6 1.7 %collective-permute-start.10 = (bf16[80,1024]{1,0:T(8,128)(2,1)S(1)}, bf16[80,1024]{1,0:T(8,128)(2,1)S(1)}, u32[]{:S(2)}, u32[]{:S(2)}) collective-permute-start(bf16[80,1024]{1,0:T(8,128)(2,1)S(1)} %add_convert_fusion.1), channel_id=1, source_target_pairs={{0,16},{2,18},{4,20},{6,22},{8,24},{10,26},{12,28},{14,30},{16,0},... | collective-permute-start | bytes 491528 | tf_op jit(solution)/shard_map/ppermute | solution.py:21
  121.2 9.9 %collective-permute-done.31 = bf16[1,1,256,256]{3,2,1,0:T(8,128)(2,1)S(1)} collective-permute-done((bf16[1,1,256,256]{3,2,1,0:T(8,128)(2,1)S(1)}, bf16[1,1,256,256]{3,2,1,0:T(8,128)(2,1)S(1)}, u32[]{:S(2)}, u32[]{:S(2)}) %collective-permute-start.31) | collective-permute-done | bytes 131104 | tf_op jit(solution)/shard_map/ppermute | solution.py:21
  131.8 1.1 collective-permute-done.10
  133.0 1.6 collective-permute-start.6
  134.6 3.8 %collective-permute-done.32 = bf16[2,1,256,256]{3,2,1,0:T(8,128)(2,1)S(1)} collective-permute-done((bf16[2,1,256,256]{3,2,1,0:T(8,128)(2,1)S(1)}, bf16[2,1,256,256]{3,2,1,0:T(8,128)(2,1)S(1)}, u32[]{:S(2)}, u32[]{:S(2)}) %collective-permute-start.32) | collective-permute-done | bytes 262176 | tf_op jit(solution)/shard_map/ppermute | solution.py:21
  138.5 1.5 collective-permute-start.34
  140.0 1.1 unpack.1
  141.1 1.5 collective-permute-start.12
  142.7 4.7 %collective-permute-done.6.refs_0_ = bf16[128,2048]{1,0:T(8,128)(2,1)S(1)} collective-permute-done((bf16[128,2048]{1,0:T(8,128)(2,1)S(1)}, bf16[128,2048]{1,0:T(8,128)(2,1)S(1)}, u32[]{:S(2)}, u32[]{:S(2)}) %collective-permute-start.6) | collective-permute-done | bytes 524320 | tf_op jit(solution)/shard_map/ppermute | solution.py:21
  147.4 1.4 own_rows.1
  149.4 1.0 collective-permute-done.34.refs_2_
  150.4 3.9 %join_pair.1 = (f32[1024,1024]{1,0:T(8,128)}, f32[1024,1024]{1,0:T(8,128)}, f32[8,128]{1,0:T(8,128)S(1)}) custom-call(s32[1]{0:T(128)} %bitcast.dev, bf16[4,2,256,256]{3,2,1,0:T(8,128)(2,1)S(1)} %pad_maximum_fusion.refs_0_, bf16[4,2,256,256]{3,2,1,0:T(8,128)(2,1)S(1)} %collective-permute-done.23.refs_1_, ...), custom_call_target="tpu_custom_call" | custom-call | flops 17999998976 | bytes 12587008 | tf_op jit(solution)/shard_map/join_pair/pallas_call | solution.py:110
  154.3 2.8 %join_x.1 = f32[1024,1024]{1,0:T(8,128)} custom-call(s32[1]{0:T(128)} %bitcast.dev, bf16[4,1,256,256]{3,2,1,0:T(8,128)(2,1)S(1)} %pad_maximum_fusion.2.refs_0_, bf16[4,1,256,256]{3,2,1,0:T(8,128)(2,1)S(1)} %collective-permute-done.33.refs_1_, bf16[4,1,256,256]{3,2,1,0:T(8,128)(2,1)S(1)} %collective-permute-done.34.refs_2_, ...), custom_call_target="tpu_custom_call" | custom-call | flops 12000000000 | bytes 6295552 | tf_op jit(solution)/shard_map/join_x/pallas_call | solution.py:110
  (102 shorter events, 10.8 us)
Async XLA Ops:
  0.6 14.2 %collective-permute-start.1 = (bf16[128,1024]{1,0:T(8,128)(2,1)}, bf16[128,1024]{1,0:T(8,128)(2,1)S(1)}, u32[]{:S(2)}, u32[]{:S(2)}) collective-permute-start(bf16[128,1024]{1,0:T(8,128)(2,1)} %hid.1), channel_id=1, source_target_pairs={{0,1},{1,0},{2,3},{3,2},{4,5},{5,4},{6,7},{7,6},{8,9},{9,8},{10,11... | collective-permute-start | bytes 786440 | tf_op jit(solution)/shard_map/ppermute | solution.py:21
  10.6 4.2 %copy-start.6 = (bf16[128,1024]{1,0:T(8,128)(2,1)S(1)}, bf16[128,1024]{1,0:T(8,128)(2,1)}, u32[]{:S(2)}) copy-start(bf16[128,1024]{1,0:T(8,128)(2,1)} %hid.1) | copy-start | bytes 786436
  11.1 3.7 %collective-permute-start = (f32[1,512]{1,0:T(1,128)S(1)}, f32[1,512]{1,0:T(1,128)S(1)}, u32[]{:S(2)}, u32[]{:S(2)}) collective-permute-start(f32[1,512]{1,0:T(1,128)S(1)} %get-tuple-element.101.refs_0_), channel_id=1, source_target_pairs={{0,1},{1,0},{2,3},{3,2},{4,5},{5,4},{6,7},{7,6},{8,9},{9,8},{10,11... | collective-permute-start | bytes 6152 | tf_op jit(solution)/shard_map/ppermute | solution.py:21
  11.2 15.7 %collective-permute-start.16 = (bf16[128,2048]{1,0:T(8,128)(2,1)S(1)}, bf16[128,2048]{1,0:T(8,128)(2,1)S(1)}, u32[]{:S(2)}, u32[]{:S(2)}) collective-permute-start(bf16[128,2048]{1,0:T(8,128)(2,1)S(1)} %get-tuple-element.154), channel_id=1, source_target_pairs={{0,4},{2,6},{4,0},{6,2},{8,12},{10,14},{12,8},{14,10},{16,20},{18,... | collective-permute-start | bytes 1572872 | tf_op jit(solution)/shard_map/ppermute | solution.py:21
  14.8 2.7 %copy-start.1 = (bf16[1,1024,1024]{2,1,0:T(8,128)(2,1)S(1)}, bf16[1,1024,1024]{2,1,0:T(8,128)(2,1)}, u32[]{:S(2)}) copy-start(bf16[1,1024,1024]{2,1,0:T(8,128)(2,1)} %param.22) | copy-start | bytes 6291460
  14.8 2.7 %copy-start.2 = (bf16[1,1024,1024]{2,1,0:T(8,128)(2,1)S(1)}, bf16[1,1024,1024]{2,1,0:T(8,128)(2,1)}, u32[]{:S(2)}) copy-start(bf16[1,1024,1024]{2,1,0:T(8,128)(2,1)} %param.23) | copy-start | bytes 6291460
  14.8 2.7 %copy-start.9 = (bf16[1,1024,16]{1,2,0:T(8,128)(2,1)S(1)}, bf16[1,1024,16]{1,2,0:T(8,128)(2,1)}, u32[]{:S(2)}) copy-start(bf16[1,1024,16]{1,2,0:T(8,128)(2,1)} %param.25) | copy-start | bytes 98308
  14.8 2.7 %copy-start.10 = (f32[1,4,1024]{2,1,0:T(4,128)S(1)}, f32[1,4,1024]{2,1,0:T(4,128)}, u32[]{:S(2)}) copy-start(f32[1,4,1024]{2,1,0:T(4,128)} %param.26) | copy-start | bytes 49156
  14.8 2.7 %copy-start.11 = (f32[1,1024]{1,0:T(1,128)S(1)}, f32[1,1024]{1,0:T(1,128)}, u32[]{:S(2)}) copy-start(f32[1,1024]{1,0:T(1,128)} %bx.1) | copy-start | bytes 12292
  14.9 2.6 %copy-start.20 = (f32[1,16]{1,0:T(1,128)S(1)}, f32[1,16]{1,0:T(1,128)}, u32[]{:S(2)}) copy-start(f32[1,16]{1,0:T(1,128)} %dtb.1) | copy-start | bytes 196
  15.4 5.6 %collective-permute-start.2 = (bf16[256,128]{1,0:T(8,128)(2,1)S(1)}, bf16[256,128]{1,0:T(8,128)(2,1)S(1)}, u32[]{:S(2)}, u32[]{:S(2)}) collective-permute-start(bf16[256,128]{1,0:T(8,128)(2,1)S(1)} %get-tuple-element.103), channel_id=1, source_target_pairs={{0,1},{1,0},{2,3},{3,2},{4,5},{5,4},{6,7},{7,6},{8,9},{9,8},{10,11... | collective-permute-start | bytes 196616 | tf_op jit(solution)/shard_map/ppermute | solution.py:21
  15.5 8.9 %collective-permute-start.3 = (bf16[128,1024]{1,0:T(8,128)(2,1)S(1)}, bf16[128,1024]{1,0:T(8,128)(2,1)S(1)}, u32[]{:S(2)}, u32[]{:S(2)}) collective-permute-start(bf16[128,1024]{1,0:T(8,128)(2,1)S(1)} %get-tuple-element.114.refs_0_), channel_id=1, source_target_pairs={{0,1},{1,0},{2,3},{3,2},{4,5},{5,4},{6,7},{7,6},{8,9},{9,8},{10,11... | collective-permute-start | bytes 786440 | tf_op jit(solution)/shard_map/ppermute | solution.py:21
  17.5 3.4 %copy-start = (bf16[1,1024,1024]{2,1,0:T(8,128)(2,1)S(1)}, bf16[1,1024,1024]{2,1,0:T(8,128)(2,1)}, u32[]{:S(2)}) copy-start(bf16[1,1024,1024]{2,1,0:T(8,128)(2,1)} %param.34) | copy-start | bytes 6291460
  17.5 3.4 %copy-start.12 = (f32[1,1024]{1,0:T(1,128)S(1)}, f32[1,1024]{1,0:T(1,128)}, u32[]{:S(2)}) copy-start(f32[1,1024]{1,0:T(1,128)} %gg.5) | copy-start | bytes 12292
  26.8 3.9 %collective-permute-start.4 = (f32[8,256]{1,0:T(8,128)S(1)}, f32[8,256]{1,0:T(8,128)S(1)}, u32[]{:S(2)}, u32[]{:S(2)}) collective-permute-start(f32[8,256]{1,0:T(8,128)S(1)} %get-tuple-element.117), channel_id=1, source_target_pairs={{0,1},{1,0},{2,3},{3,2},{4,5},{5,4},{6,7},{7,6},{8,9},{9,8},{10,11... | collective-permute-start | bytes 24584 | tf_op jit(solution)/shard_map/ppermute | solution.py:21
  26.9 12.0 %collective-permute-start.17 = (bf16[128,2048]{1,0:T(8,128)(2,1)S(1)}, bf16[128,2048]{1,0:T(8,128)(2,1)S(1)}, u32[]{:S(2)}, u32[]{:S(2)}) collective-permute-start(bf16[128,2048]{1,0:T(8,128)(2,1)S(1)} %collective-permute-done.16.refs_2_), channel_id=1, source_target_pairs={{0,1},{1,0},{2,3},{3,2},{4,5},{5,4},{6,7},{7,6},{8,9},{9,8},{10,11... | collective-permute-start | bytes 1572872 | tf_op jit(solution)/shard_map/ppermute | solution.py:21
  32.2 14.4 %collective-permute-start.13 = (bf16[256,512]{1,0:T(8,128)(2,1)S(1)}, bf16[256,512]{1,0:T(8,128)(2,1)S(1)}, u32[]{:S(2)}, u32[]{:S(2)}) collective-permute-start(bf16[256,512]{1,0:T(8,128)(2,1)S(1)} %get-tuple-element.151), channel_id=1, source_target_pairs={{0,2},{2,0},{4,6},{6,4},{8,10},{10,8},{12,14},{14,12},{16,18},{18,... | collective-permute-start | bytes 786440 | tf_op jit(solution)/shard_map/ppermute | solution.py:21
  32.3 14.3 %collective-permute-start.14 = (bf16[256,512]{1,0:T(8,128)(2,1)S(1)}, bf16[256,512]{1,0:T(8,128)(2,1)S(1)}, u32[]{:S(2)}, u32[]{:S(2)}) collective-permute-start(bf16[256,512]{1,0:T(8,128)(2,1)S(1)} %get-tuple-element.152), channel_id=1, source_target_pairs={{0,4},{2,6},{4,0},{6,2},{8,12},{10,14},{12,8},{14,10},{16,20},{18,... | collective-permute-start | bytes 786440 | tf_op jit(solution)/shard_map/ppermute | solution.py:21
  33.9 12.8 %collective-permute-start.15 = (bf16[256,512]{1,0:T(8,128)(2,1)S(1)}, bf16[256,512]{1,0:T(8,128)(2,1)S(1)}, u32[]{:S(2)}, u32[]{:S(2)}) collective-permute-start(bf16[256,512]{1,0:T(8,128)(2,1)S(1)} %get-tuple-element.153), channel_id=1, source_target_pairs={{0,6},{2,4},{4,2},{6,0},{8,14},{10,12},{12,10},{14,8},{16,22},{18,... | collective-permute-start | bytes 786440 | tf_op jit(solution)/shard_map/ppermute | solution.py:21
  39.2 7.4 %collective-permute-start.18 = (bf16[512,2048]{1,0:T(8,128)(2,1)S(1)}, bf16[512,2048]{1,0:T(8,128)(2,1)S(1)}, u32[]{:S(2)}, u32[]{:S(2)}) collective-permute-start(bf16[512,2048]{1,0:T(8,128)(2,1)S(1)} %plane_rows.1.refs_4_.refs_6_), channel_id=1, source_target_pairs={{0,2},{2,0},{4,6},{6,4},{8,10},{10,8},{12,14},{14,12},{16,18},{18,... | collective-permute-start | bytes 6291464 | tf_op jit(solution)/shard_map/ppermute | solution.py:21
  49.5 14.3 %collective-permute-start.19 = (bf16[2,2,256,256]{3,2,1,0:T(8,128)(2,1)S(1)}, bf16[2,2,256,256]{3,2,1,0:T(8,128)(2,1)S(1)}, u32[]{:S(2)}, u32[]{:S(2)}) collective-permute-start(bf16[2,2,256,256]{3,2,1,0:T(8,128)(2,1)S(1)} %get-tuple-element.156), channel_id=1, source_target_pairs={{0,8},{2,10},{4,12},{6,14},{8,0},{10,2},{12,4},{14,6},{16,24},{18,... | collective-permute-start | bytes 1572872 | tf_op jit(solution)/shard_map/ppermute | solution.py:21
  51.2 27.5 %collective-permute-start.5 = (bf16[256,128]{1,0:T(8,128)(2,1)S(1)}, bf16[256,128]{1,0:T(8,128)(2,1)S(1)}, u32[]{:S(2)}, u32[]{:S(2)}) collective-permute-start(bf16[256,128]{1,0:T(8,128)(2,1)S(1)} %get-tuple-element.139), channel_id=1, source_target_pairs={{0,1},{1,0},{2,3},{3,2},{4,5},{5,4},{6,7},{7,6},{8,9},{9,8},{10,11... | collective-permute-start | bytes 196616 | tf_op jit(solution)/shard_map/ppermute | solution.py:21
  52.7 39.8 %collective-permute-start.26 = (bf16[256,256]{1,0:T(8,128)(2,1)S(1)}, bf16[256,256]{1,0:T(8,128)(2,1)S(1)}, u32[]{:S(2)}, u32[]{:S(2)}) collective-permute-start(bf16[256,256]{1,0:T(8,128)(2,1)S(1)} %get-tuple-element.159), channel_id=1, source_target_pairs={{0,2},{2,0},{4,6},{6,4},{8,10},{10,8},{12,14},{14,12},{16,18},{18,... | collective-permute-start | bytes 393224 | tf_op jit(solution)/shard_map/ppermute | solution.py:21
  52.7 39.8 %collective-permute-start.27 = (bf16[256,256]{1,0:T(8,128)(2,1)S(1)}, bf16[256,256]{1,0:T(8,128)(2,1)S(1)}, u32[]{:S(2)}, u32[]{:S(2)}) collective-permute-start(bf16[256,256]{1,0:T(8,128)(2,1)S(1)} %get-tuple-element.160), channel_id=1, source_target_pairs={{0,4},{2,6},{4,0},{6,2},{8,12},{10,14},{12,8},{14,10},{16,20},{18,... | collective-permute-start | bytes 393224 | tf_op jit(solution)/shard_map/ppermute | solution.py:21
  54.2 38.3 %collective-permute-start.28 = (bf16[256,256]{1,0:T(8,128)(2,1)S(1)}, bf16[256,256]{1,0:T(8,128)(2,1)S(1)}, u32[]{:S(2)}, u32[]{:S(2)}) collective-permute-start(bf16[256,256]{1,0:T(8,128)(2,1)S(1)} %get-tuple-element.161), channel_id=1, source_target_pairs={{0,6},{2,4},{4,2},{6,0},{8,14},{10,12},{12,10},{14,8},{16,22},{18,... | collective-permute-start | bytes 393224 | tf_op jit(solution)/shard_map/ppermute | solution.py:21
  64.1 14.5 %collective-permute-start.20 = (bf16[1,2,256,256]{3,2,1,0:T(8,128)(2,1)S(1)}, bf16[1,2,256,256]{3,2,1,0:T(8,128)(2,1)S(1)}, u32[]{:S(2)}, u32[]{:S(2)}) collective-permute-start(bf16[1,2,256,256]{3,2,1,0:T(8,128)(2,1)S(1)} %slice.34), channel_id=1, source_target_pairs={{0,16},{2,18},{4,20},{6,22},{8,24},{10,26},{12,28},{14,30},{16,0},... | collective-permute-start | bytes 786440 | tf_op jit(solution)/shard_map/ppermute | solution.py:21
  66.7 11.9 %copy-start.4 = (bf16[1,1024,128]{2,1,0:T(8,128)(2,1)S(1)}, bf16[1,1024,128]{2,1,0:T(8,128)(2,1)}, u32[]{:S(2)}) copy-start(bf16[1,1024,128]{2,1,0:T(8,128)(2,1)} %param.24) | copy-start | bytes 786436
  66.7 12.0 %copy-start.15 = (f32[1,4,128]{2,1,0:T(4,128)S(1)}, f32[1,4,128]{2,1,0:T(4,128)}, u32[]{:S(2)}) copy-start(f32[1,4,128]{2,1,0:T(4,128)} %param.27) | copy-start | bytes 6148
  78.6 13.8 %collective-permute-start.21 = (bf16[1,2,256,256]{3,2,1,0:T(8,128)(2,1)S(1)}, bf16[1,2,256,256]{3,2,1,0:T(8,128)(2,1)S(1)}, u32[]{:S(2)}, u32[]{:S(2)}) collective-permute-start(bf16[1,2,256,256]{3,2,1,0:T(8,128)(2,1)S(1)} %fusion), channel_id=1, source_target_pairs={{0,16},{2,18},{4,20},{6,22},{8,24},{10,26},{12,28},{14,30},{16,0},... | collective-permute-start | bytes 786440 | tf_op jit(solution)/shard_map/ppermute | solution.py:21
  79.8 16.7 %collective-permute-start.7 = (bf16[80,1024]{1,0:T(8,128)(2,1)S(1)}, bf16[80,1024]{1,0:T(8,128)(2,1)S(1)}, u32[]{:S(2)}, u32[]{:S(2)}) collective-permute-start(bf16[80,1024]{1,0:T(8,128)(2,1)S(1)} %get-tuple-element.147), channel_id=1, source_target_pairs={{0,2},{2,0},{4,6},{6,4},{8,10},{10,8},{12,14},{14,12},{16,18},{18,... | collective-permute-start | bytes 491528 | tf_op jit(solution)/shard_map/ppermute | solution.py:21
  92.4 14.8 %collective-permute-start.22 = (bf16[2,2,256,256]{3,2,1,0:T(8,128)(2,1)S(1)}, bf16[2,2,256,256]{3,2,1,0:T(8,128)(2,1)S(1)}, u32[]{:S(2)}, u32[]{:S(2)}) collective-permute-start(bf16[2,2,256,256]{3,2,1,0:T(8,128)(2,1)S(1)} %pad_maximum_fusion.1), channel_id=1, source_target_pairs={{0,8},{2,10},{4,12},{6,14},{8,0},{10,2},{12,4},{14,6},{16,24},{18,... | collective-permute-start | bytes 1572872 | tf_op jit(solution)/shard_map/ppermute | solution.py:21
  94.4 15.5 %collective-permute-start.29 = (bf16[2,1,256,256]{3,2,1,0:T(8,128)(2,1)S(1)}, bf16[2,1,256,256]{3,2,1,0:T(8,128)(2,1)S(1)}, u32[]{:S(2)}, u32[]{:S(2)}) collective-permute-start(bf16[2,1,256,256]{3,2,1,0:T(8,128)(2,1)S(1)} %get-tuple-element.163), channel_id=1, source_target_pairs={{0,8},{2,10},{4,12},{6,14},{8,0},{10,2},{12,4},{14,6},{16,24},{18,... | collective-permute-start | bytes 786440 | tf_op jit(solution)/shard_map/ppermute | solution.py:21
  96.5 15.6 %collective-permute-start.8 = (bf16[80,1024]{1,0:T(8,128)(2,1)S(1)}, bf16[80,1024]{1,0:T(8,128)(2,1)S(1)}, u32[]{:S(2)}, u32[]{:S(2)}) collective-permute-start(bf16[80,1024]{1,0:T(8,128)(2,1)S(1)} %add_convert_fusion.3), channel_id=1, source_target_pairs={{0,4},{2,6},{4,0},{6,2},{8,12},{10,14},{12,8},{14,10},{16,20},{18,... | collective-permute-start | bytes 491528 | tf_op jit(solution)/shard_map/ppermute | solution.py:21
  107.3 24.1 %collective-permute-start.24 = (bf16[4,2,256,256]{3,2,1,0:T(8,128)(2,1)S(1)}, bf16[4,2,256,256]{3,2,1,0:T(8,128)(2,1)S(1)}, u32[]{:S(2)}, u32[]{:S(2)}) collective-permute-start(bf16[4,2,256,256]{3,2,1,0:T(8,128)(2,1)S(1)} %pad_maximum_fusion.refs_0_), channel_id=1, source_target_pairs={{0,4},{2,6},{4,0},{6,2},{8,12},{10,14},{12,8},{14,10},{16,20},{18,... | collective-permute-start | bytes 3145736 | tf_op jit(solution)/shard_map/ppermute | solution.py:21
  110.1 8.0 %collective-permute-start.30 = (bf16[1,1,256,256]{3,2,1,0:T(8,128)(2,1)S(1)}, bf16[1,1,256,256]{3,2,1,0:T(8,128)(2,1)S(1)}, u32[]{:S(2)}, u32[]{:S(2)}) collective-permute-start(bf16[1,1,256,256]{3,2,1,0:T(8,128)(2,1)S(1)} %slice.35), channel_id=1, source_target_pairs={{0,16},{2,18},{4,20},{6,22},{8,24},{10,26},{12,28},{14,30},{16,0},... | collective-permute-start | bytes 393224 | tf_op jit(solution)/shard_map/ppermute | solution.py:21
  112.1 7.4 %collective-permute-start.9 = (bf16[80,1024]{1,0:T(8,128)(2,1)S(1)}, bf16[80,1024]{1,0:T(8,128)(2,1)S(1)}, u32[]{:S(2)}, u32[]{:S(2)}) collective-permute-start(bf16[80,1024]{1,0:T(8,128)(2,1)S(1)} %add_convert_fusion.2), channel_id=1, source_target_pairs={{0,8},{2,10},{4,12},{6,14},{8,0},{10,2},{12,4},{14,6},{16,24},{18,... | collective-permute-start | bytes 491528 | tf_op jit(solution)/shard_map/ppermute | solution.py:21
  118.1 13.0 %collective-permute-start.31 = (bf16[1,1,256,256]{3,2,1,0:T(8,128)(2,1)S(1)}, bf16[1,1,256,256]{3,2,1,0:T(8,128)(2,1)S(1)}, u32[]{:S(2)}, u32[]{:S(2)}) collective-permute-start(bf16[1,1,256,256]{3,2,1,0:T(8,128)(2,1)S(1)} %fusion.1), channel_id=1, source_target_pairs={{0,16},{2,18},{4,20},{6,22},{8,24},{10,26},{12,28},{14,30},{16,0},... | collective-permute-start | bytes 393224 | tf_op jit(solution)/shard_map/ppermute | solution.py:21
  119.6 13.3 %collective-permute-start.10 = (bf16[80,1024]{1,0:T(8,128)(2,1)S(1)}, bf16[80,1024]{1,0:T(8,128)(2,1)S(1)}, u32[]{:S(2)}, u32[]{:S(2)}) collective-permute-start(bf16[80,1024]{1,0:T(8,128)(2,1)S(1)} %add_convert_fusion.1), channel_id=1, source_target_pairs={{0,16},{2,18},{4,20},{6,22},{8,24},{10,26},{12,28},{14,30},{16,0},... | collective-permute-start | bytes 491528 | tf_op jit(solution)/shard_map/ppermute | solution.py:21
  131.2 7.2 %collective-permute-start.32 = (bf16[2,1,256,256]{3,2,1,0:T(8,128)(2,1)S(1)}, bf16[2,1,256,256]{3,2,1,0:T(8,128)(2,1)S(1)}, u32[]{:S(2)}, u32[]{:S(2)}) collective-permute-start(bf16[2,1,256,256]{3,2,1,0:T(8,128)(2,1)S(1)} %pad_maximum_fusion.3), channel_id=1, source_target_pairs={{0,8},{2,10},{4,12},{6,14},{8,0},{10,2},{12,4},{14,6},{16,24},{18,... | collective-permute-start | bytes 786440 | tf_op jit(solution)/shard_map/ppermute | solution.py:21
  131.3 19.2 %collective-permute-start.23 = (bf16[4,2,256,256]{3,2,1,0:T(8,128)(2,1)S(1)}, bf16[4,2,256,256]{3,2,1,0:T(8,128)(2,1)S(1)}, u32[]{:S(2)}, u32[]{:S(2)}) collective-permute-start(bf16[4,2,256,256]{3,2,1,0:T(8,128)(2,1)S(1)} %pad_maximum_fusion.refs_0_), channel_id=1, source_target_pairs={{0,2},{2,0},{4,6},{6,4},{8,10},{10,8},{12,14},{14,12},{16,18},{18,... | collective-permute-start | bytes 3145736 | tf_op jit(solution)/shard_map/ppermute | solution.py:21
  131.3 19.1 %collective-permute-start.25 = (bf16[4,2,256,256]{3,2,1,0:T(8,128)(2,1)S(1)}, bf16[4,2,256,256]{3,2,1,0:T(8,128)(2,1)S(1)}, u32[]{:S(2)}, u32[]{:S(2)}) collective-permute-start(bf16[4,2,256,256]{3,2,1,0:T(8,128)(2,1)S(1)} %collective-permute-done.24.refs_2_), channel_id=1, source_target_pairs={{0,2},{2,0},{4,6},{6,4},{8,10},{10,8},{12,14},{14,12},{16,18},{18,... | collective-permute-start | bytes 3145736 | tf_op jit(solution)/shard_map/ppermute | solution.py:21
  133.0 7.1 %collective-permute-start.11 = (bf16[80,1024]{1,0:T(8,128)(2,1)S(1)}, bf16[80,1024]{1,0:T(8,128)(2,1)S(1)}, u32[]{:S(2)}, u32[]{:S(2)}) collective-permute-start(bf16[80,1024]{1,0:T(8,128)(2,1)S(1)} %add_convert_fusion.own), channel_id=1, source_target_pairs={{0,2},{2,0},{4,6},{6,4},{8,10},{10,8},{12,14},{14,12},{16,18},{18,... | collective-permute-start | bytes 491528 | tf_op jit(solution)/shard_map/ppermute | solution.py:21
  133.0 14.4 %collective-permute-start.6 = (bf16[128,2048]{1,0:T(8,128)(2,1)S(1)}, bf16[128,2048]{1,0:T(8,128)(2,1)S(1)}, u32[]{:S(2)}, u32[]{:S(2)}) collective-permute-start(bf16[128,2048]{1,0:T(8,128)(2,1)S(1)} %get-tuple-element.143), channel_id=1, source_target_pairs={{0,1},{1,0},{2,3},{3,2},{4,5},{5,4},{6,7},{7,6},{8,9},{9,8},{10,11... | collective-permute-start | bytes 1572872 | tf_op jit(solution)/shard_map/ppermute | solution.py:21
  138.5 8.9 %copy-start.8 = (bf16[128,1024]{1,0:T(8,128)(2,1)S(1)}, bf16[128,1024]{1,0:T(8,128)(2,1)}, u32[]{:S(2)}) copy-start(bf16[128,1024]{1,0:T(8,128)(2,1)} %cot.1) | copy-start | bytes 786436
  138.5 11.9 %collective-permute-start.34 = (bf16[4,1,256,256]{3,2,1,0:T(8,128)(2,1)S(1)}, bf16[4,1,256,256]{3,2,1,0:T(8,128)(2,1)S(1)}, u32[]{:S(2)}, u32[]{:S(2)}) collective-permute-start(bf16[4,1,256,256]{3,2,1,0:T(8,128)(2,1)S(1)} %pad_maximum_fusion.2.refs_0_), channel_id=1, source_target_pairs={{0,4},{2,6},{4,0},{6,2},{8,12},{10,14},{12,8},{14,10},{16,20},{18,... | collective-permute-start | bytes 1572872 | tf_op jit(solution)/shard_map/ppermute | solution.py:21
  141.1 7.7 %collective-permute-start.12 = (f32[1,512]{1,0:T(1,128)S(1)}, f32[1,512]{1,0:T(1,128)S(1)}, u32[]{:S(2)}, u32[]{:S(2)}) collective-permute-start(f32[1,512]{1,0:T(1,128)S(1)} %get-tuple-element.149), channel_id=1, source_target_pairs={{0,1},{1,0},{2,3},{3,2},{4,5},{5,4},{6,7},{7,6},{8,9},{9,8},{10,11... | collective-permute-start | bytes 6152 | tf_op jit(solution)/shard_map/ppermute | solution.py:21
  149.4 4.9 %collective-permute-start.33 = (bf16[4,1,256,256]{3,2,1,0:T(8,128)(2,1)S(1)}, bf16[4,1,256,256]{3,2,1,0:T(8,128)(2,1)S(1)}, u32[]{:S(2)}, u32[]{:S(2)}) collective-permute-start(bf16[4,1,256,256]{3,2,1,0:T(8,128)(2,1)S(1)} %pad_maximum_fusion.2.refs_0_), channel_id=1, source_target_pairs={{0,2},{2,0},{4,6},{6,4},{8,10},{10,8},{12,14},{14,12},{16,18},{18,... | collective-permute-start | bytes 1572872 | tf_op jit(solution)/shard_map/ppermute | solution.py:21
  150.4 3.9 %collective-permute-start.35 = (bf16[4,1,256,256]{3,2,1,0:T(8,128)(2,1)S(1)}, bf16[4,1,256,256]{3,2,1,0:T(8,128)(2,1)S(1)}, u32[]{:S(2)}, u32[]{:S(2)}) collective-permute-start(bf16[4,1,256,256]{3,2,1,0:T(8,128)(2,1)S(1)} %collective-permute-done.34.refs_2_), channel_id=1, source_target_pairs={{0,2},{2,0},{4,6},{6,4},{8,10},{10,8},{12,14},{14,12},{16,18},{18,... | collective-permute-start | bytes 1572872 | tf_op jit(solution)/shard_map/ppermute | solution.py:21
  (11 other events, 12.2 us)

commit v4 on v3

--- a/solution.py
+++ b/solution.py
@@ -13,7 +13,7 @@
 F32 = jnp.float32
 BF16 = jnp.bfloat16
 VM = 1.5
-UNIT = 3e9
+UNIT = 1.1e9
 
 
 def exchange(array, axis, bit):
@@ -76,7 +76,18 @@
     return (jax.ShapeDtypeStruct(shape, dtype), spec)
 
 
-def run(body, name, device, ins, outs, steps, scratch=(), us=1.0, pull=False):
+def run(body, name, device, ins, outs, steps, scratch=(), us=1.0, after=None):
+    ins, outs = list(ins), list(outs)
+    count, made = len(ins), len(outs)
+    if after is not None:
+        ins.append(whole(after))
+    outs.append(out_whole((8, 128), F32))
+    skip = len(ins)
+
+    def ordered(dev, *refs):
+        refs[skip + made][...] = jnp.zeros((8, 128), F32)
+        body(dev, *refs[:count], *refs[skip : skip + made], *refs[skip + made + 1 :])
+
     total = sum(a.size * a.dtype.itemsize for a, _ in ins)
     total += sum(s.size * s.dtype.itemsize for s, _ in outs)
     held = 0
@@ -87,28 +98,8 @@
         held += size * (1 if size == array.size * array.dtype.itemsize else 2)
     for buffer in scratch:
         held += buffer.dtype.itemsize * int(np.prod(buffer.shape))
-    if pull:
-        count, inner = len(ins), body
-        scratch = (
-            [pltpu.VMEM(a.shape, a.dtype) for a, _ in ins]
-            + [pltpu.SemaphoreType.DMA((count,))]
-            + list(scratch)
-        )
-        ins = [(a, pl.BlockSpec(memory_space=pltpu.HBM)) for a, _ in ins]
-
-        def body(dev, *refs):
-            held = refs[count + len(outs) :]
-            copies = [
-                pltpu.make_async_copy(refs[i], held[i], held[count].at[i]) for i in range(count)
-            ]
-            for copy in copies:
-                copy.start()
-            for copy in copies:
-                copy.wait()
-            inner(dev, *held[:count], *refs[count : count + len(outs)], *held[count + 1 :])
-
     return pl.pallas_call(
-        body,
+        ordered,
         name=name,
         out_shape=[shape for shape, _ in outs],
         grid_spec=pltpu.PrefetchScalarGridSpec(
@@ -261,6 +252,14 @@
     def span_of(dev):
         return lax.div(dev[0], S * PARTS)
 
+    tokens = {}
+
+    def launch(body, name, *rest, after=None, **options):
+        *results, tokens[name] = run(
+            body, name, *rest, after=tokens.get(after), **options
+        )
+        return results
+
     blocks = [slice(b * T, (b + 1) * T) for b in range(S)]
 
     hidden = [hidden_in] + [exchange(hidden_in, "shard", j) for j in range(1, S)]
@@ -298,13 +297,11 @@
         lane = iota((1, width), 1) // HS
         return [jnp.where(lane == g, 1.0, 0.0) for g in range(group)]
 
-    def segments(dev, ln, ow, st, hid, cot, *refs):
+    def segments(dev, ln, ow, st, cot, *refs):
         given, refs = refs[:4], refs[4:]
-        mask_r, cols_r, mine_r, cot_r = refs[:4]
-        for source, target in zip(given, refs[4:]):
+        mask_r, cols_r, cot_r = refs[:3]
+        for source, target in zip(given, refs[3:]):
             target[...] = source[...]
-        mine_r[:, 0:D] = hid[...]
-        mine_r[:, D : 2 * D] = cot[...]
         cot_r[...] = cot[...]
         me = me_of(dev)
         base = dev[0] - me
@@ -328,7 +325,7 @@
                 cols = jnp.where(lane == offset, jnp.where(mark, 1.0, 0.0), cols)
             cols_r[blocks[b], :] = cols
 
-    mask, cols, mine_rows, cot_own, own_gain, bc_weight, bc_taps, bc_bias = run(
+    mask, cols, cot_own, own_gain, bc_weight, bc_taps, bc_bias = launch(
         segments,
         "segments",
         device,
@@ -338,7 +335,6 @@
                 lens,
                 owners,
                 starts,
-                hidden_in,
                 cotangent,
                 norm_gain,
                 w_bc,
@@ -349,7 +345,6 @@
         [
             out_whole((R, 128), F32),
             out_whole((R, 128), F32),
-            out_whole((T, 2 * D), BF16),
             out_whole((T, D), BF16),
             out_whole(norm_gain.shape, F32),
             out_whole(w_bc.shape, BF16),
@@ -358,19 +353,17 @@
         ],
         1,
         us=1.5,
-        pull=True,
     )
     if S == 2:
-        gains = [own_gain, exchange(own_gain, "shard", 1)]
+        gains = [own_gain, exchange(norm_gain, "shard", 1)]
     else:
         gains = [lax.all_gather(own_gain, "shard", axis=1, tiled=True)]
-    far_rows = [exchange(mine_rows, "rep", 2)]
 
     def prepare(dev, wbc, tbc, bbc, cols_r, cot, *refs):
         parts, refs = refs[: len(gains)], refs[len(gains) :]
         hid, refs = refs[:S], refs[S:]
-        gain_r, normed_r, pbc_r, pre_r, map_r, cot_r = refs[:6]
-        sends = refs[6:]
+        gain_r, normed_r, pbc_r, pre_r, map_r, cot_r, mine_r = refs[:7]
+        sends = refs[7:]
         me = me_of(dev)
         if S == 2:
             low, high = parts[0][...], parts[1][...]
@@ -394,8 +387,10 @@
             for j in range(1, S):
                 sends[j - 1][blocks[b ^ j], :] = out
         cot_r[...] = cot[...]
-
-    outs = run(
+        mine_r[:, 0:D] = normed_r[blocks[0], :]
+        mine_r[:, D : 2 * D] = cot[...]
+
+    outs = launch(
         prepare,
         "norm_and_maps",
         device,
@@ -407,13 +402,15 @@
             out_whole((R, NB), F32),
             out_whole((R, NB), BF16),
             out_whole((T, D), BF16),
+            out_whole((T, 2 * D), BF16),
         ]
         + [out_whole((R, NB), BF16) for _ in range(1, S)],
         1,
         us=1.0,
     )
-    gain, normed, proj_bc, pre_bc, map_own, cot_own = outs[:6]
-    maps = [map_own] + [exchange(outs[5 + j], "shard", j) for j in range(1, S)]
+    gain, normed, proj_bc, pre_bc, map_own, cot_own, mine_rows = outs[:7]
+    far_rows = [exchange(mine_rows, "rep", 2)]
+    maps = [map_own] + [exchange(outs[6 + j], "shard", j) for j in range(1, S)]
     if S == 2:
         map_a, map_b = maps
     else:
@@ -457,7 +454,7 @@
             pre_r[0, blocks[b], :] = conv_rows(x_r[0, blocks[b], :], tx[...], bx[...], marks)
             cumt_r[0, b] = turned[blocks[b]].T[0:8]
 
-    z, px, pre, y, cum, cum_t, head_rows, skip_rows = run(
+    z, px, pre, y, cum, cum_t, head_rows, skip_rows = launch(
         project,
         "projections",
         device,
@@ -550,7 +547,7 @@
             for j in range(1, S):
                 sends[j - 1][...] = acc[blocks[j], :].astype(BF16)
 
-    outs = run(
+    outs = launch(
         scan_forward,
         "scan_forward",
         device,
@@ -584,8 +581,9 @@
     core, squares, out_own = outs[:3]
     out_sends = outs[3:]
 
-    def mixed_backward(dev, core_r, z_r, gg, cols_r, squares_r, wo, *refs):
+    def mixed_backward(dev, core_r, z_r, gg, cols_r, squares_r, wo, n_r, *refs):
         cot, refs = refs[:S], refs[S:]
+        group_r, refs = refs[0], refs[1:]
         dm_r, sums_r = refs[0], refs[1]
         sends, sums = refs[2 : 1 + S], refs[1 + S]
         c = pl.program_id(0)
@@ -594,6 +592,9 @@
         @pl.when(c == 0)
         def _():
             sums[...] = squares_r[...]
+            group_r[:, 0:D] = n_r[...]
+            for b in range(S):
+                group_r[blocks[b], D : 2 * D] = cot[b][...]
 
         for b in range(S):
             d_mixed = mm_rt(cot[b][...], wo[...]) * cols_r[blocks[b], 0:1]
@@ -611,7 +612,7 @@
                 for j in range(1, S):
                     sends[j - 1][:, blocks[b ^ j]] = turned
 
-    outs = run(
+    outs = launch(
         mixed_backward,
         "mixed_backward",
         device,
@@ -622,26 +623,29 @@
             whole(cols),
             whole(squares),
             rows(w_out, CH, chunk),
+            whole(normed),
         ]
         + [whole(c) for c in cots],
-        [out_chunked((PARTS, R, CH), F32), out_whole((8, R), F32)]
+        [out_whole((R, 2 * D), BF16), out_chunked((PARTS, R, CH), F32), out_whole((8, R), F32)]
         + [out_whole((8, R), F32) for _ in range(1, S)],
         PARTS,
         scratch=[pltpu.VMEM((R, 128), F32)],
         us=1.6,
     )
-    d_mixed, sums_own = outs[:2]
-    sums_all = [sums_own] + [exchange(outs[1 + j], "shard", j) for j in range(1, S)]
-
-    def gate_backward(dev, core_r, z_r, dm_r, gg, cols_r, *refs):
+    group_rows, d_mixed, sums_own = outs[:3]
+    sums_all = [sums_own] + [exchange(outs[2 + j], "shard", j) for j in range(1, S)]
+    group_other = exchange(group_rows, "rep", 1)
+
+    def gate_backward(dev, core_r, z_r, dm_r, gg, cols_r, far_in, *refs):
         parts, refs = refs[:S], refs[S:]
-        both_r = refs[:PARTS]
-        cotz_c, dcore_r, gg_r, rows_r = refs[PARTS:]
+        mixed_r, cotz_r = refs[:PARTS], refs[PARTS : 2 * PARTS]
+        cotz_c, dcore_r, gg_r, rows_r, far_out = refs[2 * PARTS :]
         c = pl.program_id(0)
         lane = iota((T, 128), 1)
 
         @pl.when(c == 0)
         def _():
+            far_out[...] = far_in[...]
             for b in range(S):
                 total = parts[0][:, blocks[b]]
                 for j in range(1, S):
@@ -678,51 +682,31 @@
             @pl.when(c == r)
             def _():
                 for b in range(S):
-                    both_r[r][blocks[b], 0:CH] = mixed_parts[b]
-                    both_r[r][blocks[b], CH : 2 * CH] = cot_parts[b]
-
-    outs = run(
+                    mixed_r[r][blocks[b], :] = mixed_parts[b]
+                    cotz_r[r][blocks[b], :] = cot_parts[b]
+
+    outs = launch(
         gate_backward,
         "gate_backward",
         device,
-        [chunked(core), chunked(z), chunked(d_mixed), columns(gate_gain, CH, chunk), whole(cols)]
+        [chunked(core), chunked(z), chunked(d_mixed), columns(gate_gain, CH, chunk), whole(cols), whole(far_rows[0])]
         + [whole(s) for s in sums_all],
-        [out_whole((R, 2 * CH), BF16) for _ in range(PARTS)]
+        [out_whole((R, CH), BF16) for _ in range(2 * PARTS)]
         + [
             out_chunked((PARTS, R, CH), BF16),
             out_chunked((PARTS, R, CH), BF16),
             out_chunked((PARTS, 8, CH), F32),
             out_whole((R, 128), F32),
+            out_whole((T, 2 * D), BF16),
         ],
         PARTS,
         us=2.2,
     )
-    cotz, d_core, gate_grads, row_scale = outs[PARTS:]
-    both_q = [outs[0]] + [exchange(outs[r], "rep", r) for r in range(1, PARTS)]
-
-    far_rows = far_rows + [exchange(far_rows[0], "shard", j) for j in range(1, S)]
-
-    def plane_rows(dev, gain_r, n_r, *refs):
-        cot, far, out_r = refs[:S], refs[S : 2 * S], refs[2 * S]
-        out_r[0:R, 0:D] = n_r[...]
-        for b in range(S):
-            out_r[blocks[b], D : 2 * D] = cot[b][...]
-            x = far[b][:, 0:D].astype(F32)
-            scale = lax.rsqrt(jnp.mean(x * x, axis=1, keepdims=True) + epsilon)
-            at = slice(R + b * T, R + (b + 1) * T)
-            out_r[at, 0:D] = (x * scale * gain_r[...]).astype(BF16)
-            out_r[at, D : 2 * D] = far[b][:, D : 2 * D]
-
-    (plane,) = run(
-        plane_rows,
-        "plane_rows",
-        device,
-        [whole(a) for a in (gain, normed, *cots, *far_rows)],
-        [out_whole((2 * R, 2 * D), BF16)],
-        1,
-        us=1.0,
-    )
-    planes = [plane, exchange(plane, "rep", 1)]
+    cotz, d_core, gate_grads, row_scale, far_own = outs[2 * PARTS :]
+    mixed_q = [outs[0]] + [exchange(outs[r], "rep", r) for r in range(1, PARTS)]
+    cotz_q = [outs[PARTS]] + [exchange(outs[PARTS + r], "rep", r) for r in range(1, PARTS)]
+
+    far_rows = [far_own] + [exchange(far_own, "shard", j) for j in range(1, S)]
 
     half_parts = PARTS // 2
 
@@ -871,7 +855,7 @@
         else:
             outs += [out_whole((S, T, T), F32)]
             scratch = [square, square]
-        return run(
+        return launch(
             partial(scan_backward, last),
             "scan_backward_near" if last else "scan_backward_far",
             device,
@@ -880,16 +864,178 @@
             half_parts,
             scratch=scratch,
             us=5.0,
+            after="plane_rows" if last else "gate_backward",
         )
 
     far = half_backward(False, None)
     cotx_far = [exchange(far[r], "rep", half_parts + r) for r in range(half_parts)]
+    def plane_rows(dev, *refs):
+        for b in range(S):
+            refs[S][blocks[b], :] = refs[b][...]
+
+    (far_group,) = launch(
+        plane_rows,
+        "plane_rows",
+        device,
+        [whole(a) for a in far_rows],
+        [out_whole((R, 2 * D), BF16)],
+        1,
+        us=0.5,
+        after="scan_backward_far",
+    )
+    planes = [group_rows, group_other, far_group, exchange(far_group, "rep", 1)]
+
     near = half_backward(True, far[half_parts + 4])
     cotx_q = [near[0], exchange(near[1], "rep", 1)] + cotx_far
     halves = [near[half_parts : half_parts + 4], far[half_parts : half_parts + 4]]
-    token = near[half_parts + 3]
     d_map_own = near[half_parts + 4]
     d_map_other = [exchange(near[half_parts + 4 + j], "shard", j) for j in range(1, S)]
+
+    def split_specs(shape):
+        half = spans // 2
+        send = pl.BlockSpec((1,) + shape, lambda i, dev: (jnp.minimum(i, half - 1), 0, 0, 0))
+        keep = pl.BlockSpec((1,) + shape, lambda i, dev: (jnp.maximum(i - half, 0), 0, 0, 0))
+        return [
+            (jax.ShapeDtypeStruct((half,) + shape, BF16), send),
+            (jax.ShapeDtypeStruct((half,) + shape, F32), keep),
+        ]
+
+    def relative(i):
+        half = spans // 2
+        return jnp.where(i < half, 2 * i + 1, 2 * (i - half))
+
+    def by_span(array, side):
+        def at(i, dev):
+            return (0, side * spans + (span_of(dev) ^ relative(i)))
+
+        return (array, pl.BlockSpec((array.shape[0], DCH), at))
+
+    def store_split(value, slot, send_r, keep_r):
+        i = pl.program_id(0)
+
+        @pl.when(i < spans // 2)
+        def _():
+            send_r[0, slot] = value.astype(BF16)
+
+        @pl.when(i >= spans // 2)
+        def _():
+            keep_r[0, slot] = value
+
+    def weight_grad(dev, *refs):
+        value = jnp.zeros((CH, DCH), F32)
+        for r in range(PARTS):
+            value = value + mm_lt(refs[r][...], refs[PARTS + r][...])
+        store_split(value, 0, *refs[2 * PARTS :])
+
+    def add_stage(dev, total, recv, *refs):
+        count = total.shape[0]
+        for i in range(count):
+            value = total[i] + recv[i].astype(F32)
+            if count == 1:
+                refs[0][0] = value.astype(BF16)
+            elif i % 2 == 0:
+                refs[0][i // 2] = value
+            else:
+                refs[1][i // 2] = value.astype(BF16)
+
+    def join_stage(dev, held, recv, out_r):
+        count = held.shape[0]
+        out_r[0:count] = held[...]
+        out_r[count : 2 * count] = recv[...]
+
+    def sum_spans(label, send, total):
+        bit, stage, held = PARTS, 0, None
+        while held is None:
+            recv = exchange(send, "rep", bit)
+            after = yield label, stage, None
+            shape = (max(total.shape[0] // 2, 1),) + total.shape[1:]
+            more = total.shape[0] > 1
+            outs = launch(
+                add_stage,
+                f"{label}_{stage}",
+                device,
+                [whole(total), whole(recv)],
+                [out_whole(shape, F32), out_whole(shape, BF16)] if more else [out_whole(shape, BF16)],
+                1,
+                us=0.5,
+                after=after,
+            )
+            stage += 1
+            if more:
+                total, send = outs
+                bit *= 2
+            else:
+                held = outs[0]
+        while bit >= PARTS:
+            recv = exchange(held, "rep", bit)
+            after = yield label, stage, None
+            shape = (2 * held.shape[0],) + held.shape[1:]
+            (held,) = launch(
+                join_stage,
+                f"{label}_{stage}",
+                device,
+                [whole(held), whole(recv)],
+                [out_whole(shape, BF16)],
+                1,
+                us=0.5,
+                after=after,
+            )
+            stage += 1
+            bit //= 2
+        far = exchange(held, "rep", 2)
+        yield label, stage, [held, exchange(held, "rep", 1), far, exchange(far, "rep", 1)]
+
+    def reversed_bits(i):
+        result = jnp.int32(0) * i
+        count = spans.bit_length() - 1
+        for b in range(count):
+            result = result | (((i >> b) & 1) << (count - 1 - b))
+        return result
+
+    def in_spec(name=None):
+        def at(i, dev):
+            return (span_of(dev) ^ reversed_bits(i), 0)
+
+        return (jax.ShapeDtypeStruct((D, C), F32), pl.BlockSpec((DCH, C), at))
+
+    def out_spec():
+        def at(i, dev):
+            return (0, span_of(dev) ^ reversed_bits(i))
+
+        return (jax.ShapeDtypeStruct((C, D), F32), pl.BlockSpec((C, DCH), at))
+
+    def join_out(dev, *refs):
+        mine = part_of(dev)
+        for m in range(PARTS):
+
+            @pl.when(mine == m)
+            def _():
+                for r in range(PARTS):
+                    at = slice((m ^ r) * CH, ((m ^ r) + 1) * CH)
+                    refs[PARTS][at, :] = refs[r][0, 0].astype(F32)
+
+    def join_x(dev, *refs):
+        mine = part_of(dev)
+        for m in range(PARTS):
+
+            @pl.when(mine == m)
+            def _():
+                for r in range(PARTS):
+                    at = slice((m ^ r) * CH, ((m ^ r) + 1) * CH)
+                    refs[PARTS][:, at] = refs[r][0, 0].astype(F32).T
+
+    send_out, keep_out = launch(
+        weight_grad,
+        "out_weight_grad",
+        device,
+        [whole(c) for c in mixed_q] + [by_span(p, 1) for p in planes],
+        split_specs((1, CH, DCH)),
+        spans,
+        us=2.0,
+        after="scan_backward_near",
+    )
+    chains = {"out": sum_spans("out", send_out, keep_out)}
+    next(chains["out"])
 
     def input_backward(dev, cz, near_x, far_x, near_dt, far_dt, wz, wx, wdt, dn_r, dt_r):
         c = pl.program_id(0)
@@ -920,7 +1066,7 @@
 
         return (array, pl.BlockSpec((1,) + array.shape[1:], at))
 
-    d_normed, cot_dt_all = run(
+    d_normed, cot_dt_all = launch(
         input_backward,
         "input_backward",
         device,
@@ -937,7 +1083,21 @@
         [out_whole((R, D), F32), out_whole((R, 128), BF16)],
         PARTS,
         us=3.0,
-    )
+        after="out_weight_grad",
+    )
+
+    send_z, keep_z = launch(
+        weight_grad,
+        "z_weight_grad",
+        device,
+        [whole(c) for c in cotz_q] + [by_span(p, 0) for p in planes],
+        split_specs((1, CH, DCH)),
+        spans,
+        us=2.0,
+        after="input_backward",
+    )
+    chains["z"] = sum_spans("z", send_z, keep_z)
+    next(chains["z"])
 
     small_half = -(-(NB + H + 15) // 32) * 16
 
@@ -1000,7 +1160,7 @@
         pack_keep[...] = pack_r[pl.ds(keep_at, small_half), :]
         pack_send[...] = pack_r[pl.ds(send_at, small_half), :].astype(BF16)
 
-    outs = run(
+    outs = launch(
         maps_backward,
         "maps_backward",
         device,
@@ -1039,9 +1199,32 @@
             pltpu.VMEM((2 * small_half, D), F32),
         ],
         us=3.0,
+        after="z_weight_grad",
     )
     dn_own, pack, pack_send = outs[:3]
     dn_other = [exchange(outs[2 + j], "shard", j) for j in range(1, S)]
+
+    chains["out"].send("maps_backward")
+    send_x, keep_x = launch(
+        weight_grad,
+        "x_weight_grad",
+        device,
+        [whole(c) for c in cotx_q] + [by_span(p, 0) for p in planes],
+        split_specs((1, CH, DCH)),
+        spans,
+        us=2.0,
+        after="out_0",
+    )
+    chains["x"] = sum_spans("x", send_x, keep_x)
+    next(chains["x"])
+    stages = 2 * (spans.bit_length() - 1)
+    turns = [(3 * k, "out") for k in range(1, stages)]
+    turns += [(3 * k + 2, "z") for k in range(stages)]
+    turns += [(3 * k + 4, "x") for k in range(stages)]
+    pieces, last = {}, "x_weight_grad"
+    for _, label in sorted(turns):
+        _, stage, pieces[label] = chains[label].send(last)
+        last = f"{label}_{stage - 1}"
 
     def own_rows(dev, hid, cot, cols_r, rows_r, gain_r, dn_r, out_r, *refs):
         others, refs = refs[: S - 1], refs[S - 1 :]
@@ -1060,7 +1243,7 @@
         dot = jnp.mean(u * x, axis=1, keepdims=True)
         grad_r[...] = used * cot[...].astype(F32) + scale * u - x * (scale * scale * scale * dot)
 
-    hidden_out, grad_hidden = run(
+    hidden_out, grad_hidden = launch(
         own_rows,
         "own_rows",
         device,
@@ -1073,154 +1256,38 @@
         + [whole(a) for a in (gain, dn_own, out_own, *dn_other)],
         [out_whole((T, D), F32), out_whole((T, D), F32)],
         1,
-    )
-
-    def split_specs(shape):
-        half = spans // 2
-        send = pl.BlockSpec((1,) + shape, lambda i, dev: (jnp.minimum(i, half - 1), 0, 0, 0))
-        keep = pl.BlockSpec((1,) + shape, lambda i, dev: (jnp.maximum(i - half, 0), 0, 0, 0))
-        return [
-            (jax.ShapeDtypeStruct((half,) + shape, BF16), send),
-            (jax.ShapeDtypeStruct((half,) + shape, F32), keep),
-        ]
-
-    def relative(i):
-        half = spans // 2
-        return jnp.where(i < half, 2 * i + 1, 2 * (i - half))
-
-    def by_span(array, side):
-        def at(i, dev):
-            return (0, side * spans + (span_of(dev) ^ relative(i)))
-
-        return (array, pl.BlockSpec((array.shape[0], DCH), at))
-
-    def four(refs):
-        ends = (slice(0, R), slice(R, 2 * R))
-        return [refs[0][ends[0], :], refs[1][ends[0], :], refs[0][ends[1], :], refs[1][ends[1], :]]
-
-    def store_split(value, slot, send_r, keep_r):
-        i = pl.program_id(0)
-
-        @pl.when(i < spans // 2)
-        def _():
-            send_r[0, slot] = value.astype(BF16)
-
-        @pl.when(i >= spans // 2)
-        def _():
-            keep_r[0, slot] = value
-
-    def pair_weight_grad(dev, *refs):
-        both, norm, cot = refs[:PARTS], four(refs[PARTS:]), four(refs[PARTS + 2 :])
-        value = jnp.zeros((CH, DCH), F32)
-        other = jnp.zeros((CH, DCH), F32)
-        for r in range(PARTS):
-            value = value + mm_lt(both[r][:, 0:CH], cot[r])
-            other = other + mm_lt(both[r][:, CH : 2 * CH], norm[r])
-        store_split(value, 0, *refs[-2:])
-        store_split(other, 1, *refs[-2:])
-
-    def x_weight_grad(dev, *refs):
-        value = jnp.zeros((CH, DCH), F32)
-        norm = four(refs[PARTS:])
-        for r in range(PARTS):
-            value = value + mm_lt(refs[r][...], norm[r])
-        store_split(value, 0, *refs[-2:])
-
-    def sum_spans(send, keep):
-        bit = PARTS
-        total = keep + exchange(send, "rep", bit).astype(F32)
-        while total.shape[0] > 1:
-            bit *= 2
-            send = total[1::2].astype(BF16)
-            total = total[0::2] + exchange(send, "rep", bit).astype(F32)
-        held = total.astype(BF16)
-        while bit >= PARTS:
-            held = jnp.concatenate([held, exchange(held, "rep", bit)], axis=0)
-            bit //= 2
-        far = exchange(held, "rep", 2)
-        return [held, exchange(held, "rep", 1), far, exchange(far, "rep", 1)]
-
-    def reversed_bits(i):
-        result = jnp.int32(0) * i
-        count = spans.bit_length() - 1
-        for b in range(count):
-            result = result | (((i >> b) & 1) << (count - 1 - b))
-        return result
-
-    def in_spec(name=None):
-        def at(i, dev):
-            return (span_of(dev) ^ reversed_bits(i), 0)
-
-        return (jax.ShapeDtypeStruct((D, C), F32), pl.BlockSpec((DCH, C), at))
-
-    def out_spec():
-        def at(i, dev):
-            return (0, span_of(dev) ^ reversed_bits(i))
-
-        return (jax.ShapeDtypeStruct((C, D), F32), pl.BlockSpec((C, DCH), at))
-
-    def join_pair(dev, *refs):
-        mine = part_of(dev)
-        for m in range(PARTS):
-
-            @pl.when(mine == m)
-            def _():
-                for r in range(PARTS):
-                    at = slice((m ^ r) * CH, ((m ^ r) + 1) * CH)
-                    refs[PARTS][at, :] = refs[r][0, 0].astype(F32)
-                    refs[PARTS + 1][:, at] = refs[r][0, 1].astype(F32).T
-        refs[PARTS + 2][...] = jnp.zeros((8, 128), F32)
-
-    def join_x(dev, *refs):
-        mine = part_of(dev)
-        for m in range(PARTS):
-
-            @pl.when(mine == m)
-            def _():
-                for r in range(PARTS):
-                    at = slice((m ^ r) * CH, ((m ^ r) + 1) * CH)
-                    refs[PARTS + 1][:, at] = refs[r][0, 0].astype(F32).T
-
-    send, keep = run(
-        pair_weight_grad,
-        "pair_weight_grad",
-        device,
-        [whole(b) for b in both_q]
-        + [by_span(p, 0) for p in planes]
-        + [by_span(p, 1) for p in planes]
-        + [whole(token)],
-        split_specs((2, CH, DCH)),
+        after="maps_backward",
+    )
+
+    (grad_out,) = launch(
+        join_out,
+        "join_out",
+        device,
+        [chunked(p) for p in pieces["out"]],
+        [out_spec()],
         spans,
-        us=5.0,
-    )
-    pieces = sum_spans(send, keep)
-    grad_out, grad_z, joined = run(
-        join_pair,
-        "join_pair",
-        device,
-        [chunked(p) for p in pieces],
-        [out_spec(), in_spec(), out_whole((8, 128), F32)],
-        spans,
-        us=6.0,
-    )
-    send, keep = run(
-        x_weight_grad,
-        "x_weight_grad",
-        device,
-        [whole(c) for c in cotx_q] + [by_span(p, 0) for p in planes],
-        split_specs((1, CH, DCH)),
-        spans,
-        us=2.5,
-    )
-    pieces = sum_spans(send, keep)
-    (grad_x,) = run(
+        us=4.0,
+        after=last,
+    )
+    (grad_z,) = launch(
         join_x,
-        "join_x",
-        device,
-        [chunked(p) for p in pieces] + [whole(joined)],
+        "join_z",
+        device,
+        [chunked(p) for p in pieces["z"]],
         [in_spec()],
         spans,
         us=4.0,
+        after="join_out",
+    )
+    (grad_x,) = launch(
+        join_x,
+        "join_x",
+        device,
+        [chunked(p) for p in pieces["x"]],
+        [in_spec()],
+        spans,
+        us=4.0,
+        after="join_z",
     )
 
     pack = pack + exchange(pack_send, "rep", 1).astype(F32)
@@ -1259,7 +1326,7 @@
                     lanes = slice((m ^ j) * (D // S), ((m ^ j) + 1) * (D // S))
                     refs[10 + j][...] = pack_r[at + 14 : at + 15, lanes]
 
-    outs = run(
+    outs = launch(
         unpack,
         "unpack",
         device,

time: 157 us -> 154 us (0.981)
  waiting for transfers between devices: 73.6 us -> 50 us
  starting transfers between devices: 36.6 us -> 53.3 us
  Pallas kernels: 37.5 us -> 42.7 us
    ppermute x36 -> x47, waiting for transfers between devices: 73.6 us -> 50 us  [exchange(): return lax.ppermute(array, axis, [(i, i ^ bit) for i in range(count)])]
    ppermute x36 -> x47, starting transfers between devices: 36.6 us -> 53.3 us  [exchange(): return lax.ppermute(array, axis, [(i, i ^ bit) for i in range(count)])]
    pallas_call x17 -> x31, Pallas kernels: 37.5 us -> 42.7 us  [run(): pl.pallas_call(ordered, name=name, out_shape=[shape for shape, _ in outs]...]
    unnamed x46 -> x44, local copies, waits for them, and re-layouts: 6.98 us -> 6.29 us
  transfers between devices with their start and end apart: 36 -> 47, of which waited for: 14 -> 14; matrix products, arithmetic and copies ran while one was open for 1% -> 0% of each run, Pallas kernels for 20% -> 23%
where the time goes in v4:
time: 154 us
  starting transfers between devices  53.3 us (35%)
  waiting for transfers between devices  50 us (32%)
  Pallas kernels  42.7 us (28%)
  local copies, waits for them, and re-layouts  6.29 us (4%)
    ppermute x47, starting transfers between devices, exchange(): return lax.ppermute(array, axis, [(i, i ^ bit) for i in range(count)])  53.3 us
    ppermute x47, waiting for transfers between devices, exchange(): return lax.ppermute(array, axis, [(i, i ^ bit) for i in range(count)])  50 us
    pallas_call x31, Pallas kernels, run(): pl.pallas_call(ordered, name=name, out_shape=[shape for shape, _ in outs]...  42.7 us
    unnamed x44, local copies, waits for them, and re-layouts  6.29 us
  transfers between devices with their start and end apart: 47, of which 14 were waited for; matrix products, arithmetic and copies ran while one was open for 0% of the time, Pallas kernels for 23%

profile of v4, /device:TPU:0, one launch (start us, length us, event | category | flops | bytes accessed | tf_op | source)
XLA Modules:
  0.0 154.1 jit_solution(12218463553039179116)
XLA Ops:
  0.6 3.0 %collective-permute-start.1 = (bf16[128,1024]{1,0:T(8,128)(2,1)}, bf16[128,1024]{1,0:T(8,128)(2,1)S(1)}, u32[]{:S(2)}, u32[]{:S(2)}) collective-permute-start(bf16[128,1024]{1,0:T(8,128)(2,1)} %refs_0_.1), channel_id=1, source_target_pairs={{0,1},{1,0},{2,3},{3,2},{4,5},{5,4},{6,7},{7,6},{8,9},{9,8},{10,11... | collective-permute-start | bytes 786440 | tf_op jit(solution)/shard_map/ppermute | solution.py:21
  11.7 1.9 %collective-permute-start.2 = (bf16[256,128]{1,0:T(8,128)(2,1)S(1)}, bf16[256,128]{1,0:T(8,128)(2,1)S(1)}, u32[]{:S(2)}, u32[]{:S(2)}) collective-permute-start(bf16[256,128]{1,0:T(8,128)(2,1)S(1)} %get-tuple-element.150), channel_id=1, source_target_pairs={{0,1},{1,0},{2,3},{3,2},{4,5},{5,4},{6,7},{7,6},{8,9},{9,8},{10,11... | collective-permute-start | bytes 196616 | tf_op jit(solution)/shard_map/ppermute | solution.py:21
  13.8 1.9 %collective-permute-start.4 = (bf16[128,2048]{1,0:T(8,128)(2,1)S(1)}, bf16[128,2048]{1,0:T(8,128)(2,1)S(1)}, u32[]{:S(2)}, u32[]{:S(2)}) collective-permute-start(bf16[128,2048]{1,0:T(8,128)(2,1)S(1)} %get-tuple-element.163), channel_id=1, source_target_pairs={{0,4},{2,6},{4,0},{6,2},{8,12},{10,14},{12,8},{14,10},{16,20},{18,... | collective-permute-start | bytes 1572872 | tf_op jit(solution)/shard_map/ppermute | solution.py:21
  15.8 3.9 %projections.1 = (f32[4,256,256]{2,1,0:T(8,128)S(1)}, f32[4,256,256]{2,1,0:T(8,128)S(1)}, f32[4,256,256]{2,1,0:T(8,128)S(1)}, f32[4,256,128]{2,1,0:T(8,128)S(1)}...) custom-call(s32[1]{0:T(128)} %bitcast.dev, ...), custom_call_target="tpu_custom_call" | custom-call | flops 4400000000 | bytes 9183424 | tf_op jit(solution)/shard_map/projections/pallas_call | solution.py:101
  19.7 4.0 %scan_forward.1 = (f32[4,256,256]{2,1,0:T(8,128)S(1)}, f32[256,128]{1,0:T(8,128)S(1)}, f32[128,1024]{1,0:T(8,128)S(1)}, bf16[128,1024]{1,0:T(8,128)(2,1)S(1)}, f32[8,128]{1,0:T(8,128)}) custom-call(s32[1]{0:T(128)} %bitcast.dev, bf16[256,128]{1,0:T(8,128)(2,1)S(1)} %get-tuple-element.149.refs_0_, bf16[256,128]{1,0:T(8,128)(2,1)S(1)} %collective-permute-done.2.refs_1_, ...), custom_call_target="tpu_custom_call" | custom-call | flops 4400000000 | bytes 7544832 | tf_op jit(solution)/shard_map/scan_forward/pallas_call | solution.py:101
  23.7 3.1 %mixed_backward.1 = (bf16[256,2048]{1,0:T(8,128)(2,1)S(1)}, f32[4,256,256]{2,1,0:T(8,128)S(1)}, f32[8,256]{1,0:T(8,128)S(1)}, f32[8,256]{1,0:T(8,128)S(1)}, f32[8,128]{1,0:T(8,128)}) custom-call(s32[1]{0:T(128)} %bitcast.dev, f32[4,256,256]{2,1,0:T(8,128)S(1)} %get-tuple-element.159.refs_0_.refs_11_, f32[4,256,256]{2,1,0:T(8,128)S(1)} %get-tuple-element.158.refs_9_.refs_1_, ...), custom_call_target="tpu_custom_call" | custom-call | flops 1760000000 | bytes 7626752 | tf_op jit(solution)/shard_map/mixed_backward/pallas_call | solution.py:101
  26.8 1.5 collective-permute-start.5
  28.3 2.1 %collective-permute-done.5.refs_7_ = f32[8,256]{1,0:T(8,128)S(1)} collective-permute-done((f32[8,256]{1,0:T(8,128)S(1)}, f32[8,256]{1,0:T(8,128)S(1)}, u32[]{:S(2)}, u32[]{:S(2)}) %collective-permute-start.5) | collective-permute-done | bytes 8224 | tf_op jit(solution)/shard_map/ppermute | solution.py:21
  30.4 1.6 %gate_backward.1 = (bf16[256,256]{1,0:T(8,128)(2,1)S(1)}, bf16[256,256]{1,0:T(8,128)(2,1)S(1)}, bf16[256,256]{1,0:T(8,128)(2,1)S(1)}, bf16[256,256]{1,0:T(8,128)...) custom-call(s32[1]{0:T(128)} %bitcast.dev, ...), custom_call_target="tpu_custom_call" | custom-call | flops 2420000000 | bytes 6610944 | tf_op jit(solution)/shard_map/gate_backward/pallas_call | solution.py:101
  32.0 1.6 %collective-permute-start.6 = (bf16[128,2048]{1,0:T(8,128)(2,1)S(1)}, bf16[128,2048]{1,0:T(8,128)(2,1)S(1)}, u32[]{:S(2)}, u32[]{:S(2)}) collective-permute-start(bf16[128,2048]{1,0:T(8,128)(2,1)S(1)} %get-tuple-element.173.refs_0_), channel_id=1, source_target_pairs={{0,1},{1,0},{2,3},{3,2},{4,5},{5,4},{6,7},{7,6},{8,9},{9,8},{10,11... | collective-permute-start | bytes 1572872 | tf_op jit(solution)/shard_map/ppermute | solution.py:21
  33.6 3.5 %scan_backward_far.1 = (bf16[256,256]{1,0:T(8,128)(2,1)S(1)}, bf16[256,256]{1,0:T(8,128)(2,1)S(1)}, bf16[2,256,256]{2,1,0:T(8,128)(2,1)S(1)}, f32[2,256,128]{2,1...) custom-call(s32[1]{0:T(128)} %bitcast.dev, ...), custom_call_target="tpu_custom_call" | custom-call | flops 5500000256 | bytes 6160384 | tf_op jit(solution)/shard_map/scan_backward_far/pallas_call | solution.py:101
  37.1 6.1 %collective-permute-done.6.refs_1_ = bf16[128,2048]{1,0:T(8,128)(2,1)S(1)} collective-permute-done((bf16[128,2048]{1,0:T(8,128)(2,1)S(1)}, bf16[128,2048]{1,0:T(8,128)(2,1)S(1)}, u32[]{:S(2)}, u32[]{:S(2)}) %collective-permute-start.6) | collective-permute-done | bytes 524320 | tf_op jit(solution)/shard_map/ppermute | solution.py:21
  45.3 3.6 %scan_backward_near.1 = (bf16[256,256]{1,0:T(8,128)(2,1)S(1)}, bf16[256,256]{1,0:T(8,128)(2,1)S(1)}, bf16[2,256,256]{2,1,0:T(8,128)(2,1)S(1)}, f32[2,256,128]{2,...) custom-call(s32[1]{0:T(128)} %bitcast.dev, ...), custom_call_target="tpu_custom_call" | custom-call | flops 5500000256 | bytes 6356992 | tf_op jit(solution)/shard_map/scan_backward_near/pallas_call | solution.py:101
  52.2 1.5 collective-permute-start.12
  53.7 2.0 %out_weight_grad.1 = (bf16[2,1,256,256]{3,2,1,0:T(8,128)(2,1)S(1)}, f32[2,1,256,256]{3,2,1,0:T(8,128)S(1)}, f32[8,128]{1,0:T(8,128)S(1)}) custom-call(s32[1]{0:T(128)} %bitcast.dev, bf16[256,256]{1,0:T(8,128)(2,1)S(1)} %get-tuple-element.184.refs_0_, bf16[256,256]{1,0:T(8,128)(2,1)S(1)} %collective-permute-done.7.refs_1_, ...), custom_call_target="tpu_custom_call" | custom-call | flops 2200000000 | bytes 5513216 | tf_op jit(solution)/shard_map/out_weight_grad/pallas_call | solution.py:101
  55.8 3.1 %input_backward.1 = (f32[256,1024]{1,0:T(8,128)S(1)}, bf16[256,128]{1,0:T(8,128)(2,1)S(1)}, f32[8,128]{1,0:T(8,128)S(1)}) custom-call(s32[1]{0:T(128)} %bitcast.dev, bf16[4,256,256]{2,1,0:T(8,128)(2,1)S(1)} %get-tuple-element.179.refs_0_, bf16[2,256,256]{2,1,0:T(8,128)(2,1)S(1)} %get-tuple-element.180.refs_1_, ...), custom_call_target="tpu_custom_call" | custom-call | flops 3300000000 | bytes 6922240 | tf_op jit(solution)/shard_map/input_backward/pallas_call | solution.py:101
  58.9 2.0 %z_weight_grad.1 = (bf16[2,1,256,256]{3,2,1,0:T(8,128)(2,1)S(1)}, f32[2,1,256,256]{3,2,1,0:T(8,128)S(1)}, f32[8,128]{1,0:T(8,128)S(1)}) custom-call(s32[1]{0:T(128)} %bitcast.dev, bf16[256,256]{1,0:T(8,128)(2,1)S(1)} %get-tuple-element.201.refs_0_, bf16[256,256]{1,0:T(8,128)(2,1)S(1)} %collective-permute-done.13.refs_1_, ...), custom_call_target="tpu_custom_call" | custom-call | flops 2200000000 | bytes 5513216 | tf_op jit(solution)/shard_map/z_weight_grad/pallas_call | solution.py:101
  61.0 1.1 maps_backward.1
  62.2 1.6 %collective-permute-start.27 = (bf16[2,1,256,256]{3,2,1,0:T(8,128)(2,1)S(1)}, bf16[2,1,256,256]{3,2,1,0:T(8,128)(2,1)S(1)}, u32[]{:S(2)}, u32[]{:S(2)}) collective-permute-start(bf16[2,1,256,256]{3,2,1,0:T(8,128)(2,1)S(1)} %get-tuple-element.224), channel_id=1, source_target_pairs={{0,8},{2,10},{4,12},{6,14},{8,0},{10,2},{12,4},{14,6},{16,24},{18,... | collective-permute-start | bytes 786440 | tf_op jit(solution)/shard_map/ppermute | solution.py:21
  63.8 1.4 collective-permute-start.25
  66.5 4.9 %collective-permute-done.27.refs_1_ = bf16[2,1,256,256]{3,2,1,0:T(8,128)(2,1)S(1)} collective-permute-done((bf16[2,1,256,256]{3,2,1,0:T(8,128)(2,1)S(1)}, bf16[2,1,256,256]{3,2,1,0:T(8,128)(2,1)S(1)}, u32[]{:S(2)}, u32[]{:S(2)}) %collective-permute-start.27) | collective-permute-done | bytes 262176 | tf_op jit(solution)/shard_map/ppermute | solution.py:21
  71.4 1.4 collective-permute-start.18
  72.8 2.7 %collective-permute-start.30 = (bf16[1,1,256,256]{3,2,1,0:T(8,128)(2,1)S(1)}, bf16[1,1,256,256]{3,2,1,0:T(8,128)(2,1)S(1)}, u32[]{:S(2)}, u32[]{:S(2)}) collective-permute-start(bf16[1,1,256,256]{3,2,1,0:T(8,128)(2,1)S(1)} %get-tuple-element.232), channel_id=1, source_target_pairs={{0,16},{2,18},{4,20},{6,22},{8,24},{10,26},{12,28},{14,30},{16,0},... | collective-permute-start | bytes 393224 | tf_op jit(solution)/shard_map/ppermute | solution.py:21
  75.5 2.0 %x_weight_grad.1 = (bf16[2,1,256,256]{3,2,1,0:T(8,128)(2,1)S(1)}, f32[2,1,256,256]{3,2,1,0:T(8,128)S(1)}, f32[8,128]{1,0:T(8,128)S(1)}) custom-call(s32[1]{0:T(128)} %bitcast.dev, bf16[256,256]{1,0:T(8,128)(2,1)S(1)} %get-tuple-element.219.refs_0_, bf16[256,256]{1,0:T(8,128)(2,1)S(1)} %collective-permute-done.24.refs_1_, ...), custom_call_target="tpu_custom_call" | custom-call | flops 2200000000 | bytes 5513216 | tf_op jit(solution)/shard_map/x_weight_grad/pallas_call | solution.py:101
  77.5 1.8 %collective-permute-done.23.refs_1_ = bf16[2,1,256,256]{3,2,1,0:T(8,128)(2,1)S(1)} collective-permute-done((bf16[2,1,256,256]{3,2,1,0:T(8,128)(2,1)S(1)}, bf16[2,1,256,256]{3,2,1,0:T(8,128)(2,1)S(1)}, u32[]{:S(2)}, u32[]{:S(2)}) %collective-permute-start.23) | collective-permute-done | bytes 262176 | tf_op jit(solution)/shard_map/ppermute | solution.py:21
  79.7 2.2 %collective-permute-start.29 = (bf16[2,1,256,256]{3,2,1,0:T(8,128)(2,1)S(1)}, bf16[2,1,256,256]{3,2,1,0:T(8,128)(2,1)S(1)}, u32[]{:S(2)}, u32[]{:S(2)}) collective-permute-start(bf16[2,1,256,256]{3,2,1,0:T(8,128)(2,1)S(1)} %get-tuple-element.230), channel_id=1, source_target_pairs={{0,8},{2,10},{4,12},{6,14},{8,0},{10,2},{12,4},{14,6},{16,24},{18,... | collective-permute-start | bytes 786440 | tf_op jit(solution)/shard_map/ppermute | solution.py:21
  82.4 6.9 %collective-permute-start.19 = (bf16[80,1024]{1,0:T(8,128)(2,1)S(1)}, bf16[80,1024]{1,0:T(8,128)(2,1)S(1)}, u32[]{:S(2)}, u32[]{:S(2)}) collective-permute-start(bf16[80,1024]{1,0:T(8,128)(2,1)S(1)} %add_convert_fusion.2), channel_id=1, source_target_pairs={{0,8},{2,10},{4,12},{6,14},{8,0},{10,2},{12,4},{14,6},{16,24},{18,... | collective-permute-start | bytes 491528 | tf_op jit(solution)/shard_map/ppermute | solution.py:21
  89.3 5.4 %collective-permute-done.29.refs_1_ = bf16[2,1,256,256]{3,2,1,0:T(8,128)(2,1)S(1)} collective-permute-done((bf16[2,1,256,256]{3,2,1,0:T(8,128)(2,1)S(1)}, bf16[2,1,256,256]{3,2,1,0:T(8,128)(2,1)S(1)}, u32[]{:S(2)}, u32[]{:S(2)}) %collective-permute-start.29) | collective-permute-done | bytes 262176 | tf_op jit(solution)/shard_map/ppermute | solution.py:21
  94.8 1.5 collective-permute-start.31
  96.3 1.5 collective-permute-start.32
  97.8 1.6 %collective-permute-start.36 = (bf16[2,1,256,256]{3,2,1,0:T(8,128)(2,1)S(1)}, bf16[2,1,256,256]{3,2,1,0:T(8,128)(2,1)S(1)}, u32[]{:S(2)}, u32[]{:S(2)}) collective-permute-start(bf16[2,1,256,256]{3,2,1,0:T(8,128)(2,1)S(1)} %get-tuple-element.245.refs_0_), channel_id=1, source_target_pairs={{0,8},{2,10},{4,12},{6,14},{8,0},{10,2},{12,4},{14,6},{16,24},{18,... | collective-permute-start | bytes 786440 | tf_op jit(solution)/shard_map/ppermute | solution.py:21
  99.5 2.9 %collective-permute-start.20 = (bf16[80,1024]{1,0:T(8,128)(2,1)S(1)}, bf16[80,1024]{1,0:T(8,128)(2,1)S(1)}, u32[]{:S(2)}, u32[]{:S(2)}) collective-permute-start(bf16[80,1024]{1,0:T(8,128)(2,1)S(1)} %add_convert_fusion.1), channel_id=1, source_target_pairs={{0,16},{2,18},{4,20},{6,22},{8,24},{10,26},{12,28},{14,30},{16,0},... | collective-permute-start | bytes 491528 | tf_op jit(solution)/shard_map/ppermute | solution.py:21
  102.4 8.8 %collective-permute-done.32.refs_1_ = bf16[1,1,256,256]{3,2,1,0:T(8,128)(2,1)S(1)} collective-permute-done((bf16[1,1,256,256]{3,2,1,0:T(8,128)(2,1)S(1)}, bf16[1,1,256,256]{3,2,1,0:T(8,128)(2,1)S(1)}, u32[]{:S(2)}, u32[]{:S(2)}) %collective-permute-start.32) | collective-permute-done | bytes 131104 | tf_op jit(solution)/shard_map/ppermute | solution.py:21
  111.4 3.5 %collective-permute-start.41 = (bf16[4,1,256,256]{3,2,1,0:T(8,128)(2,1)S(1)}, bf16[4,1,256,256]{3,2,1,0:T(8,128)(2,1)S(1)}, u32[]{:S(2)}, u32[]{:S(2)}) collective-permute-start(bf16[4,1,256,256]{3,2,1,0:T(8,128)(2,1)S(1)} %get-tuple-element.250.refs_0_), channel_id=1, source_target_pairs={{0,4},{2,6},{4,0},{6,2},{8,12},{10,14},{12,8},{14,10},{16,20},{18,... | collective-permute-start | bytes 1572872 | tf_op jit(solution)/shard_map/ppermute | solution.py:21
  114.9 1.9 %collective-permute-start.34 = (bf16[2,1,256,256]{3,2,1,0:T(8,128)(2,1)S(1)}, bf16[2,1,256,256]{3,2,1,0:T(8,128)(2,1)S(1)}, u32[]{:S(2)}, u32[]{:S(2)}) collective-permute-start(bf16[2,1,256,256]{3,2,1,0:T(8,128)(2,1)S(1)} %get-tuple-element.243.refs_0_), channel_id=1, source_target_pairs={{0,8},{2,10},{4,12},{6,14},{8,0},{10,2},{12,4},{14,6},{16,24},{18,... | collective-permute-start | bytes 786440 | tf_op jit(solution)/shard_map/ppermute | solution.py:21
  116.9 2.7 %collective-permute-done.35.refs_1_ = bf16[1,1,256,256]{3,2,1,0:T(8,128)(2,1)S(1)} collective-permute-done((bf16[1,1,256,256]{3,2,1,0:T(8,128)(2,1)S(1)}, bf16[1,1,256,256]{3,2,1,0:T(8,128)(2,1)S(1)}, u32[]{:S(2)}, u32[]{:S(2)}) %collective-permute-start.35) | collective-permute-done | bytes 131104 | tf_op jit(solution)/shard_map/ppermute | solution.py:21
  120.7 3.4 %collective-permute-done.34.refs_1_ = bf16[2,1,256,256]{3,2,1,0:T(8,128)(2,1)S(1)} collective-permute-done((bf16[2,1,256,256]{3,2,1,0:T(8,128)(2,1)S(1)}, bf16[2,1,256,256]{3,2,1,0:T(8,128)(2,1)S(1)}, u32[]{:S(2)}, u32[]{:S(2)}) %collective-permute-start.34) | collective-permute-done | bytes 262176 | tf_op jit(solution)/shard_map/ppermute | solution.py:21
  124.1 1.3 collective-permute-start.38
  125.4 2.1 %collective-permute-done.43.refs_1_ = bf16[2,1,256,256]{3,2,1,0:T(8,128)(2,1)S(1)} collective-permute-done((bf16[2,1,256,256]{3,2,1,0:T(8,128)(2,1)S(1)}, bf16[2,1,256,256]{3,2,1,0:T(8,128)(2,1)S(1)}, u32[]{:S(2)}, u32[]{:S(2)}) %collective-permute-start.43) | collective-permute-done | bytes 262176 | tf_op jit(solution)/shard_map/ppermute | solution.py:21
  127.6 2.5 %collective-permute-start.45 = (bf16[4,1,256,256]{3,2,1,0:T(8,128)(2,1)S(1)}, bf16[4,1,256,256]{3,2,1,0:T(8,128)(2,1)S(1)}, u32[]{:S(2)}, u32[]{:S(2)}) collective-permute-start(bf16[4,1,256,256]{3,2,1,0:T(8,128)(2,1)S(1)} %get-tuple-element.256.refs_0_), channel_id=1, source_target_pairs={{0,4},{2,6},{4,0},{6,2},{8,12},{10,14},{12,8},{14,10},{16,20},{18,... | collective-permute-start | bytes 1572872 | tf_op jit(solution)/shard_map/ppermute | solution.py:21
  130.3 1.1 unpack.1
  131.4 3.2 %collective-permute-done.16.refs_7_ = bf16[128,2048]{1,0:T(8,128)(2,1)S(1)} collective-permute-done((bf16[128,2048]{1,0:T(8,128)(2,1)S(1)}, bf16[128,2048]{1,0:T(8,128)(2,1)S(1)}, u32[]{:S(2)}, u32[]{:S(2)}) %collective-permute-start.16) | collective-permute-done | bytes 524320 | tf_op jit(solution)/shard_map/ppermute | solution.py:21
  135.0 3.2 %collective-permute-done.22 = f32[1,512]{1,0:T(1,128)S(1)} collective-permute-done((f32[1,512]{1,0:T(1,128)S(1)}, f32[1,512]{1,0:T(1,128)S(1)}, u32[]{:S(2)}, u32[]{:S(2)}) %collective-permute-start.22) | collective-permute-done | bytes 2080 | tf_op jit(solution)/shard_map/ppermute | solution.py:21
  138.7 1.4 own_rows.1
  140.7 5.4 %collective-permute-done.45.refs_2_ = bf16[4,1,256,256]{3,2,1,0:T(8,128)(2,1)S(1)} collective-permute-done((bf16[4,1,256,256]{3,2,1,0:T(8,128)(2,1)S(1)}, bf16[4,1,256,256]{3,2,1,0:T(8,128)(2,1)S(1)}, u32[]{:S(2)}, u32[]{:S(2)}) %collective-permute-start.45) | collective-permute-done | bytes 524320 | tf_op jit(solution)/shard_map/ppermute | solution.py:21
  146.1 2.5 %join_out.1 = (f32[1024,1024]{1,0:T(8,128)}, f32[8,128]{1,0:T(8,128)S(1)}) custom-call(s32[1]{0:T(128)} %bitcast.dev, bf16[4,1,256,256]{3,2,1,0:T(8,128)(2,1)S(1)} %get-tuple-element.250.refs_0_, bf16[4,1,256,256]{3,2,1,0:T(8,128)(2,1)S(1)} %collective-permute-done.40.refs_1_, bf16[4,1,256,256]{3,2,1,0:T(8,128)(2,1)S(1)} %collective-permute-done.41.refs_2_, ...), custom_call_target="tpu_custom_call" | custom-call | flops 4400000000 | bytes 6299648 | tf_op jit(solution)/shard_map/join_out/pallas_call | solution.py:101
  148.6 2.8 %join_z.1 = (f32[1024,1024]{1,0:T(8,128)}, f32[8,128]{1,0:T(8,128)S(1)}) custom-call(s32[1]{0:T(128)} %bitcast.dev, bf16[4,1,256,256]{3,2,1,0:T(8,128)(2,1)S(1)} %get-tuple-element.249.refs_0_, bf16[4,1,256,256]{3,2,1,0:T(8,128)(2,1)S(1)} %collective-permute-done.37.refs_1_, bf16[4,1,256,256]{3,2,1,0:T(8,128)(2,1)S(1)} %collective-permute-done.38.refs_2_, ...), custom_call_target="tpu_custom_call" | custom-call | flops 4400000000 | bytes 6299648 | tf_op jit(solution)/shard_map/join_z/pallas_call | solution.py:101
  151.4 2.8 %join_x.1 = (f32[1024,1024]{1,0:T(8,128)}, f32[8,128]{1,0:T(8,128)}) custom-call(s32[1]{0:T(128)} %bitcast.dev, bf16[4,1,256,256]{3,2,1,0:T(8,128)(2,1)S(1)} %get-tuple-element.256.refs_0_, bf16[4,1,256,256]{3,2,1,0:T(8,128)(2,1)S(1)} %collective-permute-done.44.refs_1_, bf16[4,1,256,256]{3,2,1,0:T(8,128)(2,1)S(1)} %collective-permute-done.45.refs_2_, ...), custom_call_target="tpu_custom_call" | custom-call | flops 4400000000 | bytes 6299648 | tf_op jit(solution)/shard_map/join_x/pallas_call | solution.py:101
  (126 shorter events, 19.2 us)
Async XLA Ops:
  0.6 9.8 %collective-permute-start.1 = (bf16[128,1024]{1,0:T(8,128)(2,1)}, bf16[128,1024]{1,0:T(8,128)(2,1)S(1)}, u32[]{:S(2)}, u32[]{:S(2)}) collective-permute-start(bf16[128,1024]{1,0:T(8,128)(2,1)} %refs_0_.1), channel_id=1, source_target_pairs={{0,1},{1,0},{2,3},{3,2},{4,5},{5,4},{6,7},{7,6},{8,9},{9,8},{10,11... | collective-permute-start | bytes 786440 | tf_op jit(solution)/shard_map/ppermute | solution.py:21
  3.7 6.7 %collective-permute-start = (f32[1,512]{1,0:T(1,128)}, f32[1,512]{1,0:T(1,128)S(1)}, u32[]{:S(2)}, u32[]{:S(2)}) collective-permute-start(f32[1,512]{1,0:T(1,128)} %refs_4_.2), channel_id=1, source_target_pairs={{0,1},{1,0},{2,3},{3,2},{4,5},{5,4},{6,7},{7,6},{8,9},{9,8},{10,11... | collective-permute-start | bytes 6152 | tf_op jit(solution)/shard_map/ppermute | solution.py:21
  11.7 7.9 %collective-permute-start.2 = (bf16[256,128]{1,0:T(8,128)(2,1)S(1)}, bf16[256,128]{1,0:T(8,128)(2,1)S(1)}, u32[]{:S(2)}, u32[]{:S(2)}) collective-permute-start(bf16[256,128]{1,0:T(8,128)(2,1)S(1)} %get-tuple-element.150), channel_id=1, source_target_pairs={{0,1},{1,0},{2,3},{3,2},{4,5},{5,4},{6,7},{7,6},{8,9},{9,8},{10,11... | collective-permute-start | bytes 196616 | tf_op jit(solution)/shard_map/ppermute | solution.py:21
  13.7 10.0 %collective-permute-start.3 = (bf16[128,1024]{1,0:T(8,128)(2,1)S(1)}, bf16[128,1024]{1,0:T(8,128)(2,1)S(1)}, u32[]{:S(2)}, u32[]{:S(2)}) collective-permute-start(bf16[128,1024]{1,0:T(8,128)(2,1)S(1)} %get-tuple-element.161.refs_7_), channel_id=1, source_target_pairs={{0,1},{1,0},{2,3},{3,2},{4,5},{5,4},{6,7},{7,6},{8,9},{9,8},{10,11... | collective-permute-start | bytes 786440 | tf_op jit(solution)/shard_map/ppermute | solution.py:21
  13.8 16.6 %collective-permute-start.4 = (bf16[128,2048]{1,0:T(8,128)(2,1)S(1)}, bf16[128,2048]{1,0:T(8,128)(2,1)S(1)}, u32[]{:S(2)}, u32[]{:S(2)}) collective-permute-start(bf16[128,2048]{1,0:T(8,128)(2,1)S(1)} %get-tuple-element.163), channel_id=1, source_target_pairs={{0,4},{2,6},{4,0},{6,2},{8,12},{10,14},{12,8},{14,10},{16,20},{18,... | collective-permute-start | bytes 1572872 | tf_op jit(solution)/shard_map/ppermute | solution.py:21
  26.8 3.7 %collective-permute-start.5 = (f32[8,256]{1,0:T(8,128)S(1)}, f32[8,256]{1,0:T(8,128)S(1)}, u32[]{:S(2)}, u32[]{:S(2)}) collective-permute-start(f32[8,256]{1,0:T(8,128)S(1)} %get-tuple-element.165), channel_id=1, source_target_pairs={{0,1},{1,0},{2,3},{3,2},{4,5},{5,4},{6,7},{7,6},{8,9},{9,8},{10,11... | collective-permute-start | bytes 24584 | tf_op jit(solution)/shard_map/ppermute | solution.py:21
  32.0 11.2 %collective-permute-start.6 = (bf16[128,2048]{1,0:T(8,128)(2,1)S(1)}, bf16[128,2048]{1,0:T(8,128)(2,1)S(1)}, u32[]{:S(2)}, u32[]{:S(2)}) collective-permute-start(bf16[128,2048]{1,0:T(8,128)(2,1)S(1)} %get-tuple-element.173.refs_0_), channel_id=1, source_target_pairs={{0,1},{1,0},{2,3},{3,2},{4,5},{5,4},{6,7},{7,6},{8,9},{9,8},{10,11... | collective-permute-start | bytes 1572872 | tf_op jit(solution)/shard_map/ppermute | solution.py:21
  33.6 18.6 %collective-permute-start.10 = (bf16[256,2048]{1,0:T(8,128)(2,1)S(1)}, bf16[256,2048]{1,0:T(8,128)(2,1)S(1)}, u32[]{:S(2)}, u32[]{:S(2)}) collective-permute-start(bf16[256,2048]{1,0:T(8,128)(2,1)S(1)} %get-tuple-element.188.refs_4_), channel_id=1, source_target_pairs={{0,2},{2,0},{4,6},{6,4},{8,10},{10,8},{12,14},{14,12},{16,18},{18,... | collective-permute-start | bytes 3145736 | tf_op jit(solution)/shard_map/ppermute | solution.py:21
  43.3 10.5 %collective-permute-start.11 = (bf16[256,2048]{1,0:T(8,128)(2,1)S(1)}, bf16[256,2048]{1,0:T(8,128)(2,1)S(1)}, u32[]{:S(2)}, u32[]{:S(2)}) collective-permute-start(bf16[256,2048]{1,0:T(8,128)(2,1)S(1)} %get-tuple-element.189.refs_6_), channel_id=1, source_target_pairs={{0,2},{2,0},{4,6},{6,4},{8,10},{10,8},{12,14},{14,12},{16,18},{18,... | collective-permute-start | bytes 3145736 | tf_op jit(solution)/shard_map/ppermute | solution.py:21
  43.3 5.6 %collective-permute-start.7 = (bf16[256,256]{1,0:T(8,128)(2,1)S(1)}, bf16[256,256]{1,0:T(8,128)(2,1)S(1)}, u32[]{:S(2)}, u32[]{:S(2)}) collective-permute-start(bf16[256,256]{1,0:T(8,128)(2,1)S(1)} %get-tuple-element.185), channel_id=1, source_target_pairs={{0,2},{2,0},{4,6},{6,4},{8,10},{10,8},{12,14},{14,12},{16,18},{18,... | collective-permute-start | bytes 393224 | tf_op jit(solution)/shard_map/ppermute | solution.py:21
  43.8 6.4 %collective-permute-start.8 = (bf16[256,256]{1,0:T(8,128)(2,1)S(1)}, bf16[256,256]{1,0:T(8,128)(2,1)S(1)}, u32[]{:S(2)}, u32[]{:S(2)}) collective-permute-start(bf16[256,256]{1,0:T(8,128)(2,1)S(1)} %get-tuple-element.186), channel_id=1, source_target_pairs={{0,4},{2,6},{4,0},{6,2},{8,12},{10,14},{12,8},{14,10},{16,20},{18,... | collective-permute-start | bytes 393224 | tf_op jit(solution)/shard_map/ppermute | solution.py:21
  44.5 6.7 %collective-permute-start.9 = (bf16[256,256]{1,0:T(8,128)(2,1)S(1)}, bf16[256,256]{1,0:T(8,128)(2,1)S(1)}, u32[]{:S(2)}, u32[]{:S(2)}) collective-permute-start(bf16[256,256]{1,0:T(8,128)(2,1)S(1)} %get-tuple-element.187), channel_id=1, source_target_pairs={{0,6},{2,4},{4,2},{6,0},{8,14},{10,12},{12,10},{14,8},{16,22},{18,... | collective-permute-start | bytes 393224 | tf_op jit(solution)/shard_map/ppermute | solution.py:21
  48.9 10.0 %collective-permute-start.13 = (bf16[256,256]{1,0:T(8,128)(2,1)S(1)}, bf16[256,256]{1,0:T(8,128)(2,1)S(1)}, u32[]{:S(2)}, u32[]{:S(2)}) collective-permute-start(bf16[256,256]{1,0:T(8,128)(2,1)S(1)} %get-tuple-element.202), channel_id=1, source_target_pairs={{0,2},{2,0},{4,6},{6,4},{8,10},{10,8},{12,14},{14,12},{16,18},{18,... | collective-permute-start | bytes 393224 | tf_op jit(solution)/shard_map/ppermute | solution.py:21
  50.2 8.7 %collective-permute-start.14 = (bf16[256,256]{1,0:T(8,128)(2,1)S(1)}, bf16[256,256]{1,0:T(8,128)(2,1)S(1)}, u32[]{:S(2)}, u32[]{:S(2)}) collective-permute-start(bf16[256,256]{1,0:T(8,128)(2,1)S(1)} %get-tuple-element.203), channel_id=1, source_target_pairs={{0,4},{2,6},{4,0},{6,2},{8,12},{10,14},{12,8},{14,10},{16,20},{18,... | collective-permute-start | bytes 393224 | tf_op jit(solution)/shard_map/ppermute | solution.py:21
  51.2 7.7 %collective-permute-start.15 = (bf16[256,256]{1,0:T(8,128)(2,1)S(1)}, bf16[256,256]{1,0:T(8,128)(2,1)S(1)}, u32[]{:S(2)}, u32[]{:S(2)}) collective-permute-start(bf16[256,256]{1,0:T(8,128)(2,1)S(1)} %get-tuple-element.204), channel_id=1, source_target_pairs={{0,6},{2,4},{4,2},{6,0},{8,14},{10,12},{12,10},{14,8},{16,22},{18,... | collective-permute-start | bytes 393224 | tf_op jit(solution)/shard_map/ppermute | solution.py:21
  52.2 8.7 %collective-permute-start.12 = (bf16[256,128]{1,0:T(8,128)(2,1)S(1)}, bf16[256,128]{1,0:T(8,128)(2,1)S(1)}, u32[]{:S(2)}, u32[]{:S(2)}) collective-permute-start(bf16[256,128]{1,0:T(8,128)(2,1)S(1)} %get-tuple-element.199), channel_id=1, source_target_pairs={{0,1},{1,0},{2,3},{3,2},{4,5},{5,4},{6,7},{7,6},{8,9},{9,8},{10,11... | collective-permute-start | bytes 196616 | tf_op jit(solution)/shard_map/ppermute | solution.py:21
  62.1 3.9 %collective-permute-start.17 = (bf16[80,1024]{1,0:T(8,128)(2,1)S(1)}, bf16[80,1024]{1,0:T(8,128)(2,1)S(1)}, u32[]{:S(2)}, u32[]{:S(2)}) collective-permute-start(bf16[80,1024]{1,0:T(8,128)(2,1)S(1)} %get-tuple-element.214), channel_id=1, source_target_pairs={{0,2},{2,0},{4,6},{6,4},{8,10},{10,8},{12,14},{14,12},{16,18},{18,... | collective-permute-start | bytes 491528 | tf_op jit(solution)/shard_map/ppermute | solution.py:21
  62.2 9.2 %collective-permute-start.27 = (bf16[2,1,256,256]{3,2,1,0:T(8,128)(2,1)S(1)}, bf16[2,1,256,256]{3,2,1,0:T(8,128)(2,1)S(1)}, u32[]{:S(2)}, u32[]{:S(2)}) collective-permute-start(bf16[2,1,256,256]{3,2,1,0:T(8,128)(2,1)S(1)} %get-tuple-element.224), channel_id=1, source_target_pairs={{0,8},{2,10},{4,12},{6,14},{8,0},{10,2},{12,4},{14,6},{16,24},{18,... | collective-permute-start | bytes 786440 | tf_op jit(solution)/shard_map/ppermute | solution.py:21
  63.8 9.0 %collective-permute-start.25 = (bf16[256,256]{1,0:T(8,128)(2,1)S(1)}, bf16[256,256]{1,0:T(8,128)(2,1)S(1)}, u32[]{:S(2)}, u32[]{:S(2)}) collective-permute-start(bf16[256,256]{1,0:T(8,128)(2,1)S(1)} %get-tuple-element.221), channel_id=1, source_target_pairs={{0,4},{2,6},{4,0},{6,2},{8,12},{10,14},{12,8},{14,10},{16,20},{18,... | collective-permute-start | bytes 393224 | tf_op jit(solution)/shard_map/ppermute | solution.py:21
  65.2 10.3 %collective-permute-start.26 = (bf16[256,256]{1,0:T(8,128)(2,1)S(1)}, bf16[256,256]{1,0:T(8,128)(2,1)S(1)}, u32[]{:S(2)}, u32[]{:S(2)}) collective-permute-start(bf16[256,256]{1,0:T(8,128)(2,1)S(1)} %get-tuple-element.222), channel_id=1, source_target_pairs={{0,6},{2,4},{4,2},{6,0},{8,14},{10,12},{12,10},{14,8},{16,22},{18,... | collective-permute-start | bytes 393224 | tf_op jit(solution)/shard_map/ppermute | solution.py:21
  65.3 10.1 %collective-permute-start.24 = (bf16[256,256]{1,0:T(8,128)(2,1)S(1)}, bf16[256,256]{1,0:T(8,128)(2,1)S(1)}, u32[]{:S(2)}, u32[]{:S(2)}) collective-permute-start(bf16[256,256]{1,0:T(8,128)(2,1)S(1)} %get-tuple-element.220), channel_id=1, source_target_pairs={{0,2},{2,0},{4,6},{6,4},{8,10},{10,8},{12,14},{14,12},{16,18},{18,... | collective-permute-start | bytes 393224 | tf_op jit(solution)/shard_map/ppermute | solution.py:21
  66.0 13.3 %collective-permute-start.23 = (bf16[2,1,256,256]{3,2,1,0:T(8,128)(2,1)S(1)}, bf16[2,1,256,256]{3,2,1,0:T(8,128)(2,1)S(1)}, u32[]{:S(2)}, u32[]{:S(2)}) collective-permute-start(bf16[2,1,256,256]{3,2,1,0:T(8,128)(2,1)S(1)} %get-tuple-element.218), channel_id=1, source_target_pairs={{0,8},{2,10},{4,12},{6,14},{8,0},{10,2},{12,4},{14,6},{16,24},{18,... | collective-permute-start | bytes 786440 | tf_op jit(solution)/shard_map/ppermute | solution.py:21
  71.4 11.0 %collective-permute-start.18 = (bf16[80,1024]{1,0:T(8,128)(2,1)S(1)}, bf16[80,1024]{1,0:T(8,128)(2,1)S(1)}, u32[]{:S(2)}, u32[]{:S(2)}) collective-permute-start(bf16[80,1024]{1,0:T(8,128)(2,1)S(1)} %add_convert_fusion.3), channel_id=1, source_target_pairs={{0,4},{2,6},{4,0},{6,2},{8,12},{10,14},{12,8},{14,10},{16,20},{18,... | collective-permute-start | bytes 491528 | tf_op jit(solution)/shard_map/ppermute | solution.py:21
  72.8 9.1 %collective-permute-start.30 = (bf16[1,1,256,256]{3,2,1,0:T(8,128)(2,1)S(1)}, bf16[1,1,256,256]{3,2,1,0:T(8,128)(2,1)S(1)}, u32[]{:S(2)}, u32[]{:S(2)}) collective-permute-start(bf16[1,1,256,256]{3,2,1,0:T(8,128)(2,1)S(1)} %get-tuple-element.232), channel_id=1, source_target_pairs={{0,16},{2,18},{4,20},{6,22},{8,24},{10,26},{12,28},{14,30},{16,0},... | collective-permute-start | bytes 393224 | tf_op jit(solution)/shard_map/ppermute | solution.py:21
  79.3 15.4 %collective-permute-start.28 = (bf16[1,1,256,256]{3,2,1,0:T(8,128)(2,1)S(1)}, bf16[1,1,256,256]{3,2,1,0:T(8,128)(2,1)S(1)}, u32[]{:S(2)}, u32[]{:S(2)}) collective-permute-start(bf16[1,1,256,256]{3,2,1,0:T(8,128)(2,1)S(1)} %get-tuple-element.228), channel_id=1, source_target_pairs={{0,16},{2,18},{4,20},{6,22},{8,24},{10,26},{12,28},{14,30},{16,0},... | collective-permute-start | bytes 393224 | tf_op jit(solution)/shard_map/ppermute | solution.py:21
  79.7 15.0 %collective-permute-start.29 = (bf16[2,1,256,256]{3,2,1,0:T(8,128)(2,1)S(1)}, bf16[2,1,256,256]{3,2,1,0:T(8,128)(2,1)S(1)}, u32[]{:S(2)}, u32[]{:S(2)}) collective-permute-start(bf16[2,1,256,256]{3,2,1,0:T(8,128)(2,1)S(1)} %get-tuple-element.230), channel_id=1, source_target_pairs={{0,8},{2,10},{4,12},{6,14},{8,0},{10,2},{12,4},{14,6},{16,24},{18,... | collective-permute-start | bytes 786440 | tf_op jit(solution)/shard_map/ppermute | solution.py:21
  81.9 15.8 %collective-permute-start.33 = (bf16[1,1,256,256]{3,2,1,0:T(8,128)(2,1)S(1)}, bf16[1,1,256,256]{3,2,1,0:T(8,128)(2,1)S(1)}, u32[]{:S(2)}, u32[]{:S(2)}) collective-permute-start(bf16[1,1,256,256]{3,2,1,0:T(8,128)(2,1)S(1)} %get-tuple-element.239.refs_0_), channel_id=1, source_target_pairs={{0,16},{2,18},{4,20},{6,22},{8,24},{10,26},{12,28},{14,30},{16,0},... | collective-permute-start | bytes 393224 | tf_op jit(solution)/shard_map/ppermute | solution.py:21
  82.4 17.0 %collective-permute-start.19 = (bf16[80,1024]{1,0:T(8,128)(2,1)S(1)}, bf16[80,1024]{1,0:T(8,128)(2,1)S(1)}, u32[]{:S(2)}, u32[]{:S(2)}) collective-permute-start(bf16[80,1024]{1,0:T(8,128)(2,1)S(1)} %add_convert_fusion.2), channel_id=1, source_target_pairs={{0,8},{2,10},{4,12},{6,14},{8,0},{10,2},{12,4},{14,6},{16,24},{18,... | collective-permute-start | bytes 491528 | tf_op jit(solution)/shard_map/ppermute | solution.py:21
  94.8 16.5 %collective-permute-start.31 = (bf16[1,1,256,256]{3,2,1,0:T(8,128)(2,1)S(1)}, bf16[1,1,256,256]{3,2,1,0:T(8,128)(2,1)S(1)}, u32[]{:S(2)}, u32[]{:S(2)}) collective-permute-start(bf16[1,1,256,256]{3,2,1,0:T(8,128)(2,1)S(1)} %get-tuple-element.236.refs_0_), channel_id=1, source_target_pairs={{0,16},{2,18},{4,20},{6,22},{8,24},{10,26},{12,28},{14,30},{16,0},... | collective-permute-start | bytes 393224 | tf_op jit(solution)/shard_map/ppermute | solution.py:21
  96.3 14.9 %collective-permute-start.32 = (bf16[1,1,256,256]{3,2,1,0:T(8,128)(2,1)S(1)}, bf16[1,1,256,256]{3,2,1,0:T(8,128)(2,1)S(1)}, u32[]{:S(2)}, u32[]{:S(2)}) collective-permute-start(bf16[1,1,256,256]{3,2,1,0:T(8,128)(2,1)S(1)} %get-tuple-element.238), channel_id=1, source_target_pairs={{0,16},{2,18},{4,20},{6,22},{8,24},{10,26},{12,28},{14,30},{16,0},... | collective-permute-start | bytes 393224 | tf_op jit(solution)/shard_map/ppermute | solution.py:21
  97.8 13.6 %collective-permute-start.36 = (bf16[2,1,256,256]{3,2,1,0:T(8,128)(2,1)S(1)}, bf16[2,1,256,256]{3,2,1,0:T(8,128)(2,1)S(1)}, u32[]{:S(2)}, u32[]{:S(2)}) collective-permute-start(bf16[2,1,256,256]{3,2,1,0:T(8,128)(2,1)S(1)} %get-tuple-element.245.refs_0_), channel_id=1, source_target_pairs={{0,8},{2,10},{4,12},{6,14},{8,0},{10,2},{12,4},{14,6},{16,24},{18,... | collective-permute-start | bytes 786440 | tf_op jit(solution)/shard_map/ppermute | solution.py:21
  99.5 20.6 %collective-permute-start.20 = (bf16[80,1024]{1,0:T(8,128)(2,1)S(1)}, bf16[80,1024]{1,0:T(8,128)(2,1)S(1)}, u32[]{:S(2)}, u32[]{:S(2)}) collective-permute-start(bf16[80,1024]{1,0:T(8,128)(2,1)S(1)} %add_convert_fusion.1), channel_id=1, source_target_pairs={{0,16},{2,18},{4,20},{6,22},{8,24},{10,26},{12,28},{14,30},{16,0},... | collective-permute-start | bytes 491528 | tf_op jit(solution)/shard_map/ppermute | solution.py:21
  111.2 8.3 %collective-permute-start.35 = (bf16[1,1,256,256]{3,2,1,0:T(8,128)(2,1)S(1)}, bf16[1,1,256,256]{3,2,1,0:T(8,128)(2,1)S(1)}, u32[]{:S(2)}, u32[]{:S(2)}) collective-permute-start(bf16[1,1,256,256]{3,2,1,0:T(8,128)(2,1)S(1)} %get-tuple-element.244.refs_0_), channel_id=1, source_target_pairs={{0,16},{2,18},{4,20},{6,22},{8,24},{10,26},{12,28},{14,30},{16,0},... | collective-permute-start | bytes 393224 | tf_op jit(solution)/shard_map/ppermute | solution.py:21
  111.4 18.6 %collective-permute-start.41 = (bf16[4,1,256,256]{3,2,1,0:T(8,128)(2,1)S(1)}, bf16[4,1,256,256]{3,2,1,0:T(8,128)(2,1)S(1)}, u32[]{:S(2)}, u32[]{:S(2)}) collective-permute-start(bf16[4,1,256,256]{3,2,1,0:T(8,128)(2,1)S(1)} %get-tuple-element.250.refs_0_), channel_id=1, source_target_pairs={{0,4},{2,6},{4,0},{6,2},{8,12},{10,14},{12,8},{14,10},{16,20},{18,... | collective-permute-start | bytes 1572872 | tf_op jit(solution)/shard_map/ppermute | solution.py:21
  114.9 9.2 %collective-permute-start.34 = (bf16[2,1,256,256]{3,2,1,0:T(8,128)(2,1)S(1)}, bf16[2,1,256,256]{3,2,1,0:T(8,128)(2,1)S(1)}, u32[]{:S(2)}, u32[]{:S(2)}) collective-permute-start(bf16[2,1,256,256]{3,2,1,0:T(8,128)(2,1)S(1)} %get-tuple-element.243.refs_0_), channel_id=1, source_target_pairs={{0,8},{2,10},{4,12},{6,14},{8,0},{10,2},{12,4},{14,6},{16,24},{18,... | collective-permute-start | bytes 786440 | tf_op jit(solution)/shard_map/ppermute | solution.py:21
  119.6 7.9 %collective-permute-start.43 = (bf16[2,1,256,256]{3,2,1,0:T(8,128)(2,1)S(1)}, bf16[2,1,256,256]{3,2,1,0:T(8,128)(2,1)S(1)}, u32[]{:S(2)}, u32[]{:S(2)}) collective-permute-start(bf16[2,1,256,256]{3,2,1,0:T(8,128)(2,1)S(1)} %get-tuple-element.251.refs_0_), channel_id=1, source_target_pairs={{0,8},{2,10},{4,12},{6,14},{8,0},{10,2},{12,4},{14,6},{16,24},{18,... | collective-permute-start | bytes 786440 | tf_op jit(solution)/shard_map/ppermute | solution.py:21
  120.2 7.4 %collective-permute-start.21 = (bf16[80,1024]{1,0:T(8,128)(2,1)S(1)}, bf16[80,1024]{1,0:T(8,128)(2,1)S(1)}, u32[]{:S(2)}, u32[]{:S(2)}) collective-permute-start(bf16[80,1024]{1,0:T(8,128)(2,1)S(1)} %add_convert_fusion.refs_0_), channel_id=1, source_target_pairs={{0,2},{2,0},{4,6},{6,4},{8,10},{10,8},{12,14},{14,12},{16,18},{18,... | collective-permute-start | bytes 491528 | tf_op jit(solution)/shard_map/ppermute | solution.py:21
  120.2 14.3 %collective-permute-start.16 = (bf16[128,2048]{1,0:T(8,128)(2,1)S(1)}, bf16[128,2048]{1,0:T(8,128)(2,1)S(1)}, u32[]{:S(2)}, u32[]{:S(2)}) collective-permute-start(bf16[128,2048]{1,0:T(8,128)(2,1)S(1)} %get-tuple-element.209), channel_id=1, source_target_pairs={{0,1},{1,0},{2,3},{3,2},{4,5},{5,4},{6,7},{7,6},{8,9},{9,8},{10,11... | collective-permute-start | bytes 1572872 | tf_op jit(solution)/shard_map/ppermute | solution.py:21
  124.1 14.5 %copy-start.7 = (bf16[128,1024]{1,0:T(8,128)(2,1)S(1)}, bf16[128,1024]{1,0:T(8,128)(2,1)}, u32[]{:S(2)}) copy-start(bf16[128,1024]{1,0:T(8,128)(2,1)} %refs_1_.1) | copy-start | bytes 786436
  124.1 14.0 %collective-permute-start.38 = (bf16[4,1,256,256]{3,2,1,0:T(8,128)(2,1)S(1)}, bf16[4,1,256,256]{3,2,1,0:T(8,128)(2,1)S(1)}, u32[]{:S(2)}, u32[]{:S(2)}) collective-permute-start(bf16[4,1,256,256]{3,2,1,0:T(8,128)(2,1)S(1)} %get-tuple-element.249.refs_0_), channel_id=1, source_target_pairs={{0,4},{2,6},{4,0},{6,2},{8,12},{10,14},{12,8},{14,10},{16,20},{18,... | collective-permute-start | bytes 1572872 | tf_op jit(solution)/shard_map/ppermute | solution.py:21
  127.5 13.2 %collective-permute-start.40 = (bf16[4,1,256,256]{3,2,1,0:T(8,128)(2,1)S(1)}, bf16[4,1,256,256]{3,2,1,0:T(8,128)(2,1)S(1)}, u32[]{:S(2)}, u32[]{:S(2)}) collective-permute-start(bf16[4,1,256,256]{3,2,1,0:T(8,128)(2,1)S(1)} %get-tuple-element.250.refs_0_), channel_id=1, source_target_pairs={{0,2},{2,0},{4,6},{6,4},{8,10},{10,8},{12,14},{14,12},{16,18},{18,... | collective-permute-start | bytes 1572872 | tf_op jit(solution)/shard_map/ppermute | solution.py:21
  127.6 18.5 %collective-permute-start.45 = (bf16[4,1,256,256]{3,2,1,0:T(8,128)(2,1)S(1)}, bf16[4,1,256,256]{3,2,1,0:T(8,128)(2,1)S(1)}, u32[]{:S(2)}, u32[]{:S(2)}) collective-permute-start(bf16[4,1,256,256]{3,2,1,0:T(8,128)(2,1)S(1)} %get-tuple-element.256.refs_0_), channel_id=1, source_target_pairs={{0,4},{2,6},{4,0},{6,2},{8,12},{10,14},{12,8},{14,10},{16,20},{18,... | collective-permute-start | bytes 1572872 | tf_op jit(solution)/shard_map/ppermute | solution.py:21
  130.1 16.0 %collective-permute-start.42 = (bf16[4,1,256,256]{3,2,1,0:T(8,128)(2,1)S(1)}, bf16[4,1,256,256]{3,2,1,0:T(8,128)(2,1)S(1)}, u32[]{:S(2)}, u32[]{:S(2)}) collective-permute-start(bf16[4,1,256,256]{3,2,1,0:T(8,128)(2,1)S(1)} %collective-permute-done.41.refs_2_), channel_id=1, source_target_pairs={{0,2},{2,0},{4,6},{6,4},{8,10},{10,8},{12,14},{14,12},{16,18},{18,... | collective-permute-start | bytes 1572872 | tf_op jit(solution)/shard_map/ppermute | solution.py:21
  134.6 3.6 %collective-permute-start.22 = (f32[1,512]{1,0:T(1,128)S(1)}, f32[1,512]{1,0:T(1,128)S(1)}, u32[]{:S(2)}, u32[]{:S(2)}) collective-permute-start(f32[1,512]{1,0:T(1,128)S(1)} %get-tuple-element.216), channel_id=1, source_target_pairs={{0,1},{1,0},{2,3},{3,2},{4,5},{5,4},{6,7},{7,6},{8,9},{9,8},{10,11... | collective-permute-start | bytes 6152 | tf_op jit(solution)/shard_map/ppermute | solution.py:21
  138.2 10.4 %collective-permute-start.37 = (bf16[4,1,256,256]{3,2,1,0:T(8,128)(2,1)S(1)}, bf16[4,1,256,256]{3,2,1,0:T(8,128)(2,1)S(1)}, u32[]{:S(2)}, u32[]{:S(2)}) collective-permute-start(bf16[4,1,256,256]{3,2,1,0:T(8,128)(2,1)S(1)} %get-tuple-element.249.refs_0_), channel_id=1, source_target_pairs={{0,2},{2,0},{4,6},{6,4},{8,10},{10,8},{12,14},{14,12},{16,18},{18,... | collective-permute-start | bytes 1572872 | tf_op jit(solution)/shard_map/ppermute | solution.py:21
  138.2 10.4 %collective-permute-start.39 = (bf16[4,1,256,256]{3,2,1,0:T(8,128)(2,1)S(1)}, bf16[4,1,256,256]{3,2,1,0:T(8,128)(2,1)S(1)}, u32[]{:S(2)}, u32[]{:S(2)}) collective-permute-start(bf16[4,1,256,256]{3,2,1,0:T(8,128)(2,1)S(1)} %collective-permute-done.38.refs_2_), channel_id=1, source_target_pairs={{0,2},{2,0},{4,6},{6,4},{8,10},{10,8},{12,14},{14,12},{16,18},{18,... | collective-permute-start | bytes 1572872 | tf_op jit(solution)/shard_map/ppermute | solution.py:21
  140.7 10.7 %collective-permute-start.44 = (bf16[4,1,256,256]{3,2,1,0:T(8,128)(2,1)S(1)}, bf16[4,1,256,256]{3,2,1,0:T(8,128)(2,1)S(1)}, u32[]{:S(2)}, u32[]{:S(2)}) collective-permute-start(bf16[4,1,256,256]{3,2,1,0:T(8,128)(2,1)S(1)} %get-tuple-element.256.refs_0_), channel_id=1, source_target_pairs={{0,2},{2,0},{4,6},{6,4},{8,10},{10,8},{12,14},{14,12},{16,18},{18,... | collective-permute-start | bytes 1572872 | tf_op jit(solution)/shard_map/ppermute | solution.py:21
  146.1 5.3 %collective-permute-start.46 = (bf16[4,1,256,256]{3,2,1,0:T(8,128)(2,1)S(1)}, bf16[4,1,256,256]{3,2,1,0:T(8,128)(2,1)S(1)}, u32[]{:S(2)}, u32[]{:S(2)}) collective-permute-start(bf16[4,1,256,256]{3,2,1,0:T(8,128)(2,1)S(1)} %collective-permute-done.45.refs_2_), channel_id=1, source_target_pairs={{0,2},{2,0},{4,6},{6,4},{8,10},{10,8},{12,14},{14,12},{16,18},{18,... | collective-permute-start | bytes 1572872 | tf_op jit(solution)/shard_map/ppermute | solution.py:21
  (21 other events, 66.7 us)
